TPU v7x, 32 devices: a whole 2x2x4 slice. The times are simulated.
32 devices in a mesh: dp: 4 (over z), ctx: 4 (over y, core), tensor: 2 (over x).
Axes of the slice: x: 2, y: 2, z: 4, core: 2. Of those that a mesh axis runs over, the one named last changes fastest.
Arguments:
- inputs: bfloat16 [4, 1024, 2048], P('dp', 'ctx'), may hold values from -6 to 6
- segments: int32 [4, 1024], P('dp'), may hold values from 0 to 4, as said below
- first_gain: bfloat16 [2048], replicated, may hold values from 0.5 to 1.5
- first_shift: bfloat16 [2048], replicated, may hold values from -3 to 3
- in_weight: bfloat16 [2048, 3, 2048], P(None, None, 'tensor'), may hold values from -0.125 to 0.125
- in_bias: bfloat16 [2, 2048], P(None, 'tensor'), may hold values from -2 to 2
- out_weight: bfloat16 [2048, 2048], P(None, 'tensor'), may hold values from -1 to 1
- out_bias: bfloat16 [2048], replicated, may hold values from -2 to 2
- second_gain: bfloat16 [2048], replicated, may hold values from 0.5 to 1.5
- second_shift: bfloat16 [2048], replicated, may hold values from -3 to 3
- up_weight: bfloat16 [2048, 8192], P(None, 'tensor'), may hold values from -0.125 to 0.125
- up_bias: bfloat16 [8192], P('tensor'), may hold values from -3 to 3
- down_weight: bfloat16 [2048, 8192], P(None, 'tensor'), may hold values from -0.0625 to 0.0625
- down_bias: bfloat16 [2048], replicated, may hold values from -2 to 2
- cotangent: bfloat16 [4, 1024, 2048], P('dp', 'ctx'), may hold values from -6 to 6
Outputs:
- outputs: bfloat16 [4, 1024, 2048], P('dp', ('ctx', 'tensor'))
- input_grad: bfloat16 [4, 1024, 2048], P('dp', ('ctx', 'tensor'))
- first_gain_grad: float32 [2048], replicated
- first_shift_grad: float32 [2048], replicated
- in_weight_grad: float32 [2048, 3, 2048], P(('dp', 'ctx'), None, 'tensor')
- in_bias_grad: float32 [2, 2048], P(None, 'tensor')
- out_weight_grad: float32 [2048, 2048], P(('dp', 'ctx'), 'tensor')
- out_bias_grad: float32 [2048], replicated
- second_gain_grad: float32 [2048], replicated
- second_shift_grad: float32 [2048], replicated
- up_weight_grad: float32 [2048, 8192], P(('dp', 'ctx'), 'tensor')
- up_bias_grad: float32 [8192], P('tensor')
- down_weight_grad: float32 [2048, 8192], P(('dp', 'ctx'), 'tensor')
- down_bias_grad: float32 [2048], replicated
Inputs may be any that keep to these rules, and one draw needn't show every extreme that they name: `segments`: along each sequence the numbers start at 0 and rise by one at each document boundary; every sequence holds exactly five documents.
All inputs are finite; a program needn't handle non-finite values.
Results may differ from a plain program's by a relative error of at most 0.019.
Values may be sent and summed in bfloat16 or wider, within the bound.
No kernel may reach another device: no remote copies, remote signals or barrier semaphores. Data moves between devices by JAX's collectives and lax.ppermute only.
A program may use at most 192 MiB of HBM per device.

v0:
```python
import math

import jax
import jax.numpy as jnp
from jax import lax
from jax.sharding import PartitionSpec as P

H = 16
HD = 128


EPSILON = 1e-05


def layer_norm(values, norm_gain, norm_shift):
    average = jnp.mean(values, axis=-1, keepdims=True)
    centered = values - average
    spread = jnp.mean(centered * centered, axis=-1, keepdims=True)
    return centered * lax.rsqrt(spread + EPSILON) * norm_gain + norm_shift


def contract(left, right, left_dim, right_dim):
    return lax.dot_general(
        left, right, (((left_dim,), (right_dim,)), ((), ())), preferred_element_type=jnp.float32
    )


def gelu_tanh(values):
    return jax.nn.gelu(values, approximate=True)


def shards(
    inputs,
    segments,
    first_gain,
    first_shift,
    in_weight,
    in_bias,
    out_weight,
    out_bias,
    second_gain,
    second_shift,
    up_weight,
    up_bias,
    down_weight,
    down_bias,
    cotangent,
):
    rows = inputs.shape[1]
    width = inputs.shape[2]
    local_width = in_weight.shape[2]
    local_hidden = up_weight.shape[1]
    heads_here = local_width // HD
    seq_length = segments.shape[1]
    share = rows // lax.axis_size("tensor")
    tensor_place = lax.axis_index("tensor")
    share_start = tensor_place * share
    scale = 1.0 / math.sqrt(HD)
    context_place = lax.axis_index("ctx")
    first_head = (tensor_place * heads_here).astype(jnp.float32)
    slopes = jnp.exp2(-8.0 * (first_head + jnp.arange(heads_here, dtype=jnp.float32) + 1.0) / H)
    segment_row = segments[0]
    query_pos = context_place * rows + jnp.arange(rows, dtype=jnp.int32)
    query_seg = lax.dynamic_slice_in_dim(segment_row, context_place * rows, rows)
    residual = inputs[0].astype(jnp.float32)
    residual_share = lax.dynamic_slice_in_dim(residual, share_start, share, 0)
    first_norm = (first_gain.astype(jnp.float32), first_shift.astype(jnp.float32))
    second_norm = (second_gain.astype(jnp.float32), second_shift.astype(jnp.float32))
    normed_first = layer_norm(residual, first_norm[0], first_norm[1]).astype(jnp.bfloat16)
    projected = jnp.einsum(
        "td,dcf->tcf", normed_first, in_weight, preferred_element_type=jnp.float32
    )
    bias_pair = in_bias.astype(jnp.float32)
    query_grid = (projected[:, 0] + bias_pair[0]).astype(jnp.bfloat16).reshape(rows, heads_here, HD)
    key_grid = projected[:, 1].astype(jnp.bfloat16).reshape(rows, heads_here, HD)
    value_grid = (projected[:, 2] + bias_pair[1]).astype(jnp.bfloat16).reshape(rows, heads_here, HD)
    keys_all, values_all = (
        lax.all_gather(key_grid, "ctx", axis=0, tiled=True),
        lax.all_gather(value_grid, "ctx", axis=0, tiled=True),
    )
    key_block = min(seq_length, max(rows, 512))
    needed = keys_all.shape[0] // key_block

    def block_scores(block):
        start = block * key_block
        key_part = lax.dynamic_slice_in_dim(keys_all, start, key_block, 0)
        value_part = lax.dynamic_slice_in_dim(values_all, start, key_block, 0)
        key_pos = start + jnp.arange(key_block, dtype=jnp.int32)
        key_seg = lax.dynamic_slice_in_dim(segment_row, start, key_block)
        raw = (
            jnp.einsum("qhd,khd->hqk", query_grid, key_part, preferred_element_type=jnp.float32)
            * scale
        )
        offset = (key_pos[None, :] - query_pos[:, None]).astype(jnp.float32)
        raw = raw + slopes[:, None, None] * offset[None]
        allowed = (
            (key_pos[None, :] <= query_pos[:, None]) & (key_seg[None, :] == query_seg[:, None])
        )[None]
        return (jnp.where(allowed, raw, -1e30), allowed, start, key_part, value_part)

    def stats_step(block, carry):
        top, total = carry
        scores, allowed, start, key_part, value_part = block_scores(block)
        new_top = jnp.maximum(top, jnp.max(scores, axis=-1))
        fresh = jnp.where(allowed, jnp.exp(scores - new_top[:, :, None]), 0.0)
        return (new_top, total * jnp.exp(top - new_top) + jnp.sum(fresh, axis=-1))

    start_top = jnp.full((heads_here, rows), -1e30, jnp.float32)
    start_total = jnp.zeros((heads_here, rows), jnp.float32)
    top, total = lax.fori_loop(0, needed, stats_step, (start_top, start_total))

    def probs_for(scores, allowed):
        return jnp.where(allowed, jnp.exp(scores - top[:, :, None]), 0.0) / total[:, :, None]

    def mix_step(block, carry):
        high_part, rest_part = carry
        scores, allowed, start, key_part, value_part = block_scores(block)
        probs = probs_for(scores, allowed)
        probs_low = lax.optimization_barrier(probs.astype(jnp.bfloat16))
        rest_low = (probs - probs_low.astype(jnp.float32)).astype(jnp.bfloat16)
        high_part = high_part + jnp.einsum(
            "hqk,khd->qhd", probs_low, value_part, preferred_element_type=jnp.float32
        )
        rest_part = rest_part + jnp.einsum(
            "hqk,khd->qhd", rest_low, value_part, preferred_element_type=jnp.float32
        )
        return (high_part, rest_part)

    empty_mix = jnp.zeros((rows, heads_here, HD), jnp.float32)
    mixed_high, mixed_rest = lax.fori_loop(0, needed, mix_step, (empty_mix, empty_mix))
    mixed_exact = (mixed_high + mixed_rest).reshape(rows, local_width)
    mixed_low = mixed_high.reshape(rows, local_width).astype(jnp.bfloat16)
    attention_share = lax.psum_scatter(
        contract(mixed_low, out_weight, 1, 1).astype(jnp.bfloat16),
        "tensor",
        scatter_dimension=0,
        tiled=True,
    ).astype(jnp.float32)
    middle_share = residual_share + attention_share + out_bias.astype(jnp.float32)
    normed_share, second_pull = jax.vjp(layer_norm, middle_share, second_norm[0], second_norm[1])
    normed_second = lax.all_gather(normed_share.astype(jnp.bfloat16), "tensor", axis=0, tiled=True)
    upper = jnp.dot(normed_second, up_weight, preferred_element_type=jnp.float32) + up_bias.astype(
        jnp.float32
    )
    active_full, gelu_pull = jax.vjp(gelu_tanh, upper)
    active = active_full.astype(jnp.bfloat16)
    feed_share = lax.psum_scatter(
        contract(active, down_weight, 1, 1).astype(jnp.bfloat16),
        "tensor",
        scatter_dimension=0,
        tiled=True,
    ).astype(jnp.float32)
    outputs = (middle_share + feed_share + down_bias.astype(jnp.float32)).astype(jnp.bfloat16)
    cotangent_low = cotangent[0]
    cotangent_share = lax.dynamic_slice_in_dim(cotangent_low, share_start, share, 0).astype(
        jnp.float32
    )
    down_whole = contract(cotangent_low, active, 0, 0)
    down_bias_term = jnp.sum(cotangent_share, axis=0)
    grad_active = jnp.dot(cotangent_low, down_weight, preferred_element_type=jnp.float32)
    grad_upper = gelu_pull(grad_active)[0].astype(jnp.bfloat16)
    up_bias_term = jnp.sum(grad_upper.astype(jnp.float32), axis=0)
    up_whole = contract(normed_second, grad_upper, 0, 0)
    grad_normed_share = lax.psum_scatter(
        contract(grad_upper, up_weight, 1, 1).astype(jnp.bfloat16),
        "tensor",
        scatter_dimension=0,
        tiled=True,
    ).astype(jnp.float32)
    grad_from_second, second_gain_term, second_shift_term = second_pull(grad_normed_share)
    grad_middle_share = cotangent_share + grad_from_second
    out_bias_term = jnp.sum(grad_middle_share, axis=0)
    grad_middle_low = lax.all_gather(
        grad_middle_share.astype(jnp.bfloat16), "tensor", axis=0, tiled=True
    )
    grad_mixed = jnp.dot(grad_middle_low, out_weight, preferred_element_type=jnp.float32).astype(
        jnp.bfloat16
    )
    out_whole = contract(grad_middle_low, mixed_low, 0, 0)
    delta = jnp.sum(
        (grad_mixed.astype(jnp.float32) * mixed_exact).reshape(rows, heads_here, HD), axis=-1
    ).T
    grad_mixed_grid = grad_mixed.reshape(rows, heads_here, HD)

    def back_step(block, carry):
        grad_query, grad_keys, grad_values = carry
        scores, allowed, start, key_part, value_part = block_scores(block)
        probs = probs_for(scores, allowed)
        probs_low = probs.astype(jnp.bfloat16)
        grad_probs = jnp.einsum(
            "qhd,khd->hqk", grad_mixed_grid, value_part, preferred_element_type=jnp.float32
        )
        grad_scores = (probs * (grad_probs - delta[:, :, None])).astype(jnp.bfloat16)
        grad_query = (
            grad_query
            + jnp.einsum("hqk,khd->qhd", grad_scores, key_part, preferred_element_type=jnp.float32)
            * scale
        )
        key_term = (
            jnp.einsum("hqk,qhd->khd", grad_scores, query_grid, preferred_element_type=jnp.float32)
            * scale
        )
        value_term = jnp.einsum(
            "hqk,qhd->khd", probs_low, grad_mixed_grid, preferred_element_type=jnp.float32
        )
        grad_keys = lax.dynamic_update_slice_in_dim(
            grad_keys, lax.dynamic_slice_in_dim(grad_keys, start, key_block, 0) + key_term, start, 0
        )
        grad_values = lax.dynamic_update_slice_in_dim(
            grad_values,
            lax.dynamic_slice_in_dim(grad_values, start, key_block, 0) + value_term,
            start,
            0,
        )
        return (grad_query, grad_keys, grad_values)

    empty_keys = jnp.zeros((keys_all.shape[0], heads_here, HD), jnp.float32)
    grad_query, grad_keys, grad_values = lax.fori_loop(
        0, needed, back_step, (empty_mix, empty_keys, empty_keys)
    )
    key_grad_part, value_grad_part = (
        lax.psum_scatter(
            grad_keys.astype(jnp.bfloat16), "ctx", scatter_dimension=0, tiled=True
        ).astype(jnp.float32),
        lax.psum_scatter(
            grad_values.astype(jnp.bfloat16), "ctx", scatter_dimension=0, tiled=True
        ).astype(jnp.float32),
    )
    grad_projected = jnp.stack(
        [
            grad_query.reshape(rows, local_width),
            key_grad_part.reshape(rows, local_width),
            value_grad_part.reshape(rows, local_width),
        ],
        axis=1,
    ).astype(jnp.bfloat16)
    in_bias_term = jnp.sum(grad_projected[:, 0::2].astype(jnp.float32), axis=0)
    in_whole = jnp.einsum(
        "td,tcf->dcf", normed_first, grad_projected, preferred_element_type=jnp.float32
    )
    grad_first_share = lax.psum_scatter(
        jnp.einsum(
            "tcf,dcf->td", grad_projected, in_weight, preferred_element_type=jnp.float32
        ).astype(jnp.bfloat16),
        "tensor",
        scatter_dimension=0,
        tiled=True,
    ).astype(jnp.float32)
    normed_again, first_pull = jax.vjp(layer_norm, residual_share, first_norm[0], first_norm[1])
    grad_from_first, first_gain_term, first_shift_term = first_pull(grad_first_share)
    input_grad = (grad_middle_share + grad_from_first).astype(jnp.bfloat16)
    in_weight_grad, out_weight_grad, up_weight_grad, down_weight_grad = (
        lax.psum_scatter(
            in_whole.astype(jnp.bfloat16), ("dp", "ctx"), scatter_dimension=0, tiled=True
        ).astype(jnp.float32),
        lax.psum_scatter(
            out_whole.astype(jnp.bfloat16), ("dp", "ctx"), scatter_dimension=0, tiled=True
        ).astype(jnp.float32),
        lax.psum_scatter(
            up_whole.astype(jnp.bfloat16), ("dp", "ctx"), scatter_dimension=0, tiled=True
        ).astype(jnp.float32),
        lax.psum_scatter(
            down_whole.astype(jnp.bfloat16), ("dp", "ctx"), scatter_dimension=0, tiled=True
        ).astype(jnp.float32),
    )
    in_bias_whole = lax.dynamic_update_slice(
        jnp.zeros((2, width), jnp.float32), in_bias_term, (0, tensor_place * local_width)
    )
    up_bias_whole = lax.dynamic_update_slice(
        jnp.zeros((local_hidden * lax.axis_size("tensor"),), jnp.float32),
        up_bias_term,
        (tensor_place * local_hidden,),
    )
    small_sums = lax.psum(
        (
            first_gain_term,
            first_shift_term,
            in_bias_whole,
            out_bias_term,
            second_gain_term,
            second_shift_term,
            up_bias_whole,
            down_bias_term,
        ),
        ("dp", "ctx", "tensor"),
    )
    in_bias_grad = lax.dynamic_slice_in_dim(
        small_sums[2], tensor_place * local_width, local_width, 1
    )
    up_bias_grad = lax.dynamic_slice_in_dim(
        small_sums[6], tensor_place * local_hidden, local_hidden, 0
    )
    return (
        outputs[None],
        input_grad[None],
        small_sums[0],
        small_sums[1],
        in_weight_grad,
        in_bias_grad,
        out_weight_grad,
        small_sums[3],
        small_sums[4],
        small_sums[5],
        up_weight_grad,
        up_bias_grad,
        down_weight_grad,
        small_sums[7],
    )


def solution(mesh):
    return jax.shard_map(
        shards,
        mesh=mesh,
        in_specs=(
            P("dp", "ctx", None),
            P("dp", None),
            P(),
            P(),
            P(None, None, "tensor"),
            P(None, "tensor"),
            P(None, "tensor"),
            P(),
            P(),
            P(),
            P(None, "tensor"),
            P("tensor"),
            P(None, "tensor"),
            P(),
            P("dp", "ctx", None),
        ),
        out_specs=(
            P("dp", ("ctx", "tensor"), None),
            P("dp", ("ctx", "tensor"), None),
            P(),
            P(),
            P(("dp", "ctx"), None, "tensor"),
            P(None, "tensor"),
            P(("dp", "ctx"), "tensor"),
            P(),
            P(),
            P(),
            P(("dp", "ctx"), "tensor"),
            P("tensor"),
            P(("dp", "ctx"), "tensor"),
            P(),
        ),
        check_vma=False,
    )
```

profile of v0, /device:TPU:0, one launch (start us, length us, event | category | flops | bytes accessed | tf_op | source)
XLA Modules:
  0.0 1117.6 jit_solution(4887311695506873772)
XLA Ops:
  11.7 7.0 fusion.87
  25.9 21.1 %all-gather.7.cloned.1.call-done = bf16[1024,8,128]{2,0,1:T(8,128)(2,1)} async-done(((bf16[256,8,128]{2,0,1:T(8,128)(2,1)}), bf16[1024,8,128]{2,0,1:T(8,128)(2,1)}) %all-gather.7.cloned.1.call-update) | async-done | bytes 2097168 | tf_op jit(solution)/shard_map/all_gather | solution.py:78
  47.0 16.6 %while.50 = (s32[]{:T(128)}, f32[8,256]{1,0:T(8,128)S(1)}, f32[8,256]{1,0:T(8,128)S(1)}, s32[1024]{0:T(1024)S(1)}, s32[256]{0:T(256)S(1)}, /*index=5*/bf16[1024,...) while((s32[]{:T(128)}, f32[8,256]{1,0:T(8,128)S(1)}, ...), condition=%wide.region_5.6_spmd.clone, body=%wide.region_2.5_spmd.clone.sunk | while | flops 281684768 | bytes 12050738 | solution.py:110
  55.7 4.3 fusion.148
  63.6 8.1 all-gather.5.cloned.1.call-done
  71.7 25.0 %while.51 = (s32[]{:T(128)}, f32[256,8,128]{0,2,1:T(8,128)}, f32[256,8,128]{0,2,1:T(8,128)S(1)}, bf16[1024,8,128]{2,0,1:T(8,128)(2,1)}, s32[1024]{0:T(1024)S(1)}...) while((s32[]{:T(128)}, f32[256,8,128]{0,2,1:T(8,128)}, ...), condition=%wide.region_7.8_spmd.clone, body=%wide.region_6.7_spmd.clone.sunk | while | flops 818545408 | bytes 32276812 | solution.py:130
  73.0 5.1 fusion.154
  85.4 5.1 fusion.154
  99.5 4.7 convolution_convert_fusion.5
  105.1 19.6 %reduce-scatter.13.cloned.1.call-done = bf16[128,2048]{1,0:T(8,128)(2,1)} async-done(((bf16[256,2048]{1,0:T(8,128)(2,1)}), bf16[128,2048]{1,0:T(8,128)(2,1)}) %reduce-scatter.13.cloned.1.call-update) | async-done | bytes 524304 | tf_op jit(solution)/shard_map/reduce_scatter | solution.py:133
  127.4 21.4 %all-gather.9.cloned.1.call-done = bf16[256,2048]{1,0:T(8,128)(2,1)} async-done(((bf16[128,2048]{1,0:T(8,128)(2,1)}), bf16[256,2048]{1,0:T(8,128)(2,1)}) %all-gather.9.cloned.1.call-update) | async-done | bytes 1048592 | tf_op jit(solution)/shard_map/all_gather | solution.py:141
  148.8 8.5 convolution_add_fusion
  157.3 12.7 %convert_reduce_fusion = (f32[4096]{0:T(1024)S(1)}, bf16[256,4096]{1,0:T(8,128)(2,1)}) fusion(f32[256,4096]{1,0:T(8,128)S(1)} %convolution_add_fusion, bf16[2048,4096]{1,0:T(8,128)(2,1)} %param.33, bf16[1,256,2048]{2,1,0:T(8,128)(2,1)S(1)} %copy-done.22), kind=kOutput, calls=%fused_computation.85 | convolution fusion | flops 4318031872 | bytes 24133632 | tf_op jit(solution)/shard_map/dot_general | solution.py:160
  170.0 11.9 %convolution_convert_fusion.3 = bf16[256,2048]{1,0:T(8,128)(2,1)} fusion(bf16[256,4096]{1,0:T(8,128)(2,1)} %get-tuple-element.946, bf16[2048,4096]{1,0:T(8,128)(2,1)} %param.31), kind=kOutput, calls=%fused_computation.89 | convolution fusion | flops 4295491584 | bytes 19922944 | tf_op jit(solution)/shard_map/dot_general | solution.py:23
  182.2 13.3 %convolution_convert_fusion.4 = bf16[256,2048]{1,0:T(8,128)(2,1)} fusion(bf16[2048,4096]{1,0:T(8,128)(2,1)} %param.33, f32[256,4096]{1,0:T(8,128)} %copy-done.47), kind=kOutput, calls=%fused_computation.90 | convolution fusion | flops 4304928768 | bytes 22020096 | tf_op jit(solution)/shard_map/dot_general | solution.py:23
  195.6 6.8 reduce-scatter.17.cloned.1.call-done
  206.7 18.2 %reduce-scatter.15.cloned.1.call-done = bf16[128,2048]{1,0:T(8,128)(2,1)} async-done(((bf16[256,2048]{1,0:T(8,128)(2,1)}), bf16[128,2048]{1,0:T(8,128)(2,1)}) %reduce-scatter.15.cloned.1.call-update) | async-done | bytes 524304 | tf_op jit(solution)/shard_map/reduce_scatter | solution.py:147
  230.5 20.8 %all-gather.11.cloned.1.call-done = bf16[256,2048]{1,0:T(8,128)(2,1)} async-done(((bf16[128,2048]{1,0:T(8,128)(2,1)}), bf16[256,2048]{1,0:T(8,128)(2,1)}) %all-gather.11.cloned.1.call-update) | async-done | bytes 1048592 | tf_op jit(solution)/shard_map/all_gather | solution.py:173
  260.6 32.2 %while.52 = (s32[]{:T(128)}, f32[256,8,128]{0,2,1:T(8,128)}, f32[1024,8,128]{2,0,1:T(8,128)}, f32[1024,8,128]{2,0,1:T(8,128)}, bf16[1024,8,128]{2,0,1:T(8,128)(2...) while((s32[]{:T(128)}, f32[256,8,128]{0,2,1:T(8,128)}, ...), condition=%wide.region_17.18_spmd.clone, body=%wide.region_16.17_spmd.clone.sunk | while | flops 1356727040 | bytes 111452632 | solution.py:218
  301.3 27.0 %reduce-scatter.21.cloned.1.call-done = bf16[256,8,128]{2,0,1:T(8,128)(2,1)} async-done(((bf16[1024,8,128]{2,0,1:T(8,128)(2,1)}), bf16[256,8,128]{2,0,1:T(8,128)(2,1)}) %reduce-scatter.21.cloned.1.call-update) | async-done | bytes 524304 | tf_op jit(solution)/shard_map/reduce_scatter | solution.py:225
  329.9 32.4 %reduce-scatter.19.cloned.1.call-done = bf16[256,8,128]{2,0,1:T(8,128)(2,1)} async-done(((bf16[1024,8,128]{2,0,1:T(8,128)(2,1)}), bf16[256,8,128]{2,0,1:T(8,128)(2,1)}) %reduce-scatter.19.cloned.1.call-update) | async-done | bytes 524304 | tf_op jit(solution)/shard_map/reduce_scatter | solution.py:222
  364.0 9.2 fusion.60
  381.9 11.7 %reduce-scatter.23.cloned.1.call-done = bf16[128,2048]{1,0:T(8,128)(2,1)} async-done(((bf16[256,2048]{1,0:T(8,128)(2,1)}), bf16[128,2048]{1,0:T(8,128)(2,1)}) %reduce-scatter.23.cloned.1.call-update) | async-done | bytes 524304 | tf_op jit(solution)/shard_map/reduce_scatter | solution.py:241
  398.2 14.2 %convert_bitcast_fusion = bf16[2048,4096]{0,1:T(8,128)(2,1)} fusion(bf16[1,256,2048]{2,1,0:T(8,128)(2,1)} %param.35, f32[256,4096]{1,0:T(8,128)} %copy-done.47), kind=kOutput, calls=%fused_computation.72 | convolution fusion | flops 4312793088 | bytes 22020096 | tf_op jit(solution)/shard_map/dot_general | solution.py:23
  412.5 21.0 %copy.68 = bf16[2048,4096]{1,0:T(8,128)(2,1)} copy(bf16[2048,4096]{0,1:T(8,128)(2,1)} %convert_bitcast_fusion) | data formatting | bytes 33554432
  434.7 9.9 convolution_convert_fusion
  445.9 8.0 convolution_convert_fusion.1
  453.9 16.0 %reduce-scatter.27.cloned.1.call-done = bf16[128,1024]{1,0:T(8,128)(2,1)} async-done(((bf16[2048,1024]{1,0:T(8,128)(2,1)}), bf16[128,1024]{1,0:T(8,128)(2,1)}) %reduce-scatter.27.cloned.1.call-update) | async-done | bytes 262160 | tf_op jit(solution)/shard_map/reduce_scatter | solution.py:256
  473.9 127.5 %all-reduce.3.cloned.1.call-done = (f32[2048]{0:T(1024)}, f32[2048]{0:T(1024)}, f32[2,2048]{1,0:T(2,128)}, f32[2048]{0:T(1024)}, f32[2048]{0:T(1024)}, /*index=5*/f32[2048]{0:T(1024)}, f32[8192]{0:T(1024)}, f32[2048]{0:T(1024)}) async-done(((f32[2048]{0:T(1024)}, f32[2048]{0:T(1024)}, f32[2,2048]{1,0:T(2,128)}, f32[2048]{0:T(1024)}, f32[2048]{0:T(1024)}, /*index=5*/f32[2048]{0:T(1024)}, f32[8192]{0:T(1024)}, ...) | async-done | bytes 98320 | tf_op jit(solution)/shard_map/psum | solution.py:274
  604.0 181.2 %reduce-scatter.31.cloned.1.call-done = bf16[128,4096]{1,0:T(8,128)(2,1)} async-done(((bf16[2048,4096]{1,0:T(8,128)(2,1)}), bf16[128,4096]{1,0:T(8,128)(2,1)}) %reduce-scatter.31.cloned.1.call-update) | async-done | bytes 1048592
  788.5 178.3 %reduce-scatter.29.cloned.1.call-done = bf16[128,4096]{1,0:T(8,128)(2,1)} async-done(((bf16[2048,4096]{1,0:T(8,128)(2,1)}), bf16[128,4096]{1,0:T(8,128)(2,1)}) %reduce-scatter.29.cloned.1.call-update) | async-done | bytes 1048592 | tf_op jit(solution)/shard_map/reduce_scatter | solution.py:259
  969.5 134.9 %reduce-scatter.25.cloned.1.call-done = bf16[128,3,1024]{2,0,1:T(8,128)(2,1)} async-done(((bf16[2048,3,1024]{2,0,1:T(8,128)(2,1)}), bf16[128,3,1024]{2,0,1:T(8,128)(2,1)}) %reduce-scatter.25.cloned.1.call-update) | async-done | bytes 786448 | tf_op jit(solution)/shard_map/reduce_scatter | solution.py:253
  (281 shorter events, 142.2 us)
Async XLA Ops:
  7.2 39.8 %all-gather.7.cloned.1.call-start = ((), (), s32[]{:S(2)}) async-start(), calls=%async_computation.11 | async-start | bytes 2621440 | tf_op jit(solution)/shard_map/all_gather | solution.py:78
  21.5 50.2 %all-gather.5.cloned.1.call-start = ((), (), s32[]{:S(2)}) async-start(), calls=%async_computation.10 | async-start | bytes 2621440 | tf_op jit(solution)/shard_map/all_gather | solution.py:79
  24.5 100.1 %reduce-scatter.13.cloned.1.call-start = ((), (), s32[]{:S(2)}) async-start(), calls=%async_computation.12 | async-start | bytes 1572864 | tf_op jit(solution)/shard_map/reduce_scatter | solution.py:133
  104.2 23.1 %copy-start.30 = (bf16[4096]{0:T(1024)(128)(2,1)S(1)}, bf16[4096]{0:T(1024)(128)(2,1)}, u32[]{:S(2)}) copy-start(bf16[4096]{0:T(1024)(128)(2,1)} %param.32) | copy-start | bytes 24580
  104.2 44.5 %all-gather.9.cloned.1.call-start = ((), (), s32[]{:S(2)}) async-start(), calls=%async_computation.13 | async-start | bytes 1572864 | tf_op jit(solution)/shard_map/all_gather | solution.py:141
  105.0 52.3 %copy-start.7 = (f32[1,256,2048]{2,1,0:T(8,128)}, f32[1,256,2048]{2,1,0:T(8,128)S(1)}, u32[]{:S(2)}) copy-start(f32[1,256,2048]{2,1,0:T(8,128)S(1)} %convert_element_type.219) | copy-start | bytes 6291460
  127.3 75.1 %reduce-scatter.17.cloned.1.call-start = ((), (), s32[]{:S(2)}) async-start(), calls=%async_computation.15 | async-start | bytes 1572864 | tf_op jit(solution)/shard_map/reduce_scatter | solution.py:164
  181.9 13.6 %copy-start.42 = (bf16[2048]{0:T(1024)(128)(2,1)S(1)}, bf16[2048]{0:T(1024)(128)(2,1)}, u32[]{:S(2)}) copy-start(bf16[2048]{0:T(1024)(128)(2,1)} %param.34) | copy-start | bytes 12292
  181.9 42.9 %reduce-scatter.15.cloned.1.call-start = ((), (), s32[]{:S(2)}) async-start(), calls=%async_computation.14 | async-start | bytes 1572864 | tf_op jit(solution)/shard_map/reduce_scatter | solution.py:147
  195.5 29.4 %copy-start.23 = (bf16[1,256,2048]{2,1,0:T(8,128)(2,1)S(1)}, bf16[1,256,2048]{2,1,0:T(8,128)(2,1)}, u32[]{:S(2)}) copy-start(bf16[1,256,2048]{2,1,0:T(8,128)(2,1)} %param.35) | copy-start | bytes 3145732
  195.5 55.9 %all-gather.11.cloned.1.call-start = ((), (), s32[]{:S(2)}) async-start(), calls=%async_computation.16 | async-start | bytes 1572864 | tf_op jit(solution)/shard_map/all_gather | solution.py:173
  204.4 25.8 %copy-start.13 = (f32[256,8,128]{0,2,1:T(8,128)S(1)}, f32[256,8,128]{0,2,1:T(8,128)}, u32[]{:S(2)}) copy-start(f32[256,8,128]{0,2,1:T(8,128)} %get-tuple-element.938) | copy-start | bytes 3145732
  229.9 98.4 %reduce-scatter.21.cloned.1.call-start = ((), (), s32[]{:S(2)}) async-start(), calls=%async_computation.18 | async-start | bytes 2621440 | tf_op jit(solution)/shard_map/reduce_scatter | solution.py:225
  296.7 65.6 %reduce-scatter.19.cloned.1.call-start = ((), (), s32[]{:S(2)}) async-start(), calls=%async_computation.17 | async-start | bytes 2621440 | tf_op jit(solution)/shard_map/reduce_scatter | solution.py:222
  300.7 92.9 %reduce-scatter.23.cloned.1.call-start = ((), (), s32[]{:S(2)}) async-start(), calls=%async_computation.19 | async-start | bytes 1572864 | tf_op jit(solution)/shard_map/reduce_scatter | solution.py:241
  301.3 79.1 %copy-start.18 = (bf16[256,1,1024]{2,0,1:T(8,128)(2,1)}, bf16[256,1,1024]{2,0,1:T(8,128)(2,1)S(1)}, u32[]{:S(2)}) copy-start(bf16[256,1,1024]{2,0,1:T(8,128)(2,1)S(1)} %copy.66) | copy-start | bytes 1572868
  329.9 50.5 %copy-start.19 = (bf16[256,1,1024]{2,0,1:T(8,128)(2,1)}, bf16[256,1,1024]{2,0,1:T(8,128)(2,1)S(1)}, u32[]{:S(2)}) copy-start(bf16[256,1,1024]{2,0,1:T(8,128)(2,1)S(1)} %stack_reshape.14) | copy-start | bytes 1572868
  373.2 96.7 %reduce-scatter.27.cloned.1.call-start = ((), (), s32[]{:S(2)}) async-start(), calls=%async_computation.21 | async-start | bytes 4456448 | tf_op jit(solution)/shard_map/reduce_scatter | solution.py:256
  376.5 17.1 %copy-start.26 = (f32[2048]{0:T(1024)S(1)}, f32[2048]{0:T(1024)}, u32[]{:S(2)}) copy-start(f32[2048]{0:T(1024)} %copy-done.25) | copy-start | bytes 24580
  376.5 224.9 %all-reduce.3.cloned.1.call-start = ((), (), s32[]{:S(2)}) async-start(), calls=%async_computation.24 | async-start | bytes 196608 | tf_op jit(solution)/shard_map/psum | solution.py:274
  380.4 17.5 %copy-start.27 = (f32[8192]{0:T(1024)}, f32[8192]{0:T(1024)S(1)}, u32[]{:S(2)}) copy-start(f32[8192]{0:T(1024)S(1)} %dynamic_update_slice.21) | copy-start | bytes 98308
  381.9 16.0 %copy-start.28 = (f32[2,2048]{1,0:T(2,128)}, f32[2,2048]{1,0:T(2,128)S(1)}, u32[]{:S(2)}) copy-start(f32[2,2048]{1,0:T(2,128)S(1)} %constant_dynamic-update-slice_fusion) | copy-start | bytes 49156
  397.9 387.3 %reduce-scatter.31.cloned.1.call-start = ((), (), s32[]{:S(2)}) async-start(), calls=%async_computation.23 | async-start | bytes 17825792
  433.5 533.3 %reduce-scatter.29.cloned.1.call-start = ((), (), s32[]{:S(2)}) async-start(), calls=%async_computation.22 | async-start | bytes 17825792 | tf_op jit(solution)/shard_map/reduce_scatter | solution.py:259
  444.7 659.8 %reduce-scatter.25.cloned.1.call-start = ((), (), s32[]{:S(2)}) async-start(), calls=%async_computation.20 | async-start | bytes 13369344 | tf_op jit(solution)/shard_map/reduce_scatter | solution.py:253
  453.8 17.9 %copy-start.12 = (f32[128,2048]{1,0:T(8,128)S(1)}, f32[128,2048]{1,0:T(8,128)}, u32[]{:S(2)}) copy-start(f32[128,2048]{1,0:T(8,128)} %copy-done.11) | copy-start | bytes 3145732
  786.8 320.1 %copy-start.38 = (f32[2048]{0:T(1024)S(1)}, f32[2048]{0:T(1024)}, u32[]{:S(2)}) copy-start(f32[2048]{0:T(1024)} %get-tuple-element.1320) | copy-start | bytes 24580
  786.8 320.7 %copy-start.37 = (f32[2048]{0:T(1024)S(1)}, f32[2048]{0:T(1024)}, u32[]{:S(2)}) copy-start(f32[2048]{0:T(1024)} %get-tuple-element.1321) | copy-start | bytes 24580
  786.8 321.3 %copy-start.36 = (f32[2048]{0:T(1024)S(1)}, f32[2048]{0:T(1024)}, u32[]{:S(2)}) copy-start(f32[2048]{0:T(1024)} %get-tuple-element.1325) | copy-start | bytes 24580
  786.9 321.9 %copy-start.35 = (f32[2048]{0:T(1024)S(1)}, f32[2048]{0:T(1024)}, u32[]{:S(2)}) copy-start(f32[2048]{0:T(1024)} %get-tuple-element.1326) | copy-start | bytes 24580
  786.9 322.5 %copy-start.34 = (f32[2048]{0:T(1024)S(1)}, f32[2048]{0:T(1024)}, u32[]{:S(2)}) copy-start(f32[2048]{0:T(1024)} %get-tuple-element.1327) | copy-start | bytes 24580
  786.9 323.1 %copy-start.33 = (f32[2048]{0:T(1024)S(1)}, f32[2048]{0:T(1024)}, u32[]{:S(2)}) copy-start(f32[2048]{0:T(1024)} %get-tuple-element.1331) | copy-start | bytes 24580
  (37 other events, 177.4 us)
Sparse Core Ops, SparseCore 0:
  21.7 25.2 all-gather.6
  49.1 22.5 all-gather.4
  104.3 20.3 reduce-scatter.12
  127.4 21.2 all-gather.8
  182.1 20.3 reduce-scatter.16
  204.5 20.3 reduce-scatter.14
  230.0 21.2 all-gather.10
  296.8 31.4 reduce-scatter.20
  330.8 31.4 reduce-scatter.18
  373.3 20.2 reduce-scatter.22
  397.5 72.3 reduce-scatter.26
  478.5 122.9 all-reduce.2
  605.5 179.6 reduce-scatter.30
  789.2 177.5 reduce-scatter.28
  970.7 133.7 reduce-scatter.24
where the time goes:
time: 1130 us; the launch traced here: 1120 us
  waiting for transfers between devices  825 us (73%)
  matrix products  161 us (14%)
  local copies, waits for them, and re-layouts  57.5 us (5%)
  other arithmetic  56.4 us (5%)
  between operations  15.2 us (1%)
    unnamed x16, waiting for transfers between devices  181 us
    reduce_scatter x1, waiting for transfers between devices, shards(): lax.psum_scatter(up_whole.astype(jnp.bfloat16), ('dp', 'ctx'), scatter_di...  178 us
    reduce_scatter x1, waiting for transfers between devices, shards(): lax.psum_scatter(in_whole.astype(jnp.bfloat16), ('dp', 'ctx'), scatter_di...  135 us
    psum x1, waiting for transfers between devices, shards(): lax.psum((first_gain_term, first_shift_term, in_bias_whole, out_bias_term...  127 us
    dot_general x6, matrix products, contract(): lax.dot_general(left, right, (((left_dim,), (right_dim,)), ((), ())), pre...  57.3 us
    unnamed x101, local copies, waits for them, and re-layouts  37 us
    reduce_scatter x1, waiting for transfers between devices, shards(): lax.psum_scatter(grad_keys.astype(jnp.bfloat16), 'ctx', scatter_dimension...  32.4 us
    reduce_scatter x1, waiting for transfers between devices, shards(): lax.psum_scatter(grad_values.astype(jnp.bfloat16), 'ctx', scatter_dimensi...  27 us
  transfers between devices with their start and end apart: 15, of which 15 were waited for; matrix products, arithmetic and copies ran while one was open for 11% of the time, Pallas kernels for 0%

commit v1 on v0

v1 whole, which is shorter than its diff:
```python
import functools
import math

import jax
import jax.numpy as jnp
from jax import lax
from jax.experimental import pallas as pl
from jax.experimental.pallas import tpu as pltpu
from jax.sharding import PartitionSpec as P

H = 16
HD = 128
EPSILON = 1e-05
MASKED = -1e30
MIB = 1 << 20
GELU_C = math.sqrt(2.0 / math.pi)
GELU_A = 0.044715

BF16 = jnp.bfloat16
F32 = jnp.float32


def params(limit):
    return pltpu.CompilerParams(vmem_limit_bytes=limit * MIB)


def cost(flops, nbytes, trans=0):
    return pl.CostEstimate(
        flops=int(flops), bytes_accessed=int(nbytes), transcendentals=int(trans)
    )


def xperm(values, axis, bit, wanted=None):
    pairs = [
        (i, i ^ bit) for i in range(lax.axis_size(axis)) if wanted is None or wanted(i)
    ]
    return lax.ppermute(values, axis, pairs)


def after(values, *deps):
    return lax.optimization_barrier((values,) + deps)[0]


def ctx_bits():
    n = lax.axis_size("ctx")
    return [1 << b for b in reversed(range(n.bit_length() - 1))]


def ctx_offsets():
    offsets = [0]
    for bit in ctx_bits():
        offsets = offsets + [o ^ bit for o in offsets]
    return offsets


def gather_ctx(block):
    blocks = [block]
    for bit in ctx_bits():
        blocks = blocks + [xperm(b, "ctx", bit) for b in blocks]
    return blocks


def gather_ctx_causal(block):
    blocks, offsets = [block], [0]
    for bit in ctx_bits():
        fresh = []
        for b, o in zip(blocks, offsets):
            fresh.append(
                xperm(b, "ctx", bit, lambda i, o=o, bit=bit: (i ^ o) < (i ^ bit))
            )
        blocks = blocks + fresh
        offsets = offsets + [o ^ bit for o in offsets]
    return blocks


def mm_kernel(*refs, n_pairs, trans):
    lefts, rights = refs[:n_pairs], refs[n_pairs : 2 * n_pairs]
    extras, out = refs[2 * n_pairs : -1], refs[-1]
    total = None
    for left, right in zip(lefts, rights):
        term = lax.dot_general(
            left[...],
            right[...],
            (((1,), (1 if trans else 0,)), ((), ())),
            preferred_element_type=F32,
        )
        total = term if total is None else total + term
    for extra in extras:
        total = total + extra[...].astype(F32)
    out[...] = total.astype(out.dtype)


def mm(lefts, rights, *, trans, start, size, tile, out_dtype, extras=()):
    rows = lefts[0].shape[0]
    tile = min(tile, size)
    first = start // tile
    specs, operands = [], []
    flops = nbytes = 0
    for left in lefts:
        specs.append(pl.BlockSpec(left.shape, lambda i: (0, 0)))
        operands.append(left)
        nbytes += left.size * 2
        flops += 2 * left.size * size
    for left, right in zip(lefts, rights):
        depth = left.shape[1]
        lead = None
        if isinstance(right, tuple):
            right, lead = right
        shape = (tile, depth) if trans else (depth, tile)
        place = (
            (lambda i, lead=lead: ((lead,) if lead is not None else ()) + (first + i, 0))
            if trans
            else (lambda i, lead=lead: ((lead,) if lead is not None else ()) + (0, first + i))
        )
        specs.append(pl.BlockSpec(((None,) if lead is not None else ()) + shape, place))
        operands.append(right)
        nbytes += depth * size * 2
    for extra in extras:
        specs.append(pl.BlockSpec((extra.shape[0], tile), lambda i: (0, first + i)))
        operands.append(extra)
        nbytes += extra.shape[0] * size * extra.dtype.itemsize
    nbytes += rows * size * jnp.dtype(out_dtype).itemsize
    return pl.pallas_call(
        functools.partial(mm_kernel, n_pairs=len(lefts), trans=trans),
        grid=(size // tile,),
        in_specs=specs,
        out_specs=pl.BlockSpec((rows, tile), lambda i: (0, i)),
        out_shape=jax.ShapeDtypeStruct((rows, size), out_dtype),
        compiler_params=params(40),
        cost_estimate=cost(flops, nbytes),
    )(*operands)


def kv_kernel(norm, weight, bias, out):
    total = jnp.dot(norm[...], weight[...], preferred_element_type=F32)
    out[...] = (total + bias[...]).astype(out.dtype)


def project_kv(norm, weight, bias, start, size, tile):
    rows, width = norm.shape
    tile = min(tile, size)
    first = start // tile
    return pl.pallas_call(
        kv_kernel,
        grid=(2, size // tile),
        in_specs=[
            pl.BlockSpec((rows, width), lambda c, i: (0, 0)),
            pl.BlockSpec((None, width, tile), lambda c, i: (c + 1, 0, first + i)),
            pl.BlockSpec((None, 1, tile), lambda c, i: (c, 0, first + i)),
        ],
        out_specs=pl.BlockSpec((None, rows, tile), lambda c, i: (c, 0, i)),
        out_shape=jax.ShapeDtypeStruct((2, rows, size), BF16),
        compiler_params=params(40),
        cost_estimate=cost(4 * rows * width * size, 4 * width * size),
    )(norm, weight, bias)


def up_kernel(norm, weight, bias, grad_active, active, grad_upper, bias_sum):
    upper = jnp.dot(norm[...], weight[...], preferred_element_type=F32) + bias[...]
    square = upper * upper
    wave = jnp.tanh(GELU_C * (upper + GELU_A * square * upper))
    half = 0.5 * (1.0 + wave)
    active[...] = (upper * half).astype(BF16)
    slope = half + 0.5 * upper * (1.0 - wave * wave) * (
        GELU_C * (1.0 + 3.0 * GELU_A * square)
    )
    grad = (grad_active[...] * slope).astype(BF16)
    grad_upper[...] = grad
    bias_sum[...] = jnp.sum(grad.astype(F32), axis=0, keepdims=True)


def up_and_gelu(norm, weight, bias, grad_active, start, size, tile):
    rows, width = norm.shape
    tile = min(tile, size)
    first = start // tile
    block = pl.BlockSpec((rows, tile), lambda i: (0, i))
    return pl.pallas_call(
        up_kernel,
        grid=(size // tile,),
        in_specs=[
            pl.BlockSpec((rows, width), lambda i: (0, 0)),
            pl.BlockSpec((width, tile), lambda i: (0, first + i)),
            pl.BlockSpec((1, tile), lambda i: (0, first + i)),
            pl.BlockSpec((rows, tile), lambda i: (0, first + i)),
        ],
        out_specs=[block, block, pl.BlockSpec((1, tile), lambda i: (0, i))],
        out_shape=[
            jax.ShapeDtypeStruct((rows, size), BF16),
            jax.ShapeDtypeStruct((rows, size), BF16),
            jax.ShapeDtypeStruct((1, size), F32),
        ],
        compiler_params=params(40),
        cost_estimate=cost(
            2 * rows * width * size, 2 * width * size + 8 * rows * size, rows * size
        ),
    )(norm, weight, bias, grad_active)


def weight_grad_kernel(place, left, *refs, offsets):
    rights, out = refs[:-1], refs[-1]
    total = None
    for right, offset in zip(rights, offsets):
        term = jnp.dot(
            left[place[0] ^ offset], right[...], preferred_element_type=F32
        )
        total = term if total is None else total + term
    out[...] = total.astype(out.dtype)


def weight_grad(place, left, rights, tile):
    rows = left.shape[1]
    tokens, size = rights[0].shape
    tile = min(tile, size)
    return pl.pallas_call(
        functools.partial(weight_grad_kernel, offsets=ctx_offsets()),
        grid_spec=pltpu.PrefetchScalarGridSpec(
            num_scalar_prefetch=1,
            grid=(size // tile,),
            in_specs=[pl.BlockSpec(left.shape, lambda i, place: (0, 0, 0))]
            + [pl.BlockSpec((tokens, tile), lambda i, place: (0, i)) for _ in rights],
            out_specs=pl.BlockSpec((rows, tile), lambda i, place: (0, i)),
        ),
        out_shape=jax.ShapeDtypeStruct((rows, size), BF16),
        compiler_params=params(40),
        cost_estimate=cost(
            2 * left.size * size, 2 * (left.size + len(rights) * tokens * size + rows * size)
        ),
    )(place, left, *rights)


def block_scores(place, slope, query, key, start_row, offset):
    rows = query.shape[0]
    raw = lax.dot_general(
        key, query, (((1,), (1,)), ((), ())), preferred_element_type=F32
    ) * (1.0 / math.sqrt(HD))
    shape = raw.shape
    key_pos = (place[0] ^ offset) * rows + lax.broadcasted_iota(jnp.int32, shape, 0)
    query_pos = place[0] * rows + lax.broadcasted_iota(jnp.int32, shape, 1)
    raw = raw + slope * (key_pos - query_pos).astype(F32)
    allowed = (key_pos <= query_pos) & (key_pos >= start_row)
    return raw, allowed


def forward_kernel(place, slopes, query, start, *refs, offsets, first_head):
    n = len(offsets)
    keyvals, (mixed, stats), (held,) = refs[:n], refs[n : n + 2], refs[n + 2 :]
    slope = slopes[first_head + pl.program_id(0)]
    top = None
    for k, offset in enumerate(offsets):
        raw, allowed = block_scores(
            place, slope, query[...], keyvals[k][0], start[...], offset
        )
        raw = jnp.where(allowed, raw, MASKED)
        held[k] = raw
        peak = jnp.max(raw, axis=0, keepdims=True)
        top = peak if top is None else jnp.maximum(top, peak)
    total = None
    for k in range(n):
        fresh = jnp.exp(held[k] - top)
        held[k] = fresh
        part = jnp.sum(fresh, axis=0, keepdims=True)
        total = part if total is None else total + part
    stats[...] = top + jnp.log(total)
    inverse = 1.0 / total
    result = None
    for k in range(n):
        probs = (held[k] * inverse).astype(BF16)
        term = lax.dot_general(
            probs, keyvals[k][1], (((0,), (0,)), ((), ())), preferred_element_type=F32
        )
        result = term if result is None else result + term
    mixed[...] = result.astype(mixed.dtype)


def attention_forward(place, slopes, query, start, keyvals, first_head, heads):
    rows = query.shape[0]
    n = len(keyvals)
    grid_spec = pltpu.PrefetchScalarGridSpec(
        num_scalar_prefetch=2,
        grid=(heads,),
        in_specs=[
            pl.BlockSpec((rows, HD), lambda h, *_: (0, first_head + h)),
            pl.BlockSpec((1, rows), lambda h, *_: (0, 0)),
        ]
        + [pl.BlockSpec((2, rows, HD), lambda h, *_: (0, 0, h))] * n,
        out_specs=[
            pl.BlockSpec((rows, HD), lambda h, *_: (0, h)),
            pl.BlockSpec((None, 1, rows), lambda h, *_: (h, 0, 0)),
        ],
        scratch_shapes=[pltpu.VMEM((n, rows, rows), F32)],
    )
    return pl.pallas_call(
        functools.partial(forward_kernel, offsets=ctx_offsets(), first_head=first_head),
        grid_spec=grid_spec,
        out_shape=[
            jax.ShapeDtypeStruct((rows, heads * HD), BF16),
            jax.ShapeDtypeStruct((heads, 1, rows), F32),
        ],
        compiler_params=params(40),
        cost_estimate=cost(
            4 * n * rows * rows * HD * heads,
            4 * n * rows * HD * heads,
            n * rows * rows * heads,
        ),
    )(place, slopes, query, start, *keyvals)


def backward_kernel(
    place, slopes, query, grad_mixed, start, stats, *refs, offsets, first_head
):
    n = len(offsets)
    keyvals = refs[:n]
    grad_query, near, far, probs_held, grads_held = refs[n:]
    slope = slopes[first_head + pl.program_id(0)]
    scale = 1.0 / math.sqrt(HD)
    delta = None
    for k, offset in enumerate(offsets):
        raw, allowed = block_scores(
            place, slope, query[...], keyvals[k][0], start[...], offset
        )
        probs = jnp.where(allowed, jnp.exp(raw - stats[...]), 0.0)
        grads = lax.dot_general(
            keyvals[k][1],
            grad_mixed[...],
            (((1,), (1,)), ((), ())),
            preferred_element_type=F32,
        )
        probs_held[k] = probs
        grads_held[k] = grads
        part = jnp.sum(probs * grads, axis=0, keepdims=True)
        delta = part if delta is None else delta + part
    total = None
    for k, offset in enumerate(offsets):
        probs = probs_held[k]
        grad_scores = (probs * (grads_held[k] - delta)).astype(BF16)
        term = lax.dot_general(
            grad_scores,
            keyvals[k][0],
            (((0,), (0,)), ((), ())),
            preferred_element_type=F32,
        )
        total = term if total is None else total + term
        key_grad = jnp.dot(grad_scores, query[...], preferred_element_type=F32) * scale
        value_grad = jnp.dot(
            probs.astype(BF16), grad_mixed[...], preferred_element_type=F32
        )
        target, slot = (near, k) if k < n - n // 2 else (far, k - (n - n // 2))
        target[0, slot] = key_grad.astype(target.dtype)
        target[1, slot] = value_grad.astype(target.dtype)
    grad_query[...] = (total * scale).astype(grad_query.dtype)


def attention_backward(
    place, slopes, query, grad_mixed, start, stats, keyvals, first_head, heads
):
    rows = query.shape[0]
    n = len(keyvals)
    n_far = n // 2
    n_near = n - n_far
    grid_spec = pltpu.PrefetchScalarGridSpec(
        num_scalar_prefetch=2,
        grid=(heads,),
        in_specs=[
            pl.BlockSpec((rows, HD), lambda h, *_: (0, first_head + h)),
            pl.BlockSpec((rows, HD), lambda h, *_: (0, first_head + h)),
            pl.BlockSpec((1, rows), lambda h, *_: (0, 0)),
            pl.BlockSpec((None, 1, rows), lambda h, *_: (h, 0, 0)),
        ]
        + [pl.BlockSpec((2, rows, HD), lambda h, *_: (0, 0, h))] * n,
        out_specs=[
            pl.BlockSpec((rows, HD), lambda h, *_: (0, h)),
            pl.BlockSpec((2, n_near, rows, HD), lambda h, *_: (0, 0, 0, h)),
            pl.BlockSpec((2, max(n_far, 1), rows, HD), lambda h, *_: (0, 0, 0, h)),
        ],
        scratch_shapes=[pltpu.VMEM((n, rows, rows), F32)] * 2,
    )
    return pl.pallas_call(
        functools.partial(backward_kernel, offsets=ctx_offsets(), first_head=first_head),
        grid_spec=grid_spec,
        out_shape=[
            jax.ShapeDtypeStruct((rows, heads * HD), BF16),
            jax.ShapeDtypeStruct((2, n_near, rows, heads * HD), BF16),
            jax.ShapeDtypeStruct((2, max(n_far, 1), rows, heads * HD), BF16),
        ],
        compiler_params=params(40),
        cost_estimate=cost(
            10 * n * rows * rows * HD * heads,
            8 * n * rows * HD * heads,
            n * rows * rows * heads,
        ),
    )(place, slopes, query, grad_mixed, start, stats, *keyvals)


def normalized(values):
    average = jnp.mean(values, axis=-1, keepdims=True)
    centered = values - average
    spread = jnp.mean(centered * centered, axis=-1, keepdims=True)
    inverse = lax.rsqrt(spread + EPSILON)
    return centered * inverse, inverse


def norm_backward(grad, unit, inverse, gain):
    scaled = grad * gain
    mean_scaled = jnp.mean(scaled, axis=-1, keepdims=True)
    mean_unit = jnp.mean(scaled * unit, axis=-1, keepdims=True)
    return inverse * (scaled - mean_scaled - unit * mean_unit)


def all_sum(values, axes):
    for axis in axes:
        bit = 1
        while bit < lax.axis_size(axis):
            values = values + xperm(values, axis, bit)
            bit *= 2
    return values


def spread_left(values):
    tokens, width = values.shape
    n_dp, n_ctx = lax.axis_size("dp"), lax.axis_size("ctx")
    grid = values.reshape(tokens, n_dp, n_ctx, width // (n_dp * n_ctx))
    parts = grid.transpose(2, 1, 3, 0).reshape(n_ctx, width // n_ctx, tokens)
    return lax.all_to_all(parts, "ctx", 0, 0, tiled=True)


def shards(
    inputs,
    segments,
    first_gain,
    first_shift,
    in_weight,
    in_bias,
    out_weight,
    out_bias,
    second_gain,
    second_shift,
    up_weight,
    up_bias,
    down_weight,
    down_bias,
    cotangent,
):
    rows = inputs.shape[1]
    width = inputs.shape[2]
    local_width = in_weight.shape[2]
    local_hidden = up_weight.shape[1]
    heads_here = local_width // HD
    n_tensor = lax.axis_size("tensor")
    n_ctx = lax.axis_size("ctx")
    share = rows // n_tensor
    tensor_place = lax.axis_index("tensor")
    context_place = lax.axis_index("ctx")
    place = context_place.astype(jnp.int32).reshape(1)
    share_start = tensor_place * share

    def mine(values):
        return lax.dynamic_slice_in_dim(values, share_start, share, 0)

    head_index = (tensor_place * heads_here).astype(F32) + jnp.arange(heads_here, dtype=F32)
    slopes = jnp.exp2(-8.0 * (head_index + 1.0) / H)
    query_seg = lax.dynamic_slice_in_dim(segments[0], context_place * rows, rows)
    doc_start = jnp.sum(
        (segments[0][:, None] < query_seg[None, :]).astype(jnp.int32), axis=0, keepdims=True
    )

    gain_one, shift_one = first_gain.astype(F32), first_shift.astype(F32)
    gain_two, shift_two = second_gain.astype(F32), second_shift.astype(F32)
    weight_in = in_weight.transpose(1, 0, 2)
    bias_pair = in_bias.astype(F32)
    cot_low = cotangent[0]

    half_width = local_width // 2
    pair_place = context_place & 1
    out_half = lax.dynamic_slice_in_dim(out_weight, pair_place * half_width, half_width, 1)
    out_halves = [xperm(out_half, "tensor", k) for k in range(1, n_tensor)]

    residual = inputs[0]
    unit_one, _ = normalized(residual.astype(F32))
    normed_first = (unit_one * gain_one + shift_one).astype(BF16)

    groups = 2 if heads_here % 2 == 0 else 1
    group_heads = heads_here // groups
    group_width = group_heads * HD
    kv_bias = jnp.stack([jnp.zeros_like(bias_pair[1]), bias_pair[1]])[:, None, :]
    own = [
        project_kv(normed_first, weight_in, kv_bias, g * group_width, group_width, 512)
        for g in range(groups)
    ]
    keyvals = [gather_ctx_causal(block) for block in own]
    query = mm(
        [normed_first], [(weight_in, 0)], trans=False, start=0, size=local_width, tile=512,
        out_dtype=BF16, extras=(bias_pair[0:1],),
    )
    grad_active = mm(
        [cot_low], [down_weight], trans=False, start=0, size=local_hidden, tile=512, out_dtype=F32,
    )
    out_others = [
        (half, xperm(half, "ctx", 1)) for half in out_halves
    ]
    keyvals, grad_active = lax.optimization_barrier((keyvals, grad_active))

    mixed_parts, stats = [], []
    mixed_others = [[] for _ in range(1, n_tensor)]
    for g in range(groups):
        part, stat = attention_forward(
            place, slopes, query, doc_start, keyvals[g], g * group_heads, group_heads
        )
        mixed_parts.append(part)
        stats.append(stat)
        for k in range(1, n_tensor):
            mixed_others[k - 1].append(xperm(part, "tensor", k))
    mixed = jnp.concatenate(mixed_parts, axis=1) if groups > 1 else mixed_parts[0]
    lefts, rights = [mixed], [out_weight]
    for parts, (half, other_half) in zip(mixed_others, out_others):
        whole = jnp.concatenate(parts, axis=1) if groups > 1 else parts[0]
        lefts.append(lax.dynamic_slice_in_dim(whole, pair_place * half_width, half_width, 1))
        rights.append(half)
        lefts.append(lax.dynamic_slice_in_dim(whole, (1 - pair_place) * half_width, half_width, 1))
        rights.append(other_half)
    middle = mm(
        lefts, rights, trans=True, start=0, size=width, tile=512, out_dtype=F32,
        extras=(residual, out_bias.astype(F32)[None]),
    )
    unit_two, inverse_two = normalized(middle)
    normed_second = (unit_two * gain_two + shift_two).astype(BF16)

    left_down = spread_left(cot_low)
    left_in = spread_left(normed_first)
    left_up = spread_left(normed_second)

    chunks = 2
    chunk = local_hidden // chunks
    actives, grad_uppers, up_bias_parts = [], [], []
    up_bias_row = up_bias.astype(F32)[None]
    for i in range(chunks):
        active, grad_upper, bias_part = up_and_gelu(
            normed_second, up_weight, up_bias_row, grad_active, i * chunk, chunk, 512
        )
        actives.append(active)
        grad_uppers.append(grad_upper)
        up_bias_parts.append(bias_part)

    def reduced(left, right, tile=512):
        whole = weight_grad(place, left, gather_ctx(right), tile)
        return lax.psum_scatter(whole, "dp", scatter_dimension=0, tiled=True)

    down_parts = [reduced(left_down, active) for active in actives]
    up_parts = [reduced(left_up, grad) for grad in grad_uppers]

    grad_hidden = jnp.concatenate(grad_uppers, axis=1)
    halves = 2
    grad_normed = []
    for i in range(halves):
        part = mm(
            [grad_hidden], [up_weight], trans=True, start=i * (width // halves),
            size=width // halves, tile=256, out_dtype=BF16,
        )
        total = part.astype(F32)
        for k in range(1, n_tensor):
            total = total + xperm(part, "tensor", k).astype(F32)
        grad_normed.append(total)
    grad_normed = jnp.concatenate(grad_normed, axis=1)
    cot = cot_low.astype(F32)
    grad_middle = cot + norm_backward(grad_normed, unit_two, inverse_two, gain_two)
    grad_middle_low = grad_middle.astype(BF16)
    grad_mixed = mm(
        [grad_middle_low], [out_weight], trans=False, start=0, size=local_width, tile=512,
        out_dtype=BF16,
    )
    left_out = spread_left(grad_middle_low)
    out_part = reduced(left_out, mixed)

    active_late = after(jnp.concatenate(actives, axis=1), grad_mixed)
    feed = mm(
        [active_late], [down_weight], trans=True, start=0, size=width, tile=256, out_dtype=BF16
    )

    def tensor_scatter(values):
        total = mine(values).astype(F32)
        for k in range(1, n_tensor):
            piece = lax.dynamic_slice_in_dim(values, (tensor_place ^ k) * share, share, 0)
            total = total + xperm(piece, "tensor", k).astype(F32)
        return total

    outputs = (mine(middle) + tensor_scatter(feed) + down_bias.astype(F32)).astype(BF16)

    grad_queries, grad_keys, grad_values = [], [], []
    for g in range(groups):
        grad_query, near, far = attention_backward(
            place, slopes, query, grad_mixed, doc_start, stats[g], keyvals[g],
            g * group_heads, group_heads,
        )
        grad_queries.append(grad_query)
        blocks = [near[:, k] for k in range(near.shape[1])]
        if n_ctx > 1:
            received = xperm(far, "ctx", 1)
            blocks = [
                (block.astype(F32) + received[:, k].astype(F32))
                for k, block in enumerate(blocks)
            ]
            bits = ctx_bits()[:-1]
            for bit in reversed(bits):
                half = len(blocks) // 2
                blocks = [
                    block
                    + xperm(sent.astype(BF16), "ctx", bit, lambda i, bit=bit: i > i ^ bit).astype(F32)
                    for block, sent in zip(blocks[:half], blocks[half:])
                ]
        final = blocks[0].astype(BF16)
        grad_keys.append(final[0])
        grad_values.append(final[1])
    grad_projected = [
        jnp.concatenate(parts, axis=1) if groups > 1 else parts[0]
        for parts in (grad_queries, grad_keys, grad_values)
    ]
    in_parts = [reduced(left_in, grad) for grad in grad_projected]
    grad_first = mm(
        grad_projected, [(weight_in, c) for c in range(3)], trans=True, start=0, size=width,
        tile=512, out_dtype=BF16,
    )
    grad_first_share = tensor_scatter(grad_first)
    unit_share, inverse_share = normalized(mine(residual).astype(F32))
    grad_from_first = norm_backward(grad_first_share, unit_share, inverse_share, gain_one)
    grad_middle_share = mine(grad_middle)
    input_grad = (grad_middle_share + grad_from_first).astype(BF16)

    def over_tokens(values):
        return jnp.sum(values, axis=0)

    grad_normed_share, unit_two_share = mine(grad_normed), mine(unit_two)
    early = jnp.stack(
        [
            over_tokens(grad_normed_share * unit_two_share),
            over_tokens(grad_normed_share),
            over_tokens(grad_middle_share),
            over_tokens(mine(cot)),
        ]
    )
    early = all_sum(early, ("tensor",))
    up_bias_row_sum = jnp.concatenate(up_bias_parts, axis=1).reshape(-1, local_width)
    early_rows = early.reshape(-1, local_width)
    early_all = all_sum(jnp.concatenate([early_rows, up_bias_row_sum]), ("ctx", "dp"))
    early = early_all[: early_rows.shape[0]].reshape(4, width)
    up_bias_grad = early_all[early_rows.shape[0] :].reshape(-1)
    late = jnp.stack(
        [over_tokens(grad_first_share * unit_share), over_tokens(grad_first_share)]
    )
    late = all_sum(late, ("tensor",)).reshape(-1, local_width)
    bias_terms = jnp.stack(
        [
            over_tokens(grad_projected[0].astype(F32)),
            over_tokens(grad_projected[2].astype(F32)),
        ]
    )
    late_all = all_sum(jnp.concatenate([late, bias_terms]), ("ctx", "dp"))
    late = late_all[: late.shape[0]].reshape(2, width)
    in_bias_grad = late_all[-2:]

    in_weight_grad = jnp.stack([part.astype(F32) for part in in_parts]).transpose(1, 0, 2)
    down_weight_grad = jnp.concatenate([part.astype(F32) for part in down_parts], axis=1)
    up_weight_grad = jnp.concatenate([part.astype(F32) for part in up_parts], axis=1)
    return (
        outputs[None],
        input_grad[None],
        late[0],
        late[1],
        in_weight_grad,
        in_bias_grad,
        out_part.astype(F32),
        early[2],
        early[0],
        early[1],
        up_weight_grad,
        up_bias_grad,
        down_weight_grad,
        early[3],
    )


def solution(mesh):
    return jax.shard_map(
        shards,
        mesh=mesh,
        in_specs=(
            P("dp", "ctx", None),
            P("dp", None),
            P(),
            P(),
            P(None, None, "tensor"),
            P(None, "tensor"),
            P(None, "tensor"),
            P(),
            P(),
            P(),
            P(None, "tensor"),
            P("tensor"),
            P(None, "tensor"),
            P(),
            P("dp", "ctx", None),
        ),
        out_specs=(
            P("dp", ("ctx", "tensor"), None),
            P("dp", ("ctx", "tensor"), None),
            P(),
            P(),
            P(("dp", "ctx"), None, "tensor"),
            P(None, "tensor"),
            P(("dp", "ctx"), "tensor"),
            P(),
            P(),
            P(),
            P(("dp", "ctx"), "tensor"),
            P("tensor"),
            P(("dp", "ctx"), "tensor"),
            P(),
        ),
        check_vma=False,
    )
```

time: 1130 us -> 604 us (0.53)
  waiting for transfers between devices: 825 us -> 252 us
  matrix products: 161 us -> 0 us
  Pallas kernels: 0 us -> 123 us
  starting transfers between devices: 2.02 us -> 57.2 us
  blocking collectives: 0 us -> 36.2 us
  local copies, waits for them, and re-layouts: 57.5 us -> 78.6 us
  other arithmetic: 56.4 us -> 38.7 us
    reduce_scatter x9 -> x8, waiting for transfers between devices: 445 us -> 0.01 us  [reduced(): return lax.psum_scatter(whole, 'dp', scatter_dimension=0, tiled=True)]
    ppermute x0 -> x52, waiting for transfers between devices: none -> 235 us  [xperm(): return lax.ppermute(values, axis, pairs)]
    unnamed x16 -> x8, waiting for transfers between devices: 181 us -> 0.13 us
    dot_general x30 -> x0, matrix products: 161 us -> none  [the longest x6 57.3 us: contract(): lax.dot_general(left, right, (((left_dim,), (right_dim,)), ((), ())), pre...]
    psum x1 -> x0, waiting for transfers between devices: 127 us -> none  [shards(): lax.psum((first_gain_term, first_shift_term, in_bias_whole, out_bias_term...]
    pallas_call x0 -> x24, Pallas kernels: none -> 123 us  [the longest x8 49 us: mm(): pl.pallas_call(functools.partial(mm_kernel, n_pairs=len(lefts), trans=tra...]
    all_gather x4 -> x0, waiting for transfers between devices: 71.4 us -> none  [the longest x1 21.4 us: shards(): lax.all_gather(normed_share.astype(jnp.bfloat16), 'tensor', axis=0, tiled...]
    ppermute x0 -> x52, starting transfers between devices: none -> 45.8 us  [xperm(): return lax.ppermute(values, axis, pairs)]
  transfers between devices with their start and end apart: 15 -> 62, of which waited for: 15 -> 28; matrix products, arithmetic and copies ran while one was open for 11% -> 11% of each run, Pallas kernels for 0% -> 16%
where the time goes in v1:
time: 604 us; the launch traced here: 601 us
  waiting for transfers between devices  252 us (42%)
  Pallas kernels  123 us (20%)
  local copies, waits for them, and re-layouts  78.6 us (13%)
  starting transfers between devices  57.2 us (9%)
  other arithmetic  38.7 us (6%)
  blocking collectives  36.2 us (6%)
  between operations  15.3 us (3%)
    ppermute x52, waiting for transfers between devices, xperm(): return lax.ppermute(values, axis, pairs)  235 us
    pallas_call x8, Pallas kernels, mm(): pl.pallas_call(functools.partial(mm_kernel, n_pairs=len(lefts), trans=tra...  49 us
    unnamed x146, local copies, waits for them, and re-layouts  47.7 us
    ppermute x52, starting transfers between devices, xperm(): return lax.ppermute(values, axis, pairs)  45.8 us
    all_to_all x2, blocking collectives, spread_left(): return lax.all_to_all(parts, 'ctx', 0, 0, tiled=True)  36.2 us
    pallas_call x8, Pallas kernels, weight_grad(): pl.pallas_call(functools.partial(weight_grad_kernel, offsets=ctx_offsets(...  28.7 us
    all_to_all x2, waiting for transfers between devices, spread_left(): return lax.all_to_all(parts, 'ctx', 0, 0, tiled=True)  17.3 us
    pallas_call x2, Pallas kernels, attention_backward(): pl.pallas_call(functools.partial(backward_kernel, offsets=ctx_offsets(),...  14.7 us
  transfers between devices with their start and end apart: 62, of which 28 were waited for; matrix products, arithmetic and copies ran while one was open for 11% of the time, Pallas kernels for 16%

profile of v1, /device:TPU:0, one launch (start us, length us, event | category | flops | bytes accessed | tf_op | source)
XLA Modules:
  0.0 601.4 jit_solution(16702021100148060574)
XLA Ops:
  13.2 44.5 %collective-permute-done.8.refs_4_ = bf16[2048,512]{1,0:T(8,128)(2,1)} collective-permute-done((bf16[2048,512]{1,0:T(8,128)(2,1)S(1)}, bf16[2048,512]{1,0:T(8,128)(2,1)}, u32[]{:S(2)}, u32[]{:S(2)}) %collective-permute-start.8) | collective-permute-done | bytes 2097184 | tf_op jit(solution)/shard_map/ppermute | solution.py:37
  64.9 4.6 collective-permute-start
  93.1 10.6 %shard_map.257.grad_active = f32[256,4096]{1,0:T(8,128)S(1)} custom-call(bf16[256,2048]{1,0:T(8,128)(2,1)S(1)} %bitcast.138, bf16[2048,4096]{1,0:T(8,128)(2,1)} %refs_1_.9), custom_call_target="tpu_custom_call" | custom-call | flops 4294967296 | bytes 22020096 | tf_op jit(solution)/shard_map/pallas_call | solution.py:123
  105.8 5.7 shard_map.258
  113.1 6.0 shard_map.259
  121.2 5.6 collective-permute-done.7
  126.9 5.1 shard_map.260
  135.9 6.6 %shard_map.261 = (bf16[256,2048]{1,0:T(8,128)(2,1)S(1)}, bf16[256,2048]{1,0:T(8,128)(2,1)S(1)}, f32[1,2048]{1,0:T(1,128)S(1)}) custom-call(bf16[256,2048]{1,0:T(8,128)(2,1)S(1)} %get-tuple-element.76.norm, bf16[2048,4096]{1,0:T(8,128)(2,1)} %refs_1_.7, f32[1,4096]{1,0:T(1,128)S(1)} %bitcast.139, f32[256,4096]{1,0:T(8,128)S(1)} %copy-done.4), custom_call_target="tpu_custom_call" | custom-call | flops 2147483648 | bytes 12582912 | tf_op jit(solution)/shard_map/pallas_call | solution.py:177
  143.5 7.8 %shard_map.262 = (bf16[256,2048]{1,0:T(8,128)(2,1)S(1)}, bf16[256,2048]{1,0:T(8,128)(2,1)}, f32[1,2048]{1,0:T(1,128)S(1)}) custom-call(bf16[256,2048]{1,0:T(8,128)(2,1)S(1)} %get-tuple-element.76.norm, bf16[2048,4096]{1,0:T(8,128)(2,1)} %refs_1_.7, f32[1,4096]{1,0:T(1,128)S(1)} %bitcast.140, f32[256,4096]{1,0:T(8,128)S(1)} %copy-done.4), custom_call_target="tpu_custom_call" | custom-call | flops 2147483648 | bytes 12582912 | tf_op jit(solution)/shard_map/pallas_call | solution.py:177
  153.1 5.6 shard_map.263
  159.3 5.6 shard_map.264
  173.8 8.5 %collective-permute-done.11 = bf16[256,1024]{1,0:T(8,128)(2,1)S(1)} collective-permute-done((bf16[256,1024]{1,0:T(8,128)(2,1)S(1)}, bf16[256,1024]{1,0:T(8,128)(2,1)S(1)}, u32[]{:S(2)}, u32[]{:S(2)}) %collective-permute-start.11) | collective-permute-done | bytes 524320 | tf_op jit(solution)/shard_map/ppermute | solution.py:37
  191.5 6.6 %all-to-all-start.1 = ((bf16[4,512,256]{2,1,0:T(8,128)(2,1)}), bf16[4,512,256]{2,1,0:T(8,128)(2,1)}, u32[]{:S(2)}, u32[]{:S(2)}) async-start(bf16[4,512,256]{2,1,0:T(8,128)(2,1)} %bitcast.146), calls=%async_computation.4 | async-start | bytes 2097152 | tf_op jit(solution)/shard_map/all_to_all | solution.py:423
  202.2 10.5 %all-to-all-done.1.left = bf16[4,512,256]{2,1,0:T(8,128)(2,1)} async-done(((bf16[4,512,256]{2,1,0:T(8,128)(2,1)}), bf16[4,512,256]{2,1,0:T(8,128)(2,1)}, u32[]{:S(2)}, u32[]{:S(2)}) %all-to-all-start.1) | async-done | bytes 1048608 | tf_op jit(solution)/shard_map/all_to_all | solution.py:423
  224.0 7.3 %shard_map.267 = (bf16[256,512]{1,0:T(8,128)(2,1)S(1)}, bf16[2,2,256,512]{3,2,1,0:T(8,128)(2,1)S(1)}, bf16[2,2,256,512]{3,2,1,0:T(8,128)(2,1)S(1)}) custom-call(s32[1]{0:T(128)} %bitcast.place, f32[8]{0:T(128)S(1)} %multiply_exponential_fusion.slopes, bf16[256,1024]{1,0:T(8,128)(2,1)S(1)} %copy-done.19, bf16[256,1024]{1,0:T(8,128)(2,1)S(1)} %shard_map.265.grad_mixed, ...), custom_call_target="tpu_custom_call" | custom-call | flops 1342177280 | bytes 4194304 | tf_op jit(solution)/shard_map/pallas_call | solution.py:377
  233.6 7.3 %shard_map.268 = (bf16[256,512]{1,0:T(8,128)(2,1)S(1)}, bf16[2,2,256,512]{3,2,1,0:T(8,128)(2,1)S(1)}, bf16[2,2,256,512]{3,2,1,0:T(8,128)(2,1)S(1)}) custom-call(s32[1]{0:T(128)} %bitcast.place, f32[8]{0:T(128)S(1)} %multiply_exponential_fusion.slopes, bf16[256,1024]{1,0:T(8,128)(2,1)S(1)} %copy-done.19, bf16[256,1024]{1,0:T(8,128)(2,1)S(1)} %shard_map.265.grad_mixed, ...), custom_call_target="tpu_custom_call" | custom-call | flops 1342177280 | bytes 4194304 | tf_op jit(solution)/shard_map/pallas_call | solution.py:377
  265.9 6.8 %all-to-all-done.left = bf16[4,512,256]{2,1,0:T(8,128)(2,1)} async-done(((bf16[4,512,256]{2,1,0:T(8,128)(2,1)}), bf16[4,512,256]{2,1,0:T(8,128)(2,1)}, u32[]{:S(2)}, u32[]{:S(2)}) %all-to-all-start) | async-done | bytes 1048608 | tf_op jit(solution)/shard_map/all_to_all | solution.py:423
  276.9 7.0 %collective-permute-done.14 = bf16[2,256,512]{2,1,0:T(8,128)(2,1)} collective-permute-done((bf16[2,256,512]{2,1,0:T(8,128)(2,1)}, bf16[2,256,512]{2,1,0:T(8,128)(2,1)}, u32[]{:S(2)}, u32[]{:S(2)}) %collective-permute-start.14) | collective-permute-done | bytes 524320 | tf_op jit(solution)/shard_map/ppermute | solution.py:37
  285.5 9.2 %collective-permute-done.16 = bf16[2,256,512]{2,1,0:T(8,128)(2,1)} collective-permute-done((bf16[2,256,512]{2,1,0:T(8,128)(2,1)}, bf16[2,256,512]{2,1,0:T(8,128)(2,1)}, u32[]{:S(2)}, u32[]{:S(2)}) %collective-permute-start.16) | collective-permute-done | bytes 524320 | tf_op jit(solution)/shard_map/ppermute | solution.py:37
  297.1 13.4 %collective-permute-done.26.refs_1_ = bf16[256,1024]{1,0:T(8,128)(2,1)S(1)} collective-permute-done((bf16[256,1024]{1,0:T(8,128)(2,1)S(1)}, bf16[256,1024]{1,0:T(8,128)(2,1)S(1)}, u32[]{:S(2)}, u32[]{:S(2)}) %collective-permute-start.26) | collective-permute-done | bytes 524320 | tf_op jit(solution)/shard_map/ppermute | solution.py:37
  318.4 13.7 %collective-permute-done.29.refs_1_ = bf16[256,1024]{1,0:T(8,128)(2,1)S(1)} collective-permute-done((bf16[256,1024]{1,0:T(8,128)(2,1)S(1)}, bf16[256,1024]{1,0:T(8,128)(2,1)S(1)}, u32[]{:S(2)}, u32[]{:S(2)}) %collective-permute-start.29) | collective-permute-done | bytes 524320 | tf_op jit(solution)/shard_map/ppermute | solution.py:37
  338.9 19.1 %collective-permute-done.46.refs_1_ = bf16[256,2048]{1,0:T(8,128)(2,1)} collective-permute-done((bf16[256,2048]{1,0:T(8,128)(2,1)}, bf16[256,2048]{1,0:T(8,128)(2,1)}, u32[]{:S(2)}, u32[]{:S(2)}) %collective-permute-start.46) | collective-permute-done | bytes 1048608 | tf_op jit(solution)/shard_map/ppermute | solution.py:37
  362.9 18.1 %all_to_all.20.left = bf16[4,512,256]{2,1,0:T(8,128)(2,1)S(1)} all-to-all(bf16[4,512,256]{2,1,0:T(8,128)(2,1)} %bitcast.147), channel_id=1, replica_groups=mesh['dp'=4,'ctx'=4,'tensor'=2] {'ctx'}, dimensions={0} | all-to-all | bytes 2097152 | tf_op jit(solution)/shard_map/all_to_all | solution.py:423
  381.0 4.6 shard_map.276
  388.4 24.4 %collective-permute-done.49.refs_1_ = bf16[256,2048]{1,0:T(8,128)(2,1)S(1)} collective-permute-done((bf16[256,2048]{1,0:T(8,128)(2,1)}, bf16[256,2048]{1,0:T(8,128)(2,1)S(1)}, u32[]{:S(2)}, u32[]{:S(2)}) %collective-permute-start.49) | collective-permute-done | bytes 1048608 | tf_op jit(solution)/shard_map/ppermute | solution.py:37
  423.8 24.7 %collective-permute-done.40.refs_1_ = bf16[256,2048]{1,0:T(8,128)(2,1)} collective-permute-done((bf16[256,2048]{1,0:T(8,128)(2,1)}, bf16[256,2048]{1,0:T(8,128)(2,1)}, u32[]{:S(2)}, u32[]{:S(2)}) %collective-permute-start.40) | collective-permute-done | bytes 1048608 | tf_op jit(solution)/shard_map/ppermute | solution.py:37
  453.6 18.1 %all_to_all.21.left = bf16[4,512,256]{2,1,0:T(8,128)(2,1)S(1)} all-to-all(bf16[4,512,256]{2,1,0:T(8,128)(2,1)} %bitcast.148), channel_id=1, replica_groups=mesh['dp'=4,'ctx'=4,'tensor'=2] {'ctx'}, dimensions={0} | all-to-all | bytes 2097152 | tf_op jit(solution)/shard_map/all_to_all | solution.py:423
  483.1 22.6 %collective-permute-done.43.refs_1_ = bf16[256,2048]{1,0:T(8,128)(2,1)} collective-permute-done((bf16[256,2048]{1,0:T(8,128)(2,1)}, bf16[256,2048]{1,0:T(8,128)(2,1)}, u32[]{:S(2)}, u32[]{:S(2)}) %collective-permute-start.43) | collective-permute-done | bytes 1048608 | tf_op jit(solution)/shard_map/ppermute | solution.py:37
  505.7 10.6 %shard_map.266 = bf16[256,2048]{1,0:T(8,128)(2,1)S(1)} custom-call(bf16[256,4096]{1,0:T(8,128)(2,1)S(1)} %pad_maximum_fusion.1.refs_0_, bf16[2048,4096]{1,0:T(8,128)(2,1)} %refs_1_.9), custom_call_target="tpu_custom_call" | custom-call | flops 4294967296 | bytes 19922944 | tf_op jit(solution)/shard_map/pallas_call | solution.py:123
  516.4 7.9 %shard_map.269 = bf16[256,2048]{1,0:T(8,128)(2,1)S(1)} custom-call(bf16[256,1024]{1,0:T(8,128)(2,1)} %constant_dynamic-update-slice_fusion.6.refs_0_, bf16[256,1024]{1,0:T(8,128)(2,1)S(1)} %copy-done.15, bf16[256,1024]{1,0:T(8,128)(2,1)S(1)} %copy-done.17, bf16[3,2048,1024]{2,1,0:T(8,128)(2,1)} %bitcast.131, bf16[3,2048,1024]{2,1,0:T(8,128)(2,1)} %bitcast.132, ...), custom_call_target="tpu_custom_call" | custom-call | flops 3221225472 | bytes 15204352 | tf_op jit(solution)/shard_map/pallas_call | solution.py:123
  535.5 4.8 collective-permute-done.17
  574.8 7.0 %collective-permute-done.39 = f32[12,1024]{1,0:T(8,128)S(1)} collective-permute-done((f32[12,1024]{1,0:T(8,128)S(1)}, f32[12,1024]{1,0:T(8,128)S(1)}, u32[]{:S(2)}, u32[]{:S(2)}) %collective-permute-start.39) | collective-permute-done | bytes 49184 | tf_op jit(solution)/shard_map/ppermute | solution.py:37
  (367 shorter events, 226.0 us)
Async XLA Ops:
  9.0 48.7 %collective-permute-start.8 = (bf16[2048,512]{1,0:T(8,128)(2,1)S(1)}, bf16[2048,512]{1,0:T(8,128)(2,1)}, u32[]{:S(2)}, u32[]{:S(2)}) collective-permute-start(bf16[2048,512]{1,0:T(8,128)(2,1)S(1)} %constant_dynamic-slice_fusion.2), channel_id=1, source_target_pairs={{0,1},{1,0},{2,3},{3,2},{4,5},{5,4},{6,7},{7,6},{8,9},{9,8},{10,11... | collective-permute-start | bytes 6291464 | tf_op jit(solution)/shard_map/ppermute | solution.py:37
  57.8 69.1 %collective-permute-start.9 = (bf16[2048,512]{1,0:T(8,128)(2,1)}, bf16[2048,512]{1,0:T(8,128)(2,1)}, u32[]{:S(2)}, u32[]{:S(2)}) collective-permute-start(bf16[2048,512]{1,0:T(8,128)(2,1)} %collective-permute-done.8.refs_4_), channel_id=1, source_target_pairs={{0,2},{2,0},{4,6},{6,4},{1,3},{3,1},{5,7},{7,5},{8,10},{10,8},{12,... | collective-permute-start | bytes 6291464 | tf_op jit(solution)/shard_map/ppermute | solution.py:37
  64.9 21.9 %collective-permute-start = (bf16[2,256,512]{2,1,0:T(8,128)(2,1)}, bf16[2,256,512]{2,1,0:T(8,128)(2,1)}, u32[]{:S(2)}, u32[]{:S(2)}) collective-permute-start(bf16[2,256,512]{2,1,0:T(8,128)(2,1)} %shard_map.255.refs_0_), channel_id=1, source_target_pairs={{0,4},{2,6},{1,5},{3,7},{8,12},{10,14},{9,13},{11,15},{16,20},{18,... | collective-permute-start | bytes 1572872 | tf_op jit(solution)/shard_map/ppermute | solution.py:37
  71.9 20.2 %collective-permute-start.3 = (bf16[2,256,512]{2,1,0:T(8,128)(2,1)}, bf16[2,256,512]{2,1,0:T(8,128)(2,1)}, u32[]{:S(2)}, u32[]{:S(2)}) collective-permute-start(bf16[2,256,512]{2,1,0:T(8,128)(2,1)} %shard_map.256.refs_0_), channel_id=1, source_target_pairs={{0,4},{2,6},{1,5},{3,7},{8,12},{10,14},{9,13},{11,15},{16,20},{18,... | collective-permute-start | bytes 1572872 | tf_op jit(solution)/shard_map/ppermute | solution.py:37
  74.0 31.7 %collective-permute-start.1 = (bf16[2,256,512]{2,1,0:T(8,128)(2,1)}, bf16[2,256,512]{2,1,0:T(8,128)(2,1)}, u32[]{:S(2)}, u32[]{:S(2)}) collective-permute-start(bf16[2,256,512]{2,1,0:T(8,128)(2,1)} %shard_map.255.refs_0_), channel_id=1, source_target_pairs={{0,2},{4,6},{1,3},{5,7},{8,10},{12,14},{9,11},{13,15},{16,18},{20,... | collective-permute-start | bytes 1572872 | tf_op jit(solution)/shard_map/ppermute | solution.py:37
  77.0 28.8 %collective-permute-start.4 = (bf16[2,256,512]{2,1,0:T(8,128)(2,1)}, bf16[2,256,512]{2,1,0:T(8,128)(2,1)}, u32[]{:S(2)}, u32[]{:S(2)}) collective-permute-start(bf16[2,256,512]{2,1,0:T(8,128)(2,1)} %shard_map.256.refs_0_), channel_id=1, source_target_pairs={{0,2},{4,6},{1,3},{5,7},{8,10},{12,14},{9,11},{13,15},{16,18},{20,... | collective-permute-start | bytes 1572872 | tf_op jit(solution)/shard_map/ppermute | solution.py:37
  166.5 32.1 %collective-permute-start.32 = (bf16[256,1024]{1,0:T(8,128)(2,1)}, bf16[256,1024]{1,0:T(8,128)(2,1)}, u32[]{:S(2)}, u32[]{:S(2)}) collective-permute-start(bf16[256,1024]{1,0:T(8,128)(2,1)} %constant_dynamic-update-slice_fusion.refs_0_), channel_id=1, source_target_pairs={{0,4},{2,6},{4,0},{6,2},{1,5},{3,7},{5,1},{7,3},{8,12},{10,14},{12... | collective-permute-start | bytes 1572872 | tf_op jit(solution)/shard_map/ppermute | solution.py:37
  191.5 21.2 %all-to-all-start.1 = ((bf16[4,512,256]{2,1,0:T(8,128)(2,1)}), bf16[4,512,256]{2,1,0:T(8,128)(2,1)}, u32[]{:S(2)}, u32[]{:S(2)}) async-start(bf16[4,512,256]{2,1,0:T(8,128)(2,1)} %bitcast.146), calls=%async_computation.4 | async-start | bytes 2097152 | tf_op jit(solution)/shard_map/all_to_all | solution.py:423
  198.1 386.8 %reduce-scatter.15.cloned.1.call-start = ((), (), s32[]{:S(2)}) async-start(), calls=%async_computation.15 | async-start | bytes 1310720 | tf_op jit(solution)/shard_map/reduce_scatter | solution.py:545
  233.4 25.7 %collective-permute-start.13 = (bf16[2,2,256,512]{3,2,0,1:T(8,128)(2,1)}, bf16[2,2,256,512]{3,2,0,1:T(8,128)(2,1)}, u32[]{:S(2)}, u32[]{:S(2)}) collective-permute-start(bf16[2,2,256,512]{3,2,0,1:T(8,128)(2,1)} %copy.52), channel_id=1, source_target_pairs={{0,2},{2,0},{4,6},{6,4},{1,3},{3,1},{5,7},{7,5},{8,10},{10,8},{12,... | collective-permute-start | bytes 3145736 | tf_op jit(solution)/shard_map/ppermute | solution.py:37
  243.0 19.5 %collective-permute-start.15 = (bf16[2,2,256,512]{3,2,0,1:T(8,128)(2,1)}, bf16[2,2,256,512]{3,2,0,1:T(8,128)(2,1)}, u32[]{:S(2)}, u32[]{:S(2)}) collective-permute-start(bf16[2,2,256,512]{3,2,0,1:T(8,128)(2,1)} %copy.55), channel_id=1, source_target_pairs={{0,2},{2,0},{4,6},{6,4},{1,3},{3,1},{5,7},{7,5},{8,10},{10,8},{12,... | collective-permute-start | bytes 3145736 | tf_op jit(solution)/shard_map/ppermute | solution.py:37
  257.7 329.0 %reduce-scatter.9.cloned.1.call-start = ((), (), s32[]{:S(2)}) async-start(), calls=%async_computation.12 | async-start | bytes 1310720 | tf_op jit(solution)/shard_map/reduce_scatter | solution.py:545
  261.2 22.7 %collective-permute-start.14 = (bf16[2,256,512]{2,1,0:T(8,128)(2,1)}, bf16[2,256,512]{2,1,0:T(8,128)(2,1)}, u32[]{:S(2)}, u32[]{:S(2)}) collective-permute-start(bf16[2,256,512]{2,1,0:T(8,128)(2,1)} %fusion.28), channel_id=1, source_target_pairs={{4,0},{6,2},{5,1},{7,3},{12,8},{14,10},{13,9},{15,11},{20,16},{22,... | collective-permute-start | bytes 1572872 | tf_op jit(solution)/shard_map/ppermute | solution.py:37
  264.6 30.1 %collective-permute-start.16 = (bf16[2,256,512]{2,1,0:T(8,128)(2,1)}, bf16[2,256,512]{2,1,0:T(8,128)(2,1)}, u32[]{:S(2)}, u32[]{:S(2)}) collective-permute-start(bf16[2,256,512]{2,1,0:T(8,128)(2,1)} %fusion.29), channel_id=1, source_target_pairs={{4,0},{6,2},{5,1},{7,3},{12,8},{14,10},{13,9},{15,11},{20,16},{22,... | collective-permute-start | bytes 1572872 | tf_op jit(solution)/shard_map/ppermute | solution.py:37
  276.9 309.8 %reduce-scatter.11.cloned.1.call-start = ((), (), s32[]{:S(2)}) async-start(), calls=%async_computation.13 | async-start | bytes 1310720 | tf_op jit(solution)/shard_map/reduce_scatter | solution.py:545
  317.0 269.7 %reduce-scatter.13.cloned.1.call-start = ((), (), s32[]{:S(2)}) async-start(), calls=%async_computation.14 | async-start | bytes 1310720 | tf_op jit(solution)/shard_map/reduce_scatter | solution.py:545
  332.1 25.9 %collective-permute-start.46 = (bf16[256,2048]{1,0:T(8,128)(2,1)}, bf16[256,2048]{1,0:T(8,128)(2,1)}, u32[]{:S(2)}, u32[]{:S(2)}) collective-permute-start(bf16[256,2048]{1,0:T(8,128)(2,1)} %copy-done.38), channel_id=1, source_target_pairs={{0,4},{2,6},{4,0},{6,2},{1,5},{3,7},{5,1},{7,3},{8,12},{10,14},{12... | collective-permute-start | bytes 3145736 | tf_op jit(solution)/shard_map/ppermute | solution.py:37
  338.6 250.5 %reduce-scatter.21.cloned.1.call-start = ((), (), s32[]{:S(2)}) async-start(), calls=%async_computation.18 | async-start | bytes 2621440 | tf_op jit(solution)/shard_map/reduce_scatter | solution.py:545
  338.6 42.4 %collective-permute-start.47 = (bf16[256,2048]{1,0:T(8,128)(2,1)}, bf16[256,2048]{1,0:T(8,128)(2,1)}, u32[]{:S(2)}, u32[]{:S(2)}) collective-permute-start(bf16[256,2048]{1,0:T(8,128)(2,1)} %copy-done.38), channel_id=1, source_target_pairs={{0,2},{2,0},{4,6},{6,4},{1,3},{3,1},{5,7},{7,5},{8,10},{10,8},{12,... | collective-permute-start | bytes 3145736 | tf_op jit(solution)/shard_map/ppermute | solution.py:37
  358.0 23.1 %collective-permute-start.48 = (bf16[256,2048]{1,0:T(8,128)(2,1)}, bf16[256,2048]{1,0:T(8,128)(2,1)}, u32[]{:S(2)}, u32[]{:S(2)}) collective-permute-start(bf16[256,2048]{1,0:T(8,128)(2,1)} %collective-permute-done.46.refs_1_), channel_id=1, source_target_pairs={{0,2},{2,0},{4,6},{6,4},{1,3},{3,1},{5,7},{7,5},{8,10},{10,8},{12,... | collective-permute-start | bytes 3145736 | tf_op jit(solution)/shard_map/ppermute | solution.py:37
  387.9 201.2 %reduce-scatter.23.cloned.1.call-start = ((), (), s32[]{:S(2)}) async-start(), calls=%async_computation.19 | async-start | bytes 2621440 | tf_op jit(solution)/shard_map/reduce_scatter | solution.py:545
  388.0 24.8 %collective-permute-start.49 = (bf16[256,2048]{1,0:T(8,128)(2,1)}, bf16[256,2048]{1,0:T(8,128)(2,1)S(1)}, u32[]{:S(2)}, u32[]{:S(2)}) collective-permute-start(bf16[256,2048]{1,0:T(8,128)(2,1)} %copy-done.40), channel_id=1, source_target_pairs={{0,4},{2,6},{4,0},{6,2},{1,5},{3,7},{5,1},{7,3},{8,12},{10,14},{12... | collective-permute-start | bytes 3145736 | tf_op jit(solution)/shard_map/ppermute | solution.py:37
  388.4 24.4 %collective-permute-start.50 = (bf16[256,2048]{1,0:T(8,128)(2,1)}, bf16[256,2048]{1,0:T(8,128)(2,1)S(1)}, u32[]{:S(2)}, u32[]{:S(2)}) collective-permute-start(bf16[256,2048]{1,0:T(8,128)(2,1)} %copy-done.40), channel_id=1, source_target_pairs={{0,2},{2,0},{4,6},{6,4},{1,3},{3,1},{5,7},{7,5},{8,10},{10,8},{12,... | collective-permute-start | bytes 3145736 | tf_op jit(solution)/shard_map/ppermute | solution.py:37
  422.6 169.2 %reduce-scatter.17.cloned.1.call-start = ((), (), s32[]{:S(2)}) async-start(), calls=%async_computation.16 | async-start | bytes 2621440 | tf_op jit(solution)/shard_map/reduce_scatter | solution.py:545
  422.9 25.6 %collective-permute-start.40 = (bf16[256,2048]{1,0:T(8,128)(2,1)}, bf16[256,2048]{1,0:T(8,128)(2,1)}, u32[]{:S(2)}, u32[]{:S(2)}) collective-permute-start(bf16[256,2048]{1,0:T(8,128)(2,1)} %copy-done.29), channel_id=1, source_target_pairs={{0,4},{2,6},{4,0},{6,2},{1,5},{3,7},{5,1},{7,3},{8,12},{10,14},{12... | collective-permute-start | bytes 3145736 | tf_op jit(solution)/shard_map/ppermute | solution.py:37
  423.8 47.8 %collective-permute-start.41 = (bf16[256,2048]{1,0:T(8,128)(2,1)}, bf16[256,2048]{1,0:T(8,128)(2,1)}, u32[]{:S(2)}, u32[]{:S(2)}) collective-permute-start(bf16[256,2048]{1,0:T(8,128)(2,1)} %copy-done.29), channel_id=1, source_target_pairs={{0,2},{2,0},{4,6},{6,4},{1,3},{3,1},{5,7},{7,5},{8,10},{10,8},{12,... | collective-permute-start | bytes 3145736 | tf_op jit(solution)/shard_map/ppermute | solution.py:37
  448.5 23.1 %collective-permute-start.42 = (bf16[256,2048]{1,0:T(8,128)(2,1)}, bf16[256,2048]{1,0:T(8,128)(2,1)}, u32[]{:S(2)}, u32[]{:S(2)}) collective-permute-start(bf16[256,2048]{1,0:T(8,128)(2,1)} %collective-permute-done.40.refs_1_), channel_id=1, source_target_pairs={{0,2},{2,0},{4,6},{6,4},{1,3},{3,1},{5,7},{7,5},{8,10},{10,8},{12,... | collective-permute-start | bytes 3145736 | tf_op jit(solution)/shard_map/ppermute | solution.py:37
  478.6 113.2 %reduce-scatter.19.cloned.1.call-start = ((), (), s32[]{:S(2)}) async-start(), calls=%async_computation.17 | async-start | bytes 2621440 | tf_op jit(solution)/shard_map/reduce_scatter | solution.py:545
  480.4 25.3 %collective-permute-start.43 = (bf16[256,2048]{1,0:T(8,128)(2,1)}, bf16[256,2048]{1,0:T(8,128)(2,1)}, u32[]{:S(2)}, u32[]{:S(2)}) collective-permute-start(bf16[256,2048]{1,0:T(8,128)(2,1)} %get-tuple-element.54.refs_0_), channel_id=1, source_target_pairs={{0,4},{2,6},{4,0},{6,2},{1,5},{3,7},{5,1},{7,3},{8,12},{10,14},{12... | collective-permute-start | bytes 3145736 | tf_op jit(solution)/shard_map/ppermute | solution.py:37
  481.2 48.4 %collective-permute-start.44 = (bf16[256,2048]{1,0:T(8,128)(2,1)}, bf16[256,2048]{1,0:T(8,128)(2,1)}, u32[]{:S(2)}, u32[]{:S(2)}) collective-permute-start(bf16[256,2048]{1,0:T(8,128)(2,1)} %get-tuple-element.54.refs_0_), channel_id=1, source_target_pairs={{0,2},{2,0},{4,6},{6,4},{1,3},{3,1},{5,7},{7,5},{8,10},{10,8},{12,... | collective-permute-start | bytes 3145736 | tf_op jit(solution)/shard_map/ppermute | solution.py:37
  505.7 23.8 %collective-permute-start.45 = (bf16[256,2048]{1,0:T(8,128)(2,1)}, bf16[256,2048]{1,0:T(8,128)(2,1)S(1)}, u32[]{:S(2)}, u32[]{:S(2)}) collective-permute-start(bf16[256,2048]{1,0:T(8,128)(2,1)} %collective-permute-done.43.refs_1_), channel_id=1, source_target_pairs={{0,2},{2,0},{4,6},{6,4},{1,3},{3,1},{5,7},{7,5},{8,10},{10,8},{12,... | collective-permute-start | bytes 3145736 | tf_op jit(solution)/shard_map/ppermute | solution.py:37
  526.7 40.8 %collective-permute-start.12 = (bf16[128,2048]{1,0:T(8,128)(2,1)}, bf16[128,2048]{1,0:T(8,128)(2,1)}, u32[]{:S(2)}, u32[]{:S(2)}) collective-permute-start(bf16[128,2048]{1,0:T(8,128)(2,1)} %constant_dynamic-slice_fusion.1), channel_id=1, source_target_pairs={{0,1},{1,0},{2,3},{3,2},{4,5},{5,4},{6,7},{7,6},{8,9},{9,8},{10,11... | collective-permute-start | bytes 1572872 | tf_op jit(solution)/shard_map/ppermute | solution.py:37
  (96 other events, 850.3 us)
Sparse Core Ops, SparseCore 0:
  218.9 26.4 reduce-scatter.14
  277.0 26.5 reduce-scatter.8
  317.1 26.5 reduce-scatter.10
  345.9 25.7 reduce-scatter.12
  388.1 43.2 reduce-scatter.20
  433.6 43.1 reduce-scatter.22
  479.1 43.1 reduce-scatter.16
  535.6 47.4 reduce-scatter.18

commit v2 on v1

v2 whole, which is shorter than its diff:
```python
import functools
import math

import jax
import jax.numpy as jnp
from jax import lax
from jax.experimental import pallas as pl
from jax.experimental.pallas import tpu as pltpu
from jax.sharding import PartitionSpec as P

H = 16
HD = 128
EPSILON = 1e-05
MASKED = -1e30
MIB = 1 << 20
GELU_C = math.sqrt(2.0 / math.pi)
GELU_A = 0.044715

BF16 = jnp.bfloat16
F32 = jnp.float32


VMEM = 56


def params(limit):
    return pltpu.CompilerParams(vmem_limit_bytes=limit * MIB)


def load(level=0):
    if not level:
        return None
    return pl.CostEstimate(flops=10 ** (8 + 2 * level), bytes_accessed=10**7, transcendentals=0)


def xperm(values, axis, bit, wanted=None):
    pairs = [
        (i, i ^ bit) for i in range(lax.axis_size(axis)) if wanted is None or wanted(i)
    ]
    return lax.ppermute(values, axis, pairs)


def after(values, *deps):
    return lax.optimization_barrier((values,) + deps)[0]


def ctx_bits():
    n = lax.axis_size("ctx")
    return [1 << b for b in reversed(range(n.bit_length() - 1))]


def ctx_offsets():
    offsets = [0]
    for bit in ctx_bits():
        offsets = offsets + [o ^ bit for o in offsets]
    return offsets


def gather_ctx(block, gates=()):
    blocks = [block]
    for hop, bit in enumerate(ctx_bits()):
        held_back = 0 < hop <= len(gates)
        sent = lax.optimization_barrier((blocks, gates[hop - 1]))[0] if held_back else blocks
        blocks = blocks + [xperm(b, "ctx", bit) for b in sent]
    return blocks


def gather_ctx_causal(block, gate):
    blocks, offsets = [block], [0]
    for bit in ctx_bits():
        fresh = []
        for b, o in zip(blocks, offsets):
            b = after(b, gate) if o else b
            fresh.append(
                xperm(b, "ctx", bit, lambda i, o=o, bit=bit: (i ^ o) < (i ^ bit))
            )
        blocks = blocks + fresh
        offsets = offsets + [o ^ bit for o in offsets]
    return blocks


def mm_kernel(*refs, n_pairs, trans):
    lefts, rights = refs[:n_pairs], refs[n_pairs : 2 * n_pairs]
    extras, out = refs[2 * n_pairs : -1], refs[-1]
    total = None
    for left, right in zip(lefts, rights):
        term = lax.dot_general(
            left[...],
            right[...],
            (((1,), (1 if trans else 0,)), ((), ())),
            preferred_element_type=F32,
        )
        total = term if total is None else total + term
    for extra in extras:
        row = extra[0:1, :] if extra.shape[0] == 2 else extra[...]
        total = total + row.astype(F32)
    out[...] = total.astype(out.dtype)


def mm(lefts, rights, *, trans, start, size, tile, out_dtype, extras=(), heavy=0):
    lefts = [left if isinstance(left, tuple) else (left, 0, left.shape[1]) for left in lefts]
    rows = lefts[0][0].shape[0]
    tile = math.gcd(tile, size)
    first = start // tile
    specs, operands = [], []
    for left, column, depth in lefts:
        specs.append(pl.BlockSpec((rows, depth), lambda i, column=column: (0, column)))
        operands.append(left)
    for (left, column, depth), right in zip(lefts, rights):
        lead, part = None, 0
        if isinstance(right, tuple):
            right, lead, part = right
        shape = (tile, depth) if trans else (depth, tile)

        def place(i, lead=lead, part=part):
            where = (first + i, part) if trans else (part, first + i)
            return where if lead is None else (lead,) + where

        specs.append(pl.BlockSpec(((None,) if lead is not None else ()) + shape, place))
        operands.append(right)
    for extra in extras:
        specs.append(pl.BlockSpec((extra.shape[0], tile), lambda i: (0, first + i)))
        operands.append(extra)
    return pl.pallas_call(
        functools.partial(mm_kernel, n_pairs=len(lefts), trans=trans),
        grid=(size // tile,),
        in_specs=specs,
        out_specs=pl.BlockSpec((rows, tile), lambda i: (0, i)),
        out_shape=jax.ShapeDtypeStruct((rows, size), out_dtype),
        compiler_params=params(VMEM),
        cost_estimate=load(heavy),
    )(*operands)


def kv_kernel(values, pair, weight, bias, norm, *outs):
    @pl.when(pl.program_id(0) == 0)
    def _():
        unit, _ = normalized(values[...].astype(F32))
        norm[...] = (unit * pair[0:1, :] + pair[1:2, :]).astype(BF16)

    shifted = bias[1:2, :].astype(F32) * pl.program_id(0).astype(F32)
    total = jnp.dot(norm[...], weight[...], preferred_element_type=F32) + shifted
    size = outs[0].shape[1]
    for k, out in enumerate(outs):
        out[...] = total[:, k * size : (k + 1) * size].astype(out.dtype)


def project_kv(values, pair, weight, bias, groups):
    rows, width = values.shape
    columns = weight.shape[2]
    size = columns // groups
    whole = pl.BlockSpec((rows, width), lambda c: (0, 0))
    return pl.pallas_call(
        kv_kernel,
        grid=(2,),
        in_specs=[
            whole,
            pl.BlockSpec((2, width), lambda c: (0, 0)),
            pl.BlockSpec((None, width, columns), lambda c: (c + 1, 0, 0)),
            pl.BlockSpec((2, columns), lambda c: (0, 0)),
        ],
        out_specs=[whole]
        + [pl.BlockSpec((None, rows, size), lambda c: (c, 0, 0))] * groups,
        out_shape=[jax.ShapeDtypeStruct((rows, width), BF16)]
        + [jax.ShapeDtypeStruct((2, rows, size), BF16)] * groups,
        compiler_params=params(VMEM),
        cost_estimate=load(),
    )(values, pair, weight, bias)


def normalized(values):
    average = jnp.mean(values, axis=-1, keepdims=True)
    centered = values - average
    spread = jnp.mean(centered * centered, axis=-1, keepdims=True)
    inverse = lax.rsqrt(spread + EPSILON)
    return centered * inverse, inverse


def up_block(norm, weight, bias, grad_active, active, grad_upper, bias_sum):
    upper = jnp.dot(norm[...], weight[...], preferred_element_type=F32) + bias[...]
    square = upper * upper
    wave = jnp.tanh(GELU_C * (upper + GELU_A * square * upper))
    half = 0.5 * (1.0 + wave)
    active[...] = (upper * half).astype(BF16)
    slope = half + 0.5 * upper * (1.0 - wave * wave) * (
        GELU_C * (1.0 + 3.0 * GELU_A * square)
    )
    grad = (grad_active[...] * slope).astype(BF16)
    grad_upper[...] = grad
    bias_sum[...] = jnp.sum(grad.astype(F32), axis=0, keepdims=True)


def up_kernel(norm, weight, bias, grad_active, *refs):
    up_block(norm, weight, bias, grad_active, *refs[-3:])


def first_up_kernel(*refs, n_terms):
    values, vectors = refs[:2]
    terms, (weight, bias, grad_active) = refs[2 : 2 + n_terms], refs[2 + n_terms : 5 + n_terms]
    middle, norm, active, grad_upper, bias_sum = refs[5 + n_terms :]

    @pl.when(pl.program_id(0) == 0)
    def _():
        total = terms[0][...].astype(F32)
        for term in terms[1:]:
            total = total + term[...].astype(F32)
        middle[...] = values[...].astype(F32) + total + vectors[0:1, :]
        unit, _ = normalized(middle[...])
        norm[...] = (unit * vectors[1:2, :] + vectors[2:3, :]).astype(BF16)

    up_block(norm, weight, bias, grad_active, active, grad_upper, bias_sum)


def up_specs(width, rows, tile, first, out_first=0):
    ins = [
        pl.BlockSpec((width, tile), lambda i: (0, first + i)),
        pl.BlockSpec((1, tile), lambda i: (0, first + i)),
        pl.BlockSpec((rows, tile), lambda i: (0, first + i)),
    ]
    outs = [
        pl.BlockSpec((rows, tile), lambda i: (0, i)),
        pl.BlockSpec((rows, tile), lambda i: (0, out_first + i)),
        pl.BlockSpec((1, tile), lambda i: (0, i)),
    ]
    return ins, outs


def up_shapes(rows, size, local):
    return [
        jax.ShapeDtypeStruct((rows, size), BF16),
        jax.ShapeDtypeStruct((rows, local), BF16),
        jax.ShapeDtypeStruct((1, size), F32),
    ]


def first_up(values, vectors, terms, weight, bias, grad_active, size, local, tile):
    rows, width = values.shape
    whole = pl.BlockSpec((rows, width), lambda i: (0, 0))
    ins, outs = up_specs(width, rows, tile, 0)
    return pl.pallas_call(
        functools.partial(first_up_kernel, n_terms=len(terms)),
        grid=(size // tile,),
        in_specs=[whole, pl.BlockSpec((3, width), lambda i: (0, 0))] + [whole] * len(terms) + ins,
        out_specs=[whole, whole] + outs,
        out_shape=[
            jax.ShapeDtypeStruct((rows, width), F32),
            jax.ShapeDtypeStruct((rows, width), BF16),
        ]
        + up_shapes(rows, size, local),
        compiler_params=params(VMEM),
        cost_estimate=load(),
    )(values, vectors, *terms, weight, bias, grad_active)


def more_up(norm, weight, bias, grad_active, start, size, tile, held=None):
    rows, width = norm.shape
    ins, outs = up_specs(width, rows, tile, start // tile, 0 if held is None else start // tile)
    in_specs = [pl.BlockSpec((rows, width), lambda i: (0, 0))] + ins
    operands = [norm, weight, bias, grad_active]
    if held is not None:
        in_specs.append(pl.BlockSpec(memory_space=pl.ANY))
        operands.append(held)
    return pl.pallas_call(
        up_kernel,
        grid=(size // tile,),
        in_specs=in_specs,
        out_specs=outs,
        out_shape=up_shapes(rows, size, size if held is None else held.shape[1]),
        input_output_aliases={} if held is None else {4: 1},
        compiler_params=params(VMEM),
        cost_estimate=load(),
    )(*operands)


def weight_grad_kernel(*refs, blocks, n):
    out, step, first = refs[-1], pl.program_id(0), 0

    def summed(lefts, rights):
        total = None
        for left, right in zip(lefts, rights):
            term = jnp.dot(left[...], right[...], preferred_element_type=F32)
            total = term if total is None else total + term
        out[...] = total.astype(out.dtype)

    for part, count in enumerate(blocks):
        lefts = refs[2 * n * part : 2 * n * part + n]
        rights = refs[2 * n * part + n : 2 * n * (part + 1)]
        if len(blocks) == 1:
            summed(lefts, rights)
        else:
            pl.when((step >= first) & (step < first + count))(
                functools.partial(summed, lefts, rights)
            )
        first += count


def weight_grad(parts, rows, tile):
    n = len(parts[0][0])
    tokens = parts[0][0][0].shape[1]
    for _, _, rights in parts:
        tile = math.gcd(tile, rights[0].shape[1])
    blocks = [rights[0].shape[1] // tile for _, _, rights in parts]
    specs, operands, first = [], [], 0
    for (lefts, row, rights), count in zip(parts, blocks):

        def place(i, first=first, count=count):
            return (0, jnp.clip(i - first, 0, count - 1))

        specs += [pl.BlockSpec((rows, tokens), lambda i, row=row: (row, 0))] * n
        specs += [pl.BlockSpec((tokens, tile), place)] * n
        operands += list(lefts) + list(rights)
        first += count
    return pl.pallas_call(
        functools.partial(weight_grad_kernel, blocks=blocks, n=n),
        grid=(first,),
        in_specs=specs,
        out_specs=pl.BlockSpec((rows, tile), lambda i: (0, i)),
        out_shape=jax.ShapeDtypeStruct((rows, first * tile), BF16),
        compiler_params=params(VMEM),
        cost_estimate=load(),
    )(*operands)


def widen_kernel(values, first, other):
    @pl.when(pl.program_id(0) == 0)
    def _():
        first[...] = values[...].astype(F32)

    @pl.when(pl.program_id(0) > 0)
    def _():
        other[...] = values[...].astype(F32)


def widen_joint(values, tile):
    rows, size = values.shape
    blocks = size // tile
    return pl.pallas_call(
        widen_kernel,
        grid=(blocks,),
        in_specs=[pl.BlockSpec((rows, tile), lambda i: (0, i))],
        out_specs=[
            pl.BlockSpec((rows, tile), lambda i: (0, 0)),
            pl.BlockSpec((None, rows, tile), lambda i: (jnp.maximum(i - 1, 0), 0, 0)),
        ],
        out_shape=[
            jax.ShapeDtypeStruct((rows, tile), F32),
            jax.ShapeDtypeStruct((blocks - 1, rows, tile), F32),
        ],
        compiler_params=params(VMEM),
        cost_estimate=load(),
    )(values)


def block_scores(place, slope, query, key, start_row, offset):
    rows = query.shape[0]
    raw = lax.dot_general(
        key, query, (((1,), (1,)), ((), ())), preferred_element_type=F32
    ) * (1.0 / math.sqrt(HD))
    shape = raw.shape
    key_pos = (place[0] ^ offset) * rows + lax.broadcasted_iota(jnp.int32, shape, 0)
    query_pos = place[0] * rows + lax.broadcasted_iota(jnp.int32, shape, 1)
    raw = raw + slope * (key_pos - query_pos).astype(F32)
    allowed = (key_pos <= query_pos) & (key_pos >= start_row)
    return raw, allowed


def forward_kernel(place, slopes, query, start, *refs, offsets, first_head):
    n = len(offsets)
    keyvals, (mixed, stats, held) = refs[:n], refs[-3:]
    slope = slopes[first_head + pl.program_id(0)]
    top = None
    for k, offset in enumerate(offsets):
        raw, allowed = block_scores(
            place, slope, query[...], keyvals[k][0], start[...], offset
        )
        raw = jnp.where(allowed, raw, MASKED)
        held[k] = raw
        peak = jnp.max(raw, axis=0, keepdims=True)
        top = peak if top is None else jnp.maximum(top, peak)
    total = None
    for k in range(n):
        fresh = jnp.exp(held[k] - top)
        held[k] = fresh
        part = jnp.sum(fresh, axis=0, keepdims=True)
        total = part if total is None else total + part
    stats[...] = top + jnp.log(total)
    inverse = 1.0 / total
    result = None
    for k in range(n):
        probs = (held[k] * inverse).astype(BF16)
        term = lax.dot_general(
            probs, keyvals[k][1], (((0,), (0,)), ((), ())), preferred_element_type=F32
        )
        result = term if result is None else result + term
    mixed[...] = result.astype(mixed.dtype)


def attention_forward(place, slopes, query, start, keyvals, first_head, heads, held=None):
    rows, columns = query.shape
    extra = [] if held is None else [held]
    n = len(keyvals)
    grid_spec = pltpu.PrefetchScalarGridSpec(
        num_scalar_prefetch=2,
        grid=(heads,),
        in_specs=[
            pl.BlockSpec((rows, HD), lambda h, *_: (0, first_head + h)),
            pl.BlockSpec((1, rows), lambda h, *_: (0, 0)),
        ]
        + [pl.BlockSpec((2, rows, HD), lambda h, *_: (0, 0, h))] * n
        + [pl.BlockSpec(memory_space=pl.ANY)] * len(extra),
        out_specs=[
            pl.BlockSpec((rows, HD), lambda h, *_: (0, first_head + h)),
            pl.BlockSpec((None, 1, rows), lambda h, *_: (h, 0, 0)),
        ],
        scratch_shapes=[pltpu.VMEM((n, rows, rows), F32)],
    )
    return pl.pallas_call(
        functools.partial(forward_kernel, offsets=ctx_offsets(), first_head=first_head),
        grid_spec=grid_spec,
        out_shape=[
            jax.ShapeDtypeStruct((rows, columns), BF16),
            jax.ShapeDtypeStruct((heads, 1, rows), F32),
        ],
        input_output_aliases={4 + n: 0} if extra else {},
        compiler_params=params(VMEM),
        cost_estimate=load(),
    )(place, slopes, query, start, *keyvals, *extra)


def backward_kernel(
    place, slopes, query, grad_mixed, start, stats, *refs, offsets, first_head
):
    n = len(offsets)
    keyvals = refs[:n]
    grad_query, near, far, probs_held, grads_held = refs[-5:]
    slope = slopes[first_head + pl.program_id(0)]
    scale = 1.0 / math.sqrt(HD)
    delta = None
    for k, offset in enumerate(offsets):
        raw, allowed = block_scores(
            place, slope, query[...], keyvals[k][0], start[...], offset
        )
        probs = jnp.where(allowed, jnp.exp(raw - stats[...]), 0.0)
        grads = lax.dot_general(
            keyvals[k][1],
            grad_mixed[...],
            (((1,), (1,)), ((), ())),
            preferred_element_type=F32,
        )
        probs_held[k] = probs
        grads_held[k] = grads
        part = jnp.sum(probs * grads, axis=0, keepdims=True)
        delta = part if delta is None else delta + part
    total = None
    for k, offset in enumerate(offsets):
        probs = probs_held[k]
        grad_scores = (probs * (grads_held[k] - delta)).astype(BF16)
        term = lax.dot_general(
            grad_scores,
            keyvals[k][0],
            (((0,), (0,)), ((), ())),
            preferred_element_type=F32,
        )
        total = term if total is None else total + term
        key_grad = jnp.dot(grad_scores, query[...], preferred_element_type=F32) * scale
        value_grad = jnp.dot(
            probs.astype(BF16), grad_mixed[...], preferred_element_type=F32
        )
        target, slot = (near, k) if k < n - n // 2 else (far, k - (n - n // 2))
        target[0, slot] = key_grad.astype(target.dtype)
        target[1, slot] = value_grad.astype(target.dtype)
    grad_query[...] = (total * scale).astype(grad_query.dtype)


def attention_backward(
    place, slopes, query, grad_mixed, start, stats, keyvals, first_head, heads, held=None,
    heavy=0,
):
    rows, columns = query.shape
    extra = [] if held is None else [held]
    n = len(keyvals)
    n_far = n // 2
    n_near = n - n_far
    grid_spec = pltpu.PrefetchScalarGridSpec(
        num_scalar_prefetch=2,
        grid=(heads,),
        in_specs=[
            pl.BlockSpec((rows, HD), lambda h, *_: (0, first_head + h)),
            pl.BlockSpec((rows, HD), lambda h, *_: (0, first_head + h)),
            pl.BlockSpec((1, rows), lambda h, *_: (0, 0)),
            pl.BlockSpec((None, 1, rows), lambda h, *_: (h, 0, 0)),
        ]
        + [pl.BlockSpec((2, rows, HD), lambda h, *_: (0, 0, h))] * n
        + [pl.BlockSpec(memory_space=pl.ANY)] * len(extra),
        out_specs=[
            pl.BlockSpec((rows, HD), lambda h, *_: (0, first_head + h)),
            pl.BlockSpec((2, n_near, rows, HD), lambda h, *_: (0, 0, 0, h)),
            pl.BlockSpec((2, max(n_far, 1), rows, HD), lambda h, *_: (0, 0, 0, h)),
        ],
        scratch_shapes=[pltpu.VMEM((n, rows, rows), F32)] * 2,
    )
    return pl.pallas_call(
        functools.partial(backward_kernel, offsets=ctx_offsets(), first_head=first_head),
        grid_spec=grid_spec,
        out_shape=[
            jax.ShapeDtypeStruct((rows, columns), BF16),
            jax.ShapeDtypeStruct((2, n_near, rows, heads * HD), BF16),
            jax.ShapeDtypeStruct((2, max(n_far, 1), rows, heads * HD), BF16),
        ],
        input_output_aliases={6 + n: 0} if extra else {},
        compiler_params=params(VMEM),
        cost_estimate=load(heavy),
    )(place, slopes, query, grad_mixed, start, stats, *keyvals, *extra)


def norm_backward(grad, unit, inverse, gain):
    scaled = grad * gain
    mean_scaled = jnp.mean(scaled, axis=-1, keepdims=True)
    mean_unit = jnp.mean(scaled * unit, axis=-1, keepdims=True)
    return inverse * (scaled - mean_scaled - unit * mean_unit)


def all_sum(values, axes):
    for axis in axes:
        bit = 1
        while bit < lax.axis_size(axis):
            values = values + xperm(values, axis, bit)
            bit *= 2
    return values


def spread_kernel(place, *refs, n_values, n_ctx, n_dp, piece):
    values, outs = refs[:n_values], refs[n_values:]
    for offset, out in enumerate(outs):
        for k, source in enumerate(values):
            for block in range(n_dp):
                column = (block * n_ctx + (place[0] ^ offset)) * piece
                part = source[:, pl.ds(pl.multiple_of(column, piece), piece)]
                row = (k * n_dp + block) * piece
                out[row : row + piece, :] = part.T


def spread_pieces(place, *values, heavy=0):
    tokens, width = values[0].shape
    n_dp, n_ctx = lax.axis_size("dp"), lax.axis_size("ctx")
    piece = width // (n_dp * n_ctx)
    shape = (len(values) * n_dp * piece, tokens)
    return pl.pallas_call(
        functools.partial(
            spread_kernel, n_values=len(values), n_ctx=n_ctx, n_dp=n_dp, piece=piece
        ),
        grid_spec=pltpu.PrefetchScalarGridSpec(
            num_scalar_prefetch=1,
            grid=(1,),
            in_specs=[pl.BlockSpec((tokens, width), lambda i, place: (0, 0))] * len(values),
            out_specs=[pl.BlockSpec(shape, lambda i, place: (0, 0))] * n_ctx,
        ),
        out_shape=[jax.ShapeDtypeStruct(shape, BF16)] * n_ctx,
        compiler_params=params(VMEM),
        cost_estimate=load(heavy),
    )(place, *values)


def spread_left(pieces):
    return [
        pieces[0] if offset == 0 else xperm(pieces[offset], "ctx", offset)
        for offset in ctx_offsets()
    ]


def shards(
    inputs,
    segments,
    first_gain,
    first_shift,
    in_weight,
    in_bias,
    out_weight,
    out_bias,
    second_gain,
    second_shift,
    up_weight,
    up_bias,
    down_weight,
    down_bias,
    cotangent,
):
    rows = inputs.shape[1]
    width = inputs.shape[2]
    local_width = in_weight.shape[2]
    local_hidden = up_weight.shape[1]
    heads_here = local_width // HD
    n_tensor = lax.axis_size("tensor")
    n_ctx = lax.axis_size("ctx")
    share = rows // n_tensor
    tensor_place = lax.axis_index("tensor")
    context_place = lax.axis_index("ctx")
    place = jnp.stack([context_place, lax.axis_index("dp")]).astype(jnp.int32)
    share_start = tensor_place * share

    def mine(values):
        return lax.dynamic_slice_in_dim(values, share_start, share, 0)

    head_index = (tensor_place * heads_here).astype(F32) + jnp.arange(heads_here, dtype=F32)
    slopes = jnp.exp2(-8.0 * (head_index + 1.0) / H)
    query_seg = lax.dynamic_slice_in_dim(segments[0], context_place * rows, rows)
    doc_start = jnp.sum(
        (segments[0][:, None] < query_seg[None, :]).astype(jnp.int32), axis=0, keepdims=True
    )

    gain_one, shift_one = first_gain.astype(F32), first_shift.astype(F32)
    gain_two, shift_two = second_gain.astype(F32), second_shift.astype(F32)
    second_vectors = jnp.stack([out_bias, second_gain, second_shift]).astype(F32)
    weight_in = in_weight.transpose(1, 0, 2)
    first_pair = jnp.stack([first_gain, first_shift]).astype(F32)
    cot_low = cotangent[0]

    order = []

    def then(values):
        values = after(values, order[-1]) if order else values
        return values

    def ran(values):
        order.append(jax.tree.leaves(values)[0])
        return values

    order = []

    def then(values):
        return after(values, order[-1]) if order else values

    def ran(values):
        order.append(jax.tree.leaves(values)[0])
        return values

    residual = inputs[0]
    groups = 2 if heads_here % 2 == 0 else 1
    group_heads = heads_here // groups
    group_width = group_heads * HD
    normed_first, *own = ran(
        project_kv(residual, first_pair, weight_in, in_bias, groups)
    )
    query = ran(
        mm(
            [then(normed_first)], [(weight_in, 0, 0)], trans=False, start=0, size=local_width,
            tile=1024, out_dtype=BF16, extras=(in_bias,), heavy=1,
        )
    )
    early_pieces = ran(spread_pieces(place, then(cot_low), normed_first, heavy=1))
    mixed, stats, keyvals = None, [], []
    for g in range(groups):
        keyvals.append(gather_ctx_causal(own[g], query if g == 0 else order[-1]))
        mixed, stat = ran(
            attention_forward(
                place, slopes, then(query), doc_start, keyvals[g], g * group_heads, group_heads,
                mixed,
            )
        )
        stats.append(stat)

    early_left = spread_left(lax.optimization_barrier((early_pieces, stats[0]))[0])

    def exchanged(part):
        return [part] + [xperm(part, "tensor", k) for k in range(1, n_tensor)]

    attention = exchanged(
        ran(
            mm(
                [then(mixed)], [out_weight], trans=True, start=0, size=width, tile=1024,
                out_dtype=BF16,
            )
        )
    )
    grad_active = ran(
        mm(
            [then(cot_low)], [down_weight], trans=False, start=0, size=local_hidden, tile=1024,
            out_dtype=F32,
        )
    )
    mixed_all = gather_ctx(mixed, [order[-1]])

    tile = local_hidden // 8
    half_hidden = local_hidden // 2
    up_bias_row = up_bias.astype(F32)[None]
    middle, normed_second, active_near, grad_near, bias_near = ran(
        first_up(
            residual, second_vectors, [after(then(attention[0]), early_left)] + attention[1:],
            up_weight, up_bias_row, grad_active, half_hidden, half_hidden, tile,
        )
    )
    active_far, grad_far, bias_far = ran(
        more_up(
            after(then(normed_second), mixed_all), up_weight, up_bias_row, grad_active,
            half_hidden, half_hidden, 2 * tile,
        )
    )

    def reduce_over_dp(parts, *deps):
        lefts, row, rights = parts[0]
        head = after(then(lefts[0]), *deps)
        whole = ran(
            weight_grad([([head] + lefts[1:], row, rights)] + parts[1:], width // n_ctx, 1024)
        )
        return lax.psum_scatter(whole, "dp", scatter_dimension=0, tiled=True)

    def grad_normed_part(side):
        part = ran(
            mm(
                [then(grad_near), grad_far], [(up_weight, None, 0), (up_weight, None, 1)],
                trans=True, start=side * (width // 2), size=width // 2, tile=512,
                out_dtype=BF16,
            )
        )
        return exchanged(part)

    normed_terms = [grad_normed_part(0), grad_normed_part(1)]
    near_rights = gather_ctx(active_near, [order[-1]])
    up_pieces = ran(spread_pieces(place, then(normed_second), heavy=1))
    down_parts = [reduce_over_dp([(early_left, 0, near_rights)])]
    near_sent = after(grad_near, order[-1])

    feed = ran(
        mm(
            [then(active_near), active_far],
            [(down_weight, None, 0), (down_weight, None, 1)], trans=True,
            start=0, size=width, tile=512, out_dtype=BF16, heavy=2,
        )
    )

    def tensor_scatter(values):
        total = mine(values).astype(F32)
        for k in range(1, n_tensor):
            piece = lax.dynamic_slice_in_dim(values, (tensor_place ^ k) * share, share, 0)
            total = total + xperm(piece, "tensor", k).astype(F32)
        return total

    feed_gate = order[-1]
    up_left = spread_left(up_pieces)

    def added(terms):
        total = after(terms[0], order[-1]).astype(F32)
        for term in terms[1:]:
            total = total + term.astype(F32)
        return total

    grad_normed = jnp.concatenate([added(terms) for terms in normed_terms], axis=1)
    unit_two, inverse_two = normalized(middle)
    cot = after(cot_low, order[-1]).astype(F32)
    grad_middle = cot + norm_backward(grad_normed, unit_two, inverse_two, gain_two)
    grad_middle_low = grad_middle.astype(BF16)
    grad_mixed = ran(
        mm(
            [then(grad_middle_low)], [out_weight], trans=False, start=0,
            size=local_width, tile=1024, out_dtype=BF16,
        )
    )
    down_parts.append(
        reduce_over_dp([(early_left, 0, gather_ctx(active_far, [feed_gate]))], up_left)
    )
    far_sent = after(grad_far, order[-1])
    grad_query, kv_near, kv_far = None, [], []
    for g in range(groups):
        grad_query, near, far = ran(
            attention_backward(
                place, slopes, then(query), grad_mixed, doc_start, stats[g], keyvals[g],
                g * group_heads, group_heads, grad_query, heavy=2 if g == 0 else 0,
            )
        )
        kv_near.append(near)
        kv_far.append(far)
    kv_received = [xperm(far, "ctx", 1) if n_ctx > 1 else None for far in kv_far]
    kv_near = after(kv_near, order[-1])

    near_all = gather_ctx(near_sent, [order[-1]])
    far_all = gather_ctx(far_sent, [order[-1]])
    up_part = reduce_over_dp([(up_left, 0, near_all), (up_left, 0, far_all)])
    up_gate = order[-1]
    late_pieces = ran(spread_pieces(place, then(grad_middle_low), heavy=2))
    late_left = spread_left(late_pieces)
    outputs = (mine(middle) + tensor_scatter(feed) + down_bias.astype(F32)).astype(BF16)

    grad_keys, grad_values = [], []
    for near, received in zip(kv_near, kv_received):
        blocks = [near[:, k] for k in range(near.shape[1])]
        if n_ctx > 1:
            blocks = [
                (block.astype(F32) + received[:, k].astype(F32))
                for k, block in enumerate(blocks)
            ]
            bits = ctx_bits()[:-1]
            for bit in reversed(bits):
                half = len(blocks) // 2
                got = [
                    xperm(sent.astype(BF16), "ctx", bit, lambda i, bit=bit: i > i ^ bit)
                    for sent in blocks[half:]
                ]
                blocks = [
                    after(block, order[-1]) + term.astype(F32)
                    for block, term in zip(blocks[:half], got)
                ]
        final = blocks[0].astype(BF16)
        grad_keys.append(final[0])
        grad_values.append(final[1])
    grad_keyvals = jnp.concatenate(grad_keys + grad_values, axis=1)
    gated = after(then(grad_keyvals), late_left)
    grad_first = ran(
        mm(
            [(grad_query, 0, local_width)] + [(gated, c, local_width) for c in range(2)],
            [(weight_in, c, 0) for c in range(3)], trans=True, start=0, size=width,
            tile=512, out_dtype=BF16, heavy=1,
        )
    )
    query_all = gather_ctx(after(grad_query, up_gate), [order[-1]])
    keyvals_all = gather_ctx(grad_keyvals, [order[-1]])
    joint_part = reduce_over_dp(
        [(late_left, 0, mixed_all), (early_left, 1, query_all), (early_left, 1, keyvals_all)],
        outputs,
    )
    grad_first_share = tensor_scatter(grad_first)
    unit_share, inverse_share = normalized(mine(inputs[0]).astype(F32))
    grad_from_first = norm_backward(grad_first_share, unit_share, inverse_share, gain_one)
    grad_middle_share = mine(grad_middle)
    input_grad = (grad_middle_share + grad_from_first).astype(BF16)

    def over_tokens(values):
        return jnp.sum(values, axis=0)

    grad_normed_share, unit_two_share = mine(grad_normed), mine(unit_two)
    sums = jnp.concatenate(
        [
            over_tokens(values).reshape(-1, local_width)
            for values in (
                grad_normed_share * unit_two_share,
                grad_normed_share,
                grad_middle_share,
                mine(cot),
                grad_first_share * unit_share,
                grad_first_share,
            )
        ]
    )
    count = sums.shape[0]
    sums = all_sum(sums, ("tensor",))
    sums = jnp.concatenate(
        [
            sums,
            over_tokens(grad_query.astype(F32))[None],
            over_tokens(grad_keyvals[:, local_width:].astype(F32))[None],
            jnp.concatenate([bias_near, bias_far], axis=1).reshape(-1, local_width),
        ]
    )
    sums = all_sum(sums, ("ctx", "dp"))
    vectors = sums[:count].reshape(6, width)
    in_bias_grad = sums[count : count + 2]
    up_bias_grad = sums[count + 2 :].reshape(-1)

    down_weight_grad = jnp.concatenate([part.astype(F32) for part in down_parts], axis=1)
    up_weight_grad = up_part.astype(F32)
    out_weight_grad, in_weight_grad = widen_joint(joint_part, local_width)
    return (
        outputs[None],
        input_grad[None],
        vectors[4],
        vectors[5],
        in_weight_grad.transpose(1, 0, 2),
        in_bias_grad,
        out_weight_grad,
        vectors[2],
        vectors[0],
        vectors[1],
        up_weight_grad,
        up_bias_grad,
        down_weight_grad,
        vectors[3],
    )


def solution(mesh):
    return jax.shard_map(
        shards,
        mesh=mesh,
        in_specs=(
            P("dp", "ctx", None),
            P("dp", None),
            P(),
            P(),
            P(None, None, "tensor"),
            P(None, "tensor"),
            P(None, "tensor"),
            P(),
            P(),
            P(),
            P(None, "tensor"),
            P("tensor"),
            P(None, "tensor"),
            P(),
            P("dp", "ctx", None),
        ),
        out_specs=(
            P("dp", ("ctx", "tensor"), None),
            P("dp", ("ctx", "tensor"), None),
            P(),
            P(),
            P(("dp", "ctx"), None, "tensor"),
            P(None, "tensor"),
            P(("dp", "ctx"), "tensor"),
            P(),
            P(),
            P(),
            P(("dp", "ctx"), "tensor"),
            P("tensor"),
            P(("dp", "ctx"), "tensor"),
            P(),
        ),
        check_vma=False,
    )
```

time: 604 us -> 412 us (0.68)
  waiting for transfers between devices: 252 us -> 133 us
  local copies, waits for them, and re-layouts: 78.6 us -> 22.8 us
  blocking collectives: 36.2 us -> 0 us
  Pallas kernels: 123 us -> 155 us
  starting transfers between devices: 57.2 us -> 48.1 us
    ppermute x52 -> x50, waiting for transfers between devices: 235 us -> 109 us  [xperm(): return lax.ppermute(values, axis, pairs)]
    all_to_all x2 -> x0, blocking collectives: 36.2 us -> none  [spread_left(): return lax.all_to_all(parts, 'ctx', 0, 0, tiled=True)]
    unnamed x146 -> x129, local copies, waits for them, and re-layouts: 47.7 us -> 16.9 us
    reduce_scatter x8 -> x4, waiting for transfers between devices: 0.01 us -> 23.9 us  [reduce_over_dp(): return lax.psum_scatter(whole, 'dp', scatter_dimension=0, tiled=True)]
    pallas_call x12 -> x11, Pallas kernels: 48 us -> 70.4 us  [the longest x4 32 us: weight_grad(): pl.pallas_call(functools.partial(weight_grad_kernel, blocks=blocks, n=n),...]
    all_to_all x2 -> x0, waiting for transfers between devices: 17.3 us -> none  [spread_left(): return lax.all_to_all(parts, 'ctx', 0, 0, tiled=True)]
    all_to_all x2 -> x0, starting transfers between devices: 10.9 us -> none  [spread_left(): return lax.all_to_all(parts, 'ctx', 0, 0, tiled=True)]
    reshape x7, local copies, waits for them, and re-layouts: 10.1 us -> 0.08 us  [the longest x6 0.07 us: shards(): over_tokens(values).reshape(-1, local_width)]
  transfers between devices with their start and end apart: 62 -> 54, of which waited for: 28 -> 19; matrix products, arithmetic and copies ran while one was open for 11% -> 11% of each run, Pallas kernels for 16% -> 33%
where the time goes in v2:
time: 412 us; the launch traced here: 410 us
  Pallas kernels  155 us (38%)
  waiting for transfers between devices  133 us (32%)
  starting transfers between devices  48.1 us (12%)
  other arithmetic  36.7 us (9%)
  local copies, waits for them, and re-layouts  22.8 us (6%)
  between operations  14.7 us (4%)
    ppermute x50, waiting for transfers between devices, xperm(): return lax.ppermute(values, axis, pairs)  109 us
    pallas_call x8, Pallas kernels, mm(): pl.pallas_call(functools.partial(mm_kernel, n_pairs=len(lefts), trans=tra...  55 us
    ppermute x50, starting transfers between devices, xperm(): return lax.ppermute(values, axis, pairs)  47.5 us
    pallas_call x4, Pallas kernels, weight_grad(): pl.pallas_call(functools.partial(weight_grad_kernel, blocks=blocks, n=n),...  32 us
    reduce_scatter x4, waiting for transfers between devices, reduce_over_dp(): return lax.psum_scatter(whole, 'dp', scatter_dimension=0, tiled=True)  23.9 us
    unnamed x129, local copies, waits for them, and re-layouts  16.9 us
    pallas_call x2, Pallas kernels, attention_backward(): pl.pallas_call(functools.partial(backward_kernel, offsets=ctx_offsets(),...  16 us
    pallas_call x2, Pallas kernels, attention_forward(): pl.pallas_call(functools.partial(forward_kernel, offsets=ctx_offsets(), f...  13.2 us
  transfers between devices with their start and end apart: 54, of which 19 were waited for; matrix products, arithmetic and copies ran while one was open for 11% of the time, Pallas kernels for 33%

profile of v2, /device:TPU:0, one launch (start us, length us, event | category | flops | bytes accessed | tf_op | source)
XLA Modules:
  0.0 410.2 jit_solution(11238555382267467861)
XLA Ops:
  9.2 6.5 %shard_map.254 = (bf16[256,2048]{1,0:T(8,128)(2,1)}, bf16[2,256,512]{2,1,0:T(8,128)(2,1)}, bf16[2,256,512]{2,1,0:T(8,128)(2,1)}) custom-call(bf16[256,2048]{1,0:T(8,128)(2,1)} %bitcast.101, f32[2,2048]{1,0:T(2,128)} %maximum_convert_fusion.2.pair, bf16[3,2048,1024]{2,1,0:T(8,128)(2,1)} %bitcast.96, bf16[2,1024]{1,0:T(2,128)(2,1)} %refs_2_.4), custom_call_target="tpu_custom_call" | custom-call | tf_op jit(solution)/shard_map/pallas_call | solution.py:153
  18.1 4.3 %collective-permute-start = (bf16[2,256,512]{2,1,0:T(8,128)(2,1)}, bf16[2,256,512]{2,1,0:T(8,128)(2,1)S(1)}, u32[]{:S(2)}, u32[]{:S(2)}) collective-permute-start(bf16[2,256,512]{2,1,0:T(8,128)(2,1)} %get-tuple-element.110.refs_0_), channel_id=1, source_target_pairs={{0,4},{2,6},{1,5},{3,7},{8,12},{10,14},{9,13},{11,15},{16,20},{18,... | collective-permute-start | bytes 1572872 | tf_op jit(solution)/shard_map/ppermute | solution.py:40
  25.1 4.5 %shard_map.255.query = bf16[256,1024]{1,0:T(8,128)(2,1)} custom-call(bf16[256,2048]{1,0:T(8,128)(2,1)} %get-tuple-element.106.refs_0_.refs_1_, bf16[3,2048,1024]{2,1,0:T(8,128)(2,1)} %bitcast.97, bf16[2,1024]{1,0:T(2,128)(2,1)} %refs_2_.4), custom_call_target="tpu_custom_call" | custom-call | flops 10000000000 | bytes 10000000 | tf_op jit(solution)/shard_map/pallas_call | solution.py:124
  30.3 4.8 %collective-permute-done.refs_1_ = bf16[2,256,512]{2,1,0:T(8,128)(2,1)S(1)} collective-permute-done((bf16[2,256,512]{2,1,0:T(8,128)(2,1)}, bf16[2,256,512]{2,1,0:T(8,128)(2,1)S(1)}, u32[]{:S(2)}, u32[]{:S(2)}) %collective-permute-start) | collective-permute-done | bytes 524320 | tf_op jit(solution)/shard_map/ppermute | solution.py:40
  42.2 6.6 %shard_map.257 = (bf16[256,1024]{1,0:T(8,128)(2,1)}, f32[4,1,256]{2,1,0:T(1,128)}) custom-call(s32[2]{0:T(128)} %pad_add_fusion.place, f32[8]{0:T(128)} %multiply_exponential_fusion.slopes, bf16[256,1024]{1,0:T(8,128)(2,1)} %shard_map.255.query, s32[1,256]{1,0:T(1,128)} %bitcast.115, bf16[2,256,512]{2,1,0:T(8,128)(2,1)} %get-tuple-element.110.refs_0_, ...), custom_call_target="tpu_custom_call" | custom-call | tf_op jit(solution)/shard_map/pallas_call | solution.py:417
  51.3 6.6 %shard_map.258 = (bf16[256,1024]{1,0:T(8,128)(2,1)}, f32[4,1,256]{2,1,0:T(1,128)}) custom-call(s32[2]{0:T(128)} %pad_add_fusion.place, f32[8]{0:T(128)} %multiply_exponential_fusion.slopes, bf16[256,1024]{1,0:T(8,128)(2,1)} %shard_map.255.query, s32[1,256]{1,0:T(1,128)} %bitcast.116, ...), custom_call_target="tpu_custom_call", output_to_operand_aliasing={{0}: (8, {})} | custom-call | tf_op jit(solution)/shard_map/pallas_call | solution.py:417
  63.6 5.9 %collective-permute-start.6 = (bf16[1024,256]{1,0:T(8,128)(2,1)S(1)}, bf16[1024,256]{1,0:T(8,128)(2,1)S(1)}, u32[]{:S(2)}, u32[]{:S(2)}) collective-permute-start(bf16[1024,256]{1,0:T(8,128)(2,1)S(1)} %copy-done.58), channel_id=1, source_target_pairs={{0,4},{2,6},{4,0},{6,2},{1,5},{3,7},{5,1},{7,3},{8,12},{10,14},{12... | collective-permute-start | bytes 1572872 | tf_op jit(solution)/shard_map/ppermute | solution.py:40
  73.0 10.4 %shard_map.260.refs_6_.grad_active = f32[256,4096]{1,0:T(8,128)} custom-call(bf16[256,2048]{1,0:T(8,128)(2,1)} %bitcast.104, bf16[2048,4096]{1,0:T(8,128)(2,1)} %refs_3_.5), custom_call_target="tpu_custom_call" | custom-call | tf_op jit(solution)/shard_map/pallas_call | solution.py:124
  83.4 9.6 %collective-permute-done.8.refs_3_.refs_11_.refs_19_ = bf16[1024,256]{1,0:T(8,128)(2,1)S(1)} collective-permute-done((bf16[1024,256]{1,0:T(8,128)(2,1)S(1)}, bf16[1024,256]{1,0:T(8,128)(2,1)S(1)}, u32[]{:S(2)}, u32[]{:S(2)}) %collective-permute-start.8) | collective-permute-done | bytes 524320 | tf_op jit(solution)/shard_map/ppermute | solution.py:40
  94.0 10.1 %shard_map.261 = (f32[256,2048]{1,0:T(8,128)}, bf16[256,2048]{1,0:T(8,128)(2,1)}, bf16[256,2048]{1,0:T(8,128)(2,1)}, bf16[256,2048]{1,0:T(8,128)(2,1)}, f32[1,2048]{1,0:T(1,128)}) custom-call(bf16[256,2048]{1,0:T(8,128)(2,1)} %bitcast.102, f32[3,2048]{1,0:T(4,128)} %maximum_convert_fusion.1.refs_1_, bf16[256,2048]{1,0:T(8,128)(2,1)} %shard_map.259.refs_2_, ...), custom_call_target="tpu_custom_call" | custom-call | tf_op jit(solution)/shard_map/pallas_call | solution.py:240
  108.5 8.1 %shard_map.262 = (bf16[256,2048]{1,0:T(8,128)(2,1)}, bf16[256,2048]{1,0:T(8,128)(2,1)}, f32[1,2048]{1,0:T(1,128)}) custom-call(bf16[256,2048]{1,0:T(8,128)(2,1)} %get-tuple-element.141.norm.refs_0_, bf16[2048,4096]{1,0:T(8,128)(2,1)} %refs_3_.4, f32[1,4096]{1,0:T(1,128)} %bitcast.109, f32[256,4096]{1,0:T(8,128)} %shard_map.260.refs_6_.grad_active), custom_call_target="tpu_custom_call" | custom-call | tf_op jit(solution)/shard_map/pallas_call | solution.py:263
  116.6 6.2 %shard_map.263 = bf16[256,1024]{1,0:T(8,128)(2,1)} custom-call(bf16[256,2048]{1,0:T(8,128)(2,1)} %get-tuple-element.169.refs_0_.refs_4_, bf16[256,2048]{1,0:T(8,128)(2,1)} %get-tuple-element.172.refs_1_.refs_12_, bf16[2048,4096]{1,0:T(8,128)(2,1)} %refs_3_.4, bf16[2048,4096]{1,0:T(8,128)(2,1)} %refs_3_.4), custom_call_target="tpu_custom_call" | custom-call | tf_op jit(solution)/shard_map/pallas_call | solution.py:124
  122.8 6.2 %shard_map.264 = bf16[256,1024]{1,0:T(8,128)(2,1)} custom-call(bf16[256,2048]{1,0:T(8,128)(2,1)} %get-tuple-element.169.refs_0_.refs_4_, bf16[256,2048]{1,0:T(8,128)(2,1)} %get-tuple-element.172.refs_1_.refs_12_, bf16[2048,4096]{1,0:T(8,128)(2,1)} %refs_3_.4, bf16[2048,4096]{1,0:T(8,128)(2,1)} %refs_3_.4), custom_call_target="tpu_custom_call" | custom-call | tf_op jit(solution)/shard_map/pallas_call | solution.py:124
  137.8 5.6 %shard_map.266 = bf16[512,2048]{1,0:T(8,128)(2,1)} custom-call(bf16[1024,256]{1,0:T(8,128)(2,1)} %get-tuple-element.155.refs_0_.refs_8_.refs_16_, bf16[1024,256]{1,0:T(8,128)(2,1)} %copy-done.11, bf16[1024,256]{1,0:T(8,128)(2,1)} %copy-done.12, bf16[1024,256]{1,0:T(8,128)(2,1)} %copy-done.13, bf16[256,2048]{1,0:T(8,128)(2,1)} %get-tuple-element.146.refs_4_.refs_0_, ...), custom_call_target="tpu_custom_call" | custom-call | tf_op jit(solution)/shard_map/pallas_call | solution.py:313
  143.7 10.4 %shard_map.267 = bf16[256,2048]{1,0:T(8,128)(2,1)} custom-call(bf16[256,2048]{1,0:T(8,128)(2,1)} %get-tuple-element.146.refs_4_.refs_0_, bf16[256,2048]{1,0:T(8,128)(2,1)} %get-tuple-element.156.refs_1_.refs_4_, bf16[2048,4096]{1,0:T(8,128)(2,1)} %refs_3_.5, bf16[2048,4096]{1,0:T(8,128)(2,1)} %refs_3_.5), custom_call_target="tpu_custom_call" | custom-call | flops 999999995904 | bytes 10000000 | tf_op jit(solution)/shard_map/pallas_call | solution.py:124
  165.3 4.6 %shard_map.268.grad_mixed = bf16[256,1024]{1,0:T(8,128)(2,1)} custom-call(bf16[256,2048]{1,0:T(8,128)(2,1)} %get-tuple-element.174.refs_0_, bf16[2048,1024]{1,0:T(8,128)(2,1)} %refs_1_.5), custom_call_target="tpu_custom_call" | custom-call | tf_op jit(solution)/shard_map/pallas_call | solution.py:124
  173.5 5.6 %shard_map.269 = bf16[512,2048]{1,0:T(8,128)(2,1)} custom-call(bf16[1024,256]{1,0:T(8,128)(2,1)} %get-tuple-element.155.refs_0_.refs_8_.refs_16_, bf16[1024,256]{1,0:T(8,128)(2,1)} %copy-done.11, bf16[1024,256]{1,0:T(8,128)(2,1)} %copy-done.12, bf16[1024,256]{1,0:T(8,128)(2,1)} %copy-done.13, bf16[256,2048]{1,0:T(8,128)(2,1)} %get-tuple-element.156.refs_1_.refs_4_, ...), custom_call_target="tpu_custom_call" | custom-call | tf_op jit(solution)/shard_map/pallas_call | solution.py:313
  179.7 7.9 %shard_map.270 = (bf16[256,1024]{1,0:T(8,128)(2,1)}, bf16[2,2,256,512]{3,2,1,0:T(8,128)(2,1)}, bf16[2,2,256,512]{3,2,1,0:T(8,128)(2,1)}) custom-call(s32[2]{0:T(128)} %pad_add_fusion.place, f32[8]{0:T(128)} %multiply_exponential_fusion.slopes, bf16[256,1024]{1,0:T(8,128)(2,1)} %shard_map.255.query, bf16[256,1024]{1,0:T(8,128)(2,1)} %shard_map.268.grad_mixed, ...), custom_call_target="tpu_custom_call" | custom-call | flops 999999995904 | bytes 10000000 | tf_op jit(solution)/shard_map/pallas_call | solution.py:502
  189.0 8.1 %shard_map.271 = (bf16[256,1024]{1,0:T(8,128)(2,1)}, bf16[2,2,256,512]{3,2,1,0:T(8,128)(2,1)}, bf16[2,2,256,512]{3,2,1,0:T(8,128)(2,1)}) custom-call(s32[2]{0:T(128)} %pad_add_fusion.place, f32[8]{0:T(128)} %multiply_exponential_fusion.slopes, bf16[256,1024]{1,0:T(8,128)(2,1)} %shard_map.255.query, ...), custom_call_target="tpu_custom_call", output_to_operand_aliasing={{0}: (10, {})} | custom-call | tf_op jit(solution)/shard_map/pallas_call | solution.py:502
  199.5 18.5 %collective-permute-done.29.refs_13_ = bf16[256,2048]{1,0:T(8,128)(2,1)} collective-permute-done((bf16[256,2048]{1,0:T(8,128)(2,1)}, bf16[256,2048]{1,0:T(8,128)(2,1)}, u32[]{:S(2)}, u32[]{:S(2)}) %collective-permute-start.29) | collective-permute-done | bytes 1048608 | tf_op jit(solution)/shard_map/ppermute | solution.py:40
  226.4 10.3 %shard_map.272 = bf16[512,4096]{1,0:T(8,128)(2,1)} custom-call(bf16[512,256]{1,0:T(8,128)(2,1)} %get-tuple-element.167.refs_0_.refs_8_, bf16[512,256]{1,0:T(8,128)(2,1)} %collective-permute-done.19.refs_1_.refs_9_, bf16[512,256]{1,0:T(8,128)(2,1)} %collective-permute-done.20.refs_2_.refs_10_, bf16[512,256]{1,0:T(8,128)(2,1)} %collective-permute-done.21.refs_3_.refs_11_, ...), custom_call_target="tpu_custom_call" | custom-call | tf_op jit(solution)/shard_map/pallas_call | solution.py:313
  240.3 4.2 %collective-permute-start.35 = (bf16[512,256]{1,0:T(8,128)(2,1)}, bf16[512,256]{1,0:T(8,128)(2,1)}, u32[]{:S(2)}, u32[]{:S(2)}) collective-permute-start(bf16[512,256]{1,0:T(8,128)(2,1)} %get-tuple-element.181), channel_id=1, source_target_pairs={{0,4},{2,6},{4,0},{6,2},{1,5},{3,7},{5,1},{7,3},{8,12},{10,14},{12... | collective-permute-start | bytes 786440 | tf_op jit(solution)/shard_map/ppermute | solution.py:40
  257.5 8.6 %shard_map.274 = bf16[256,2048]{1,0:T(8,128)(2,1)} custom-call(bf16[256,1024]{1,0:T(8,128)(2,1)} %get-tuple-element.190.refs_0_.refs_12_, bf16[256,2048]{1,0:T(8,128)(2,1)} %copy-done.3, bf16[256,2048]{1,0:T(8,128)(2,1)} %copy-done.3, bf16[3,2048,1024]{2,1,0:T(8,128)(2,1)} %bitcast.98, bf16[3,2048,1024]{2,1,0:T(8,128)(2,1)} %bitcast.99, ...), custom_call_target="tpu_custom_call" | custom-call | flops 10000000000 | bytes 10000000 | tf_op jit(solution)/shard_map/pallas_call | solution.py:124
  266.1 15.8 %collective-permute-done.47.refs_21_ = bf16[256,2048]{1,0:T(8,128)(2,1)} collective-permute-done((bf16[256,2048]{1,0:T(8,128)(2,1)S(1)}, bf16[256,2048]{1,0:T(8,128)(2,1)}, u32[]{:S(2)}, u32[]{:S(2)}) %collective-permute-start.47) | collective-permute-done | bytes 1048608 | tf_op jit(solution)/shard_map/ppermute | solution.py:40
  283.8 8.4 %collective-permute-done.44.refs_13_ = bf16[256,1024]{1,0:T(8,128)(2,1)} collective-permute-done((bf16[256,1024]{1,0:T(8,128)(2,1)}, bf16[256,1024]{1,0:T(8,128)(2,1)}, u32[]{:S(2)}, u32[]{:S(2)}) %collective-permute-start.44) | collective-permute-done | bytes 524320 | tf_op jit(solution)/shard_map/ppermute | solution.py:40
  292.7 4.7 %collective-permute-done.16 = bf16[128,2048]{1,0:T(8,128)(2,1)} collective-permute-done((bf16[128,2048]{1,0:T(8,128)(2,1)}, bf16[128,2048]{1,0:T(8,128)(2,1)}, u32[]{:S(2)}, u32[]{:S(2)}) %collective-permute-start.16) | collective-permute-done | bytes 524320 | tf_op jit(solution)/shard_map/ppermute | solution.py:40
  300.6 10.6 %shard_map.275 = bf16[512,4096]{1,0:T(8,128)(2,1)} custom-call(bf16[512,256]{1,0:T(8,128)(2,1)} %get-tuple-element.188.refs_0_, bf16[512,256]{1,0:T(8,128)(2,1)} %collective-permute-done.35.refs_1_, bf16[512,256]{1,0:T(8,128)(2,1)} %collective-permute-done.36.refs_2_, bf16[512,256]{1,0:T(8,128)(2,1)} %collective-permute-done.37.refs_3_, ...), custom_call_target="tpu_custom_call" | custom-call | tf_op jit(solution)/shard_map/pallas_call | solution.py:313
  320.1 6.8 %collective-permute-done.38 = bf16[128,2048]{1,0:T(8,128)(2,1)} collective-permute-done((bf16[128,2048]{1,0:T(8,128)(2,1)}, bf16[128,2048]{1,0:T(8,128)(2,1)}, u32[]{:S(2)}, u32[]{:S(2)}) %collective-permute-start.38) | collective-permute-done | bytes 524320 | tf_op jit(solution)/shard_map/ppermute | solution.py:40
  337.9 4.3 %collective-permute-done.41 = f32[18,1024]{1,0:T(8,128)S(1)} collective-permute-done((f32[18,1024]{1,0:T(8,128)S(1)}, f32[18,1024]{1,0:T(8,128)S(1)}, u32[]{:S(2)}, u32[]{:S(2)}) %collective-permute-start.41) | collective-permute-done | bytes 73760 | tf_op jit(solution)/shard_map/ppermute | solution.py:40
  343.9 8.5 %collective-permute-done.42 = f32[18,1024]{1,0:T(8,128)S(1)} collective-permute-done((f32[18,1024]{1,0:T(8,128)S(1)}, f32[18,1024]{1,0:T(8,128)S(1)}, u32[]{:S(2)}, u32[]{:S(2)}) %collective-permute-start.42) | collective-permute-done | bytes 73760 | tf_op jit(solution)/shard_map/ppermute | solution.py:40
  354.1 12.0 %collective-permute-done.43 = f32[18,1024]{1,0:T(8,128)S(1)} collective-permute-done((f32[18,1024]{1,0:T(8,128)S(1)}, f32[18,1024]{1,0:T(8,128)S(1)}, u32[]{:S(2)}, u32[]{:S(2)}) %collective-permute-start.43) | collective-permute-done | bytes 73760 | tf_op jit(solution)/shard_map/ppermute | solution.py:40
  376.5 23.9 %reduce-scatter.5.cloned.1.call-done.values = bf16[128,4096]{1,0:T(8,128)(2,1)} async-done(((bf16[512,4096]{1,0:T(8,128)(2,1)}), bf16[128,4096]{1,0:T(8,128)(2,1)}) %reduce-scatter.5.cloned.1.call-update) | async-done | bytes 1048592 | tf_op jit(solution)/shard_map/reduce_scatter | solution.py:705
  (298 shorter events, 127.0 us)
Async XLA Ops:
  7.2 363.8 %reduce-scatter.9.cloned.1.call-start = ((), (), s32[]{:S(2)}) async-start(), calls=%async_computation.6 | async-start | bytes 2621440 | tf_op jit(solution)/shard_map/reduce_scatter | solution.py:705
  15.7 25.4 %collective-permute-start.1 = (bf16[2,256,512]{2,1,0:T(8,128)(2,1)}, bf16[2,256,512]{2,1,0:T(8,128)(2,1)S(1)}, u32[]{:S(2)}, u32[]{:S(2)}) collective-permute-start(bf16[2,256,512]{2,1,0:T(8,128)(2,1)} %get-tuple-element.110.refs_0_), channel_id=1, source_target_pairs={{0,2},{4,6},{1,3},{5,7},{8,10},{12,14},{9,11},{13,15},{16,18},{20,... | collective-permute-start | bytes 1572872 | tf_op jit(solution)/shard_map/ppermute | solution.py:40
  18.1 16.9 %collective-permute-start = (bf16[2,256,512]{2,1,0:T(8,128)(2,1)}, bf16[2,256,512]{2,1,0:T(8,128)(2,1)S(1)}, u32[]{:S(2)}, u32[]{:S(2)}) collective-permute-start(bf16[2,256,512]{2,1,0:T(8,128)(2,1)} %get-tuple-element.110.refs_0_), channel_id=1, source_target_pairs={{0,4},{2,6},{1,5},{3,7},{8,12},{10,14},{9,13},{11,15},{16,20},{18,... | collective-permute-start | bytes 1572872 | tf_op jit(solution)/shard_map/ppermute | solution.py:40
  22.4 27.3 %collective-permute-start.4 = (bf16[2,256,512]{2,1,0:T(8,128)(2,1)}, bf16[2,256,512]{2,1,0:T(8,128)(2,1)S(1)}, u32[]{:S(2)}, u32[]{:S(2)}) collective-permute-start(bf16[2,256,512]{2,1,0:T(8,128)(2,1)} %get-tuple-element.114.refs_0_), channel_id=1, source_target_pairs={{0,2},{4,6},{1,3},{5,7},{8,10},{12,14},{9,11},{13,15},{16,18},{20,... | collective-permute-start | bytes 1572872 | tf_op jit(solution)/shard_map/ppermute | solution.py:40
  23.7 25.0 %collective-permute-start.3 = (bf16[2,256,512]{2,1,0:T(8,128)(2,1)}, bf16[2,256,512]{2,1,0:T(8,128)(2,1)S(1)}, u32[]{:S(2)}, u32[]{:S(2)}) collective-permute-start(bf16[2,256,512]{2,1,0:T(8,128)(2,1)} %get-tuple-element.114.refs_0_), channel_id=1, source_target_pairs={{0,4},{2,6},{1,5},{3,7},{8,12},{10,14},{9,13},{11,15},{16,20},{18,... | collective-permute-start | bytes 1572872 | tf_op jit(solution)/shard_map/ppermute | solution.py:40
  62.1 30.9 %collective-permute-start.9 = (bf16[256,2048]{1,0:T(8,128)(2,1)}, bf16[256,2048]{1,0:T(8,128)(2,1)S(1)}, u32[]{:S(2)}, u32[]{:S(2)}) collective-permute-start(bf16[256,2048]{1,0:T(8,128)(2,1)} %shard_map.259.refs_2_), channel_id=1, source_target_pairs={{0,1},{1,0},{2,3},{3,2},{4,5},{5,4},{6,7},{7,6},{8,9},{9,8},{10,11... | collective-permute-start | bytes 3145736 | tf_op jit(solution)/shard_map/ppermute | solution.py:40
  63.6 19.8 %collective-permute-start.6 = (bf16[1024,256]{1,0:T(8,128)(2,1)S(1)}, bf16[1024,256]{1,0:T(8,128)(2,1)S(1)}, u32[]{:S(2)}, u32[]{:S(2)}) collective-permute-start(bf16[1024,256]{1,0:T(8,128)(2,1)S(1)} %copy-done.58), channel_id=1, source_target_pairs={{0,4},{2,6},{4,0},{6,2},{1,5},{3,7},{5,1},{7,3},{8,12},{10,14},{12... | collective-permute-start | bytes 1572872 | tf_op jit(solution)/shard_map/ppermute | solution.py:40
  69.5 23.5 %collective-permute-start.8 = (bf16[1024,256]{1,0:T(8,128)(2,1)S(1)}, bf16[1024,256]{1,0:T(8,128)(2,1)S(1)}, u32[]{:S(2)}, u32[]{:S(2)}) collective-permute-start(bf16[1024,256]{1,0:T(8,128)(2,1)S(1)} %copy-done.56), channel_id=1, source_target_pairs={{0,6},{2,4},{4,2},{6,0},{1,7},{3,5},{5,3},{7,1},{8,14},{10,12},{12... | collective-permute-start | bytes 1572872 | tf_op jit(solution)/shard_map/ppermute | solution.py:40
  69.7 35.2 %collective-permute-start.10 = (bf16[256,1024]{1,0:T(8,128)(2,1)S(1)}, bf16[256,1024]{1,0:T(8,128)(2,1)S(1)}, u32[]{:S(2)}, u32[]{:S(2)}) collective-permute-start(bf16[256,1024]{1,0:T(8,128)(2,1)S(1)} %copy-done.16), channel_id=1, source_target_pairs={{0,4},{2,6},{4,0},{6,2},{1,5},{3,7},{5,1},{7,3},{8,12},{10,14},{12... | collective-permute-start | bytes 1572872 | tf_op jit(solution)/shard_map/ppermute | solution.py:40
  104.1 27.3 %collective-permute-start.13 = (bf16[256,2048]{1,0:T(8,128)(2,1)}, bf16[256,2048]{1,0:T(8,128)(2,1)}, u32[]{:S(2)}, u32[]{:S(2)}) collective-permute-start(bf16[256,2048]{1,0:T(8,128)(2,1)} %get-tuple-element.146.refs_4_.refs_0_), channel_id=1, source_target_pairs={{0,4},{2,6},{4,0},{6,2},{1,5},{3,7},{5,1},{7,3},{8,12},{10,14},{12... | collective-permute-start | bytes 3145736 | tf_op jit(solution)/shard_map/ppermute | solution.py:40
  129.0 28.5 %collective-permute-start.18 = (bf16[256,1024]{1,0:T(8,128)(2,1)}, bf16[256,1024]{1,0:T(8,128)(2,1)}, u32[]{:S(2)}, u32[]{:S(2)}) collective-permute-start(bf16[256,1024]{1,0:T(8,128)(2,1)} %shard_map.264), channel_id=1, source_target_pairs={{0,1},{1,0},{2,3},{3,2},{4,5},{5,4},{6,7},{7,6},{8,9},{9,8},{10,11... | collective-permute-start | bytes 1572872 | tf_op jit(solution)/shard_map/ppermute | solution.py:40
  129.5 29.8 %collective-permute-start.17 = (bf16[256,1024]{1,0:T(8,128)(2,1)}, bf16[256,1024]{1,0:T(8,128)(2,1)}, u32[]{:S(2)}, u32[]{:S(2)}) collective-permute-start(bf16[256,1024]{1,0:T(8,128)(2,1)} %shard_map.263), channel_id=1, source_target_pairs={{0,1},{1,0},{2,3},{3,2},{4,5},{5,4},{6,7},{7,6},{8,9},{9,8},{10,11... | collective-permute-start | bytes 1572872 | tf_op jit(solution)/shard_map/ppermute | solution.py:40
  131.0 26.4 %collective-permute-start.22 = (bf16[256,2048]{1,0:T(8,128)(2,1)}, bf16[256,2048]{1,0:T(8,128)(2,1)}, u32[]{:S(2)}, u32[]{:S(2)}) collective-permute-start(bf16[256,2048]{1,0:T(8,128)(2,1)} %get-tuple-element.156.refs_1_.refs_4_), channel_id=1, source_target_pairs={{0,4},{2,6},{4,0},{6,2},{1,5},{3,7},{5,1},{7,3},{8,12},{10,14},{12... | collective-permute-start | bytes 3145736 | tf_op jit(solution)/shard_map/ppermute | solution.py:40
  136.1 33.7 %collective-permute-start.19 = (bf16[512,256]{1,0:T(8,128)(2,1)}, bf16[512,256]{1,0:T(8,128)(2,1)}, u32[]{:S(2)}, u32[]{:S(2)}) collective-permute-start(bf16[512,256]{1,0:T(8,128)(2,1)} %get-tuple-element.152), channel_id=1, source_target_pairs={{0,4},{2,6},{4,0},{6,2},{1,5},{3,7},{5,1},{7,3},{8,12},{10,14},{12... | collective-permute-start | bytes 786440 | tf_op jit(solution)/shard_map/ppermute | solution.py:40
  137.8 32.1 %collective-permute-start.20 = (bf16[512,256]{1,0:T(8,128)(2,1)}, bf16[512,256]{1,0:T(8,128)(2,1)}, u32[]{:S(2)}, u32[]{:S(2)}) collective-permute-start(bf16[512,256]{1,0:T(8,128)(2,1)} %get-tuple-element.153), channel_id=1, source_target_pairs={{0,2},{2,0},{4,6},{6,4},{1,3},{3,1},{5,7},{7,5},{8,10},{10,8},{12,... | collective-permute-start | bytes 786440 | tf_op jit(solution)/shard_map/ppermute | solution.py:40
  143.4 227.6 %reduce-scatter.11.cloned.1.call-start = ((), (), s32[]{:S(2)}) async-start(), calls=%async_computation.7 | async-start | bytes 2621440 | tf_op jit(solution)/shard_map/reduce_scatter | solution.py:705
  157.5 14.0 %collective-permute-start.23 = (bf16[256,2048]{1,0:T(8,128)(2,1)}, bf16[256,2048]{1,0:T(8,128)(2,1)S(1)}, u32[]{:S(2)}, u32[]{:S(2)}) collective-permute-start(bf16[256,2048]{1,0:T(8,128)(2,1)} %get-tuple-element.156.refs_1_.refs_4_), channel_id=1, source_target_pairs={{0,2},{2,0},{4,6},{6,4},{1,3},{3,1},{5,7},{7,5},{8,10},{10,8},{12,... | collective-permute-start | bytes 3145736 | tf_op jit(solution)/shard_map/ppermute | solution.py:40
  169.9 29.1 %collective-permute-start.26 = (bf16[256,2048]{1,0:T(8,128)(2,1)}, bf16[256,2048]{1,0:T(8,128)(2,1)}, u32[]{:S(2)}, u32[]{:S(2)}) collective-permute-start(bf16[256,2048]{1,0:T(8,128)(2,1)} %get-tuple-element.169.refs_0_.refs_4_), channel_id=1, source_target_pairs={{0,4},{2,6},{4,0},{6,2},{1,5},{3,7},{5,1},{7,3},{8,12},{10,14},{12... | collective-permute-start | bytes 3145736 | tf_op jit(solution)/shard_map/ppermute | solution.py:40
  179.1 194.6 %reduce-scatter.7.cloned.1.call-start = ((), (), s32[]{:S(2)}) async-start(), calls=%async_computation.5 | async-start | bytes 5242880 | tf_op jit(solution)/shard_map/reduce_scatter | solution.py:705
  179.1 38.9 %collective-permute-start.29 = (bf16[256,2048]{1,0:T(8,128)(2,1)}, bf16[256,2048]{1,0:T(8,128)(2,1)}, u32[]{:S(2)}, u32[]{:S(2)}) collective-permute-start(bf16[256,2048]{1,0:T(8,128)(2,1)} %get-tuple-element.172.refs_1_.refs_12_), channel_id=1, source_target_pairs={{0,4},{2,6},{4,0},{6,2},{1,5},{3,7},{5,1},{7,3},{8,12},{10,14},{12... | collective-permute-start | bytes 3145736 | tf_op jit(solution)/shard_map/ppermute | solution.py:40
  188.9 29.1 %collective-permute-start.25 = (bf16[2,2,256,512]{3,2,0,1:T(8,128)(2,1)S(1)}, bf16[2,2,256,512]{3,2,0,1:T(8,128)(2,1)S(1)}, u32[]{:S(2)}, u32[]{:S(2)}) collective-permute-start(bf16[2,2,256,512]{3,2,0,1:T(8,128)(2,1)S(1)} %copy.38), channel_id=1, source_target_pairs={{0,2},{2,0},{4,6},{6,4},{1,3},{3,1},{5,7},{7,5},{8,10},{10,8},{12,... | collective-permute-start | bytes 3145736 | tf_op jit(solution)/shard_map/ppermute | solution.py:40
  198.4 21.6 %collective-permute-start.33 = (bf16[2,2,256,512]{3,2,0,1:T(8,128)(2,1)S(1)}, bf16[2,2,256,512]{3,2,0,1:T(8,128)(2,1)S(1)}, u32[]{:S(2)}, u32[]{:S(2)}) collective-permute-start(bf16[2,2,256,512]{3,2,0,1:T(8,128)(2,1)S(1)} %copy.41), channel_id=1, source_target_pairs={{0,2},{2,0},{4,6},{6,4},{1,3},{3,1},{5,7},{7,5},{8,10},{10,8},{12,... | collective-permute-start | bytes 3145736 | tf_op jit(solution)/shard_map/ppermute | solution.py:40
  199.0 23.7 %collective-permute-start.27 = (bf16[256,2048]{1,0:T(8,128)(2,1)}, bf16[256,2048]{1,0:T(8,128)(2,1)S(1)}, u32[]{:S(2)}, u32[]{:S(2)}) collective-permute-start(bf16[256,2048]{1,0:T(8,128)(2,1)} %get-tuple-element.169.refs_0_.refs_4_), channel_id=1, source_target_pairs={{0,2},{2,0},{4,6},{6,4},{1,3},{3,1},{5,7},{7,5},{8,10},{10,8},{12,... | collective-permute-start | bytes 3145736 | tf_op jit(solution)/shard_map/ppermute | solution.py:40
  199.1 24.9 %collective-permute-start.28 = (bf16[256,2048]{1,0:T(8,128)(2,1)}, bf16[256,2048]{1,0:T(8,128)(2,1)S(1)}, u32[]{:S(2)}, u32[]{:S(2)}) collective-permute-start(bf16[256,2048]{1,0:T(8,128)(2,1)} %collective-permute-done.26.refs_5_), channel_id=1, source_target_pairs={{0,2},{2,0},{4,6},{6,4},{1,3},{3,1},{5,7},{7,5},{8,10},{10,8},{12,... | collective-permute-start | bytes 3145736 | tf_op jit(solution)/shard_map/ppermute | solution.py:40
  220.0 29.5 %collective-permute-start.32 = (bf16[2,256,512]{2,1,0:T(8,128)(2,1)}, bf16[2,256,512]{2,1,0:T(8,128)(2,1)}, u32[]{:S(2)}, u32[]{:S(2)}) collective-permute-start(bf16[2,256,512]{2,1,0:T(8,128)(2,1)} %get-tuple-element.209), channel_id=1, source_target_pairs={{4,0},{6,2},{5,1},{7,3},{12,8},{14,10},{13,9},{15,11},{20,16},{22,... | collective-permute-start | bytes 1572872 | tf_op jit(solution)/shard_map/ppermute | solution.py:40
  222.7 25.5 %collective-permute-start.34 = (bf16[2,256,512]{2,1,0:T(8,128)(2,1)}, bf16[2,256,512]{2,1,0:T(8,128)(2,1)}, u32[]{:S(2)}, u32[]{:S(2)}) collective-permute-start(bf16[2,256,512]{2,1,0:T(8,128)(2,1)} %get-tuple-element.211), channel_id=1, source_target_pairs={{4,0},{6,2},{5,1},{7,3},{12,8},{14,10},{13,9},{15,11},{20,16},{22,... | collective-permute-start | bytes 1572872 | tf_op jit(solution)/shard_map/ppermute | solution.py:40
  236.7 163.7 %reduce-scatter.5.cloned.1.call-start = ((), (), s32[]{:S(2)}) async-start(), calls=%async_computation.4 | async-start | bytes 5242880 | tf_op jit(solution)/shard_map/reduce_scatter | solution.py:705
  251.6 30.3 %collective-permute-start.47 = (bf16[256,2048]{1,0:T(8,128)(2,1)S(1)}, bf16[256,2048]{1,0:T(8,128)(2,1)}, u32[]{:S(2)}, u32[]{:S(2)}) collective-permute-start(bf16[256,2048]{1,0:T(8,128)(2,1)S(1)} %pad_maximum_fusion.1.refs_1_.refs_2_.refs_20_), channel_id=1, source_target_pairs={{0,4},{2,6},{4,0},{6,2},{1,5},{3,7},{5,1},{7,3},{8,12},{10,14},{12... | collective-permute-start | bytes 3145736 | tf_op jit(solution)/shard_map/ppermute | solution.py:40
  251.7 40.5 %collective-permute-start.44 = (bf16[256,1024]{1,0:T(8,128)(2,1)}, bf16[256,1024]{1,0:T(8,128)(2,1)}, u32[]{:S(2)}, u32[]{:S(2)}) collective-permute-start(bf16[256,1024]{1,0:T(8,128)(2,1)} %get-tuple-element.190.refs_0_.refs_12_), channel_id=1, source_target_pairs={{0,4},{2,6},{4,0},{6,2},{1,5},{3,7},{5,1},{7,3},{8,12},{10,14},{12... | collective-permute-start | bytes 1572872 | tf_op jit(solution)/shard_map/ppermute | solution.py:40
  281.9 17.7 %collective-permute-start.48 = (bf16[256,2048]{1,0:T(8,128)(2,1)}, bf16[256,2048]{1,0:T(8,128)(2,1)S(1)}, u32[]{:S(2)}, u32[]{:S(2)}) collective-permute-start(bf16[256,2048]{1,0:T(8,128)(2,1)} %copy-done.3), channel_id=1, source_target_pairs={{0,2},{2,0},{4,6},{6,4},{1,3},{3,1},{5,7},{7,5},{8,10},{10,8},{12,... | collective-permute-start | bytes 3145736 | tf_op jit(solution)/shard_map/ppermute | solution.py:40
  281.9 17.7 %collective-permute-start.49 = (bf16[256,2048]{1,0:T(8,128)(2,1)}, bf16[256,2048]{1,0:T(8,128)(2,1)}, u32[]{:S(2)}, u32[]{:S(2)}) collective-permute-start(bf16[256,2048]{1,0:T(8,128)(2,1)} %collective-permute-done.47.refs_21_), channel_id=1, source_target_pairs={{0,2},{2,0},{4,6},{6,4},{1,3},{3,1},{5,7},{7,5},{8,10},{10,8},{12,... | collective-permute-start | bytes 3145736 | tf_op jit(solution)/shard_map/ppermute | solution.py:40
  283.3 14.1 %collective-permute-start.16 = (bf16[128,2048]{1,0:T(8,128)(2,1)}, bf16[128,2048]{1,0:T(8,128)(2,1)}, u32[]{:S(2)}, u32[]{:S(2)}) collective-permute-start(bf16[128,2048]{1,0:T(8,128)(2,1)} %constant_dynamic-slice_fusion.1), channel_id=1, source_target_pairs={{0,1},{1,0},{2,3},{3,2},{4,5},{5,4},{6,7},{7,6},{8,9},{9,8},{10,11... | collective-permute-start | bytes 1572872 | tf_op jit(solution)/shard_map/ppermute | solution.py:40
  (82 other events, 667.9 us)
Sparse Core Ops, SparseCore 0:
  143.5 43.3 reduce-scatter.8
  189.4 43.1 reduce-scatter.10
  236.8 79.7 reduce-scatter.6
  318.9 81.4 reduce-scatter.4

commit v3 on v2

--- a/solution.py
+++ b/solution.py
@@ -20,7 +20,8 @@
 F32 = jnp.float32
 
 
-VMEM = 56
+VMEM = 40
+ALL_VMEM = 60
 
 
 def params(limit):
@@ -56,21 +57,31 @@
     return offsets
 
 
-def gather_ctx(block, gates=()):
-    blocks = [block]
-    for hop, bit in enumerate(ctx_bits()):
-        held_back = 0 < hop <= len(gates)
-        sent = lax.optimization_barrier((blocks, gates[hop - 1]))[0] if held_back else blocks
-        blocks = blocks + [xperm(b, "ctx", bit) for b in sent]
+def gather_first(block):
+    bits = ctx_bits()
+    return [block] + ([xperm(block, "ctx", bits[0])] if bits else [])
+
+
+def gather_rest(blocks, gate):
+    blocks = lax.optimization_barrier((blocks, gate))[0]
+    for bit in ctx_bits()[1:]:
+        blocks = blocks + [xperm(b, "ctx", bit) for b in blocks]
     return blocks
 
 
-def gather_ctx_causal(block, gate):
+def gather_ctx(block, gate):
+    return gather_rest(gather_first(block), gate)
+
+
+def gather_ctx_causal(block, gate, first_gate=None):
     blocks, offsets = [block], [0]
     for bit in ctx_bits():
         fresh = []
         for b, o in zip(blocks, offsets):
-            b = after(b, gate) if o else b
+            if o:
+                b = after(b, gate)
+            elif first_gate is not None and bit > 1:
+                b = after(b, first_gate)
             fresh.append(
                 xperm(b, "ctx", bit, lambda i, o=o, bit=bit: (i ^ o) < (i ^ bit))
             )
@@ -132,11 +143,12 @@
     )(*operands)
 
 
-def kv_kernel(values, pair, weight, bias, norm, *outs):
+def kv_kernel(values, gain, shift, weight, bias, norm, *outs):
     @pl.when(pl.program_id(0) == 0)
     def _():
         unit, _ = normalized(values[...].astype(F32))
-        norm[...] = (unit * pair[0:1, :] + pair[1:2, :]).astype(BF16)
+        scale, offset = gain[...].astype(F32), shift[...].astype(F32)
+        norm[...] = (unit * scale[None, :] + offset[None, :]).astype(BF16)
 
     shifted = bias[1:2, :].astype(F32) * pl.program_id(0).astype(F32)
     total = jnp.dot(norm[...], weight[...], preferred_element_type=F32) + shifted
@@ -145,7 +157,7 @@
         out[...] = total[:, k * size : (k + 1) * size].astype(out.dtype)
 
 
-def project_kv(values, pair, weight, bias, groups):
+def project_kv(values, gain, shift, weight, bias, groups):
     rows, width = values.shape
     columns = weight.shape[2]
     size = columns // groups
@@ -155,7 +167,8 @@
         grid=(2,),
         in_specs=[
             whole,
-            pl.BlockSpec((2, width), lambda c: (0, 0)),
+            pl.BlockSpec((width,), lambda c: (0,)),
+            pl.BlockSpec((width,), lambda c: (0,)),
             pl.BlockSpec((None, width, columns), lambda c: (c + 1, 0, 0)),
             pl.BlockSpec((2, columns), lambda c: (0, 0)),
         ],
@@ -163,9 +176,9 @@
         + [pl.BlockSpec((None, rows, size), lambda c: (c, 0, 0))] * groups,
         out_shape=[jax.ShapeDtypeStruct((rows, width), BF16)]
         + [jax.ShapeDtypeStruct((2, rows, size), BF16)] * groups,
-        compiler_params=params(VMEM),
+        compiler_params=params(ALL_VMEM),
         cost_estimate=load(),
-    )(values, pair, weight, bias)
+    )(values, gain, shift, weight, bias)
 
 
 def normalized(values):
@@ -252,7 +265,7 @@
     )(values, vectors, *terms, weight, bias, grad_active)
 
 
-def more_up(norm, weight, bias, grad_active, start, size, tile, held=None):
+def more_up(norm, weight, bias, grad_active, start, size, tile, held=None, heavy=0):
     rows, width = norm.shape
     ins, outs = up_specs(width, rows, tile, start // tile, 0 if held is None else start // tile)
     in_specs = [pl.BlockSpec((rows, width), lambda i: (0, 0))] + ins
@@ -268,7 +281,7 @@
         out_shape=up_shapes(rows, size, size if held is None else held.shape[1]),
         input_output_aliases={} if held is None else {4: 1},
         compiler_params=params(VMEM),
-        cost_estimate=load(),
+        cost_estimate=load(heavy),
     )(*operands)
 
 
@@ -316,7 +329,7 @@
         in_specs=specs,
         out_specs=pl.BlockSpec((rows, tile), lambda i: (0, i)),
         out_shape=jax.ShapeDtypeStruct((rows, first * tile), BF16),
-        compiler_params=params(VMEM),
+        compiler_params=params(ALL_VMEM),
         cost_estimate=load(),
     )(*operands)
 
@@ -351,29 +364,27 @@
     )(values)
 
 
-def block_scores(place, slope, query, key, start_row, offset):
-    rows = query.shape[0]
-    raw = lax.dot_general(
-        key, query, (((1,), (1,)), ((), ())), preferred_element_type=F32
-    ) * (1.0 / math.sqrt(HD))
-    shape = raw.shape
-    key_pos = (place[0] ^ offset) * rows + lax.broadcasted_iota(jnp.int32, shape, 0)
-    query_pos = place[0] * rows + lax.broadcasted_iota(jnp.int32, shape, 1)
-    raw = raw + slope * (key_pos - query_pos).astype(F32)
-    allowed = (key_pos <= query_pos) & (key_pos >= start_row)
-    return raw, allowed
-
-
-def forward_kernel(place, slopes, query, start, *refs, offsets, first_head):
-    n = len(offsets)
+def distances(context_place, doc_start, rows):
+    query_pos = context_place * rows + jnp.arange(rows, dtype=jnp.int32)[None, :]
+    blocks = []
+    for offset in ctx_offsets():
+        key_pos = (context_place ^ offset) * rows + jnp.arange(rows, dtype=jnp.int32)[:, None]
+        allowed = (key_pos <= query_pos) & (key_pos >= doc_start)
+        blocks.append(jnp.where(allowed, (key_pos - query_pos).astype(F32), MASKED))
+    return jnp.stack(blocks)
+
+
+def block_scores(slope, query, key, distance):
+    raw = lax.dot_general(key, query, (((1,), (1,)), ((), ())), preferred_element_type=F32)
+    return raw * (1.0 / math.sqrt(HD)) + slope * distance
+
+
+def forward_kernel(slopes, query, distance, *refs, n, first_head):
     keyvals, (mixed, stats, held) = refs[:n], refs[-3:]
     slope = slopes[first_head + pl.program_id(0)]
     top = None
-    for k, offset in enumerate(offsets):
-        raw, allowed = block_scores(
-            place, slope, query[...], keyvals[k][0], start[...], offset
-        )
-        raw = jnp.where(allowed, raw, MASKED)
+    for k in range(n):
+        raw = block_scores(slope, query[...], keyvals[k][0], distance[k])
         held[k] = raw
         peak = jnp.max(raw, axis=0, keepdims=True)
         top = peak if top is None else jnp.maximum(top, peak)
@@ -395,16 +406,16 @@
     mixed[...] = result.astype(mixed.dtype)
 
 
-def attention_forward(place, slopes, query, start, keyvals, first_head, heads, held=None):
+def attention_forward(slopes, query, distance, keyvals, first_head, heads, held=None):
     rows, columns = query.shape
     extra = [] if held is None else [held]
     n = len(keyvals)
     grid_spec = pltpu.PrefetchScalarGridSpec(
-        num_scalar_prefetch=2,
+        num_scalar_prefetch=1,
         grid=(heads,),
         in_specs=[
             pl.BlockSpec((rows, HD), lambda h, *_: (0, first_head + h)),
-            pl.BlockSpec((1, rows), lambda h, *_: (0, 0)),
+            pl.BlockSpec((n, rows, rows), lambda h, *_: (0, 0, 0)),
         ]
         + [pl.BlockSpec((2, rows, HD), lambda h, *_: (0, 0, h))] * n
         + [pl.BlockSpec(memory_space=pl.ANY)] * len(extra),
@@ -415,32 +426,27 @@
         scratch_shapes=[pltpu.VMEM((n, rows, rows), F32)],
     )
     return pl.pallas_call(
-        functools.partial(forward_kernel, offsets=ctx_offsets(), first_head=first_head),
+        functools.partial(forward_kernel, n=n, first_head=first_head),
         grid_spec=grid_spec,
         out_shape=[
             jax.ShapeDtypeStruct((rows, columns), BF16),
             jax.ShapeDtypeStruct((heads, 1, rows), F32),
         ],
-        input_output_aliases={4 + n: 0} if extra else {},
+        input_output_aliases={3 + n: 0} if extra else {},
         compiler_params=params(VMEM),
         cost_estimate=load(),
-    )(place, slopes, query, start, *keyvals, *extra)
-
-
-def backward_kernel(
-    place, slopes, query, grad_mixed, start, stats, *refs, offsets, first_head
-):
-    n = len(offsets)
+    )(slopes, query, distance, *keyvals, *extra)
+
+
+def backward_kernel(slopes, query, grad_mixed, distance, stats, *refs, n, first_head):
     keyvals = refs[:n]
     grad_query, near, far, probs_held, grads_held = refs[-5:]
     slope = slopes[first_head + pl.program_id(0)]
     scale = 1.0 / math.sqrt(HD)
     delta = None
-    for k, offset in enumerate(offsets):
-        raw, allowed = block_scores(
-            place, slope, query[...], keyvals[k][0], start[...], offset
-        )
-        probs = jnp.where(allowed, jnp.exp(raw - stats[...]), 0.0)
+    for k in range(n):
+        raw = block_scores(slope, query[...], keyvals[k][0], distance[k])
+        probs = jnp.exp(raw - stats[...])
         grads = lax.dot_general(
             keyvals[k][1],
             grad_mixed[...],
@@ -452,7 +458,7 @@
         part = jnp.sum(probs * grads, axis=0, keepdims=True)
         delta = part if delta is None else delta + part
     total = None
-    for k, offset in enumerate(offsets):
+    for k in range(n):
         probs = probs_held[k]
         grad_scores = (probs * (grads_held[k] - delta)).astype(BF16)
         term = lax.dot_general(
@@ -473,7 +479,7 @@
 
 
 def attention_backward(
-    place, slopes, query, grad_mixed, start, stats, keyvals, first_head, heads, held=None,
+    slopes, query, grad_mixed, distance, stats, keyvals, first_head, heads, held=None,
     heavy=0,
 ):
     rows, columns = query.shape
@@ -482,12 +488,12 @@
     n_far = n // 2
     n_near = n - n_far
     grid_spec = pltpu.PrefetchScalarGridSpec(
-        num_scalar_prefetch=2,
+        num_scalar_prefetch=1,
         grid=(heads,),
         in_specs=[
             pl.BlockSpec((rows, HD), lambda h, *_: (0, first_head + h)),
             pl.BlockSpec((rows, HD), lambda h, *_: (0, first_head + h)),
-            pl.BlockSpec((1, rows), lambda h, *_: (0, 0)),
+            pl.BlockSpec((n, rows, rows), lambda h, *_: (0, 0, 0)),
             pl.BlockSpec((None, 1, rows), lambda h, *_: (h, 0, 0)),
         ]
         + [pl.BlockSpec((2, rows, HD), lambda h, *_: (0, 0, h))] * n
@@ -500,17 +506,17 @@
         scratch_shapes=[pltpu.VMEM((n, rows, rows), F32)] * 2,
     )
     return pl.pallas_call(
-        functools.partial(backward_kernel, offsets=ctx_offsets(), first_head=first_head),
+        functools.partial(backward_kernel, n=n, first_head=first_head),
         grid_spec=grid_spec,
         out_shape=[
             jax.ShapeDtypeStruct((rows, columns), BF16),
             jax.ShapeDtypeStruct((2, n_near, rows, heads * HD), BF16),
             jax.ShapeDtypeStruct((2, max(n_far, 1), rows, heads * HD), BF16),
         ],
-        input_output_aliases={6 + n: 0} if extra else {},
+        input_output_aliases={5 + n: 0} if extra else {},
         compiler_params=params(VMEM),
         cost_estimate=load(heavy),
-    )(place, slopes, query, grad_mixed, start, stats, *keyvals, *extra)
+    )(slopes, query, grad_mixed, distance, stats, *keyvals, *extra)
 
 
 def norm_backward(grad, unit, inverse, gain):
@@ -608,22 +614,12 @@
         (segments[0][:, None] < query_seg[None, :]).astype(jnp.int32), axis=0, keepdims=True
     )
 
+    distance = distances(context_place, doc_start, rows)
     gain_one, shift_one = first_gain.astype(F32), first_shift.astype(F32)
     gain_two, shift_two = second_gain.astype(F32), second_shift.astype(F32)
     second_vectors = jnp.stack([out_bias, second_gain, second_shift]).astype(F32)
     weight_in = in_weight.transpose(1, 0, 2)
-    first_pair = jnp.stack([first_gain, first_shift]).astype(F32)
     cot_low = cotangent[0]
-
-    order = []
-
-    def then(values):
-        values = after(values, order[-1]) if order else values
-        return values
-
-    def ran(values):
-        order.append(jax.tree.leaves(values)[0])
-        return values
 
     order = []
 
@@ -639,27 +635,26 @@
     group_heads = heads_here // groups
     group_width = group_heads * HD
     normed_first, *own = ran(
-        project_kv(residual, first_pair, weight_in, in_bias, groups)
+        project_kv(residual, first_gain, first_shift, weight_in, in_bias, groups)
     )
     query = ran(
         mm(
-            [then(normed_first)], [(weight_in, 0, 0)], trans=False, start=0, size=local_width,
+            [after(then(normed_first), distance, slopes)], [(weight_in, 0, 0)], trans=False, start=0, size=local_width,
             tile=1024, out_dtype=BF16, extras=(in_bias,), heavy=1,
         )
     )
     early_pieces = ran(spread_pieces(place, then(cot_low), normed_first, heavy=1))
     mixed, stats, keyvals = None, [], []
     for g in range(groups):
-        keyvals.append(gather_ctx_causal(own[g], query if g == 0 else order[-1]))
+        keyvals.append(
+            gather_ctx_causal(own[g], query if g == 0 else order[-1], query if g else None)
+        )
         mixed, stat = ran(
             attention_forward(
-                place, slopes, then(query), doc_start, keyvals[g], g * group_heads, group_heads,
-                mixed,
+                slopes, then(query), distance, keyvals[g], g * group_heads, group_heads, mixed,
             )
         )
         stats.append(stat)
-
-    early_left = spread_left(lax.optimization_barrier((early_pieces, stats[0]))[0])
 
     def exchanged(part):
         return [part] + [xperm(part, "tensor", k) for k in range(1, n_tensor)]
@@ -672,27 +667,30 @@
             )
         )
     )
+    out_gate = order[-1]
+    early_left = spread_left(lax.optimization_barrier((early_pieces, out_gate))[0])
+    mixed_sent = after(mixed, out_gate)
     grad_active = ran(
         mm(
-            [then(cot_low)], [down_weight], trans=False, start=0, size=local_hidden, tile=1024,
-            out_dtype=F32,
-        )
-    )
-    mixed_all = gather_ctx(mixed, [order[-1]])
+            [then(cot_low)], [down_weight], trans=False, start=0,
+            size=local_hidden, tile=1024, out_dtype=F32, heavy=2,
+        )
+    )
 
     tile = local_hidden // 8
     half_hidden = local_hidden // 2
     up_bias_row = up_bias.astype(F32)[None]
     middle, normed_second, active_near, grad_near, bias_near = ran(
         first_up(
-            residual, second_vectors, [after(then(attention[0]), early_left)] + attention[1:],
+            residual, second_vectors, [then(attention[0])] + attention[1:],
             up_weight, up_bias_row, grad_active, half_hidden, half_hidden, tile,
         )
     )
+    mixed_seen = gather_first(mixed_sent)
     active_far, grad_far, bias_far = ran(
         more_up(
-            after(then(normed_second), mixed_all), up_weight, up_bias_row, grad_active,
-            half_hidden, half_hidden, 2 * tile,
+            after(then(normed_second), early_left), up_weight, up_bias_row, grad_active,
+            half_hidden, half_hidden, 2 * tile, heavy=2,
         )
     )
 
@@ -707,7 +705,8 @@
     def grad_normed_part(side):
         part = ran(
             mm(
-                [then(grad_near), grad_far], [(up_weight, None, 0), (up_weight, None, 1)],
+                [after(then(grad_near), mixed_seen), grad_far],
+                [(up_weight, None, 0), (up_weight, None, 1)],
                 trans=True, start=side * (width // 2), size=width // 2, tile=512,
                 out_dtype=BF16,
             )
@@ -715,7 +714,7 @@
         return exchanged(part)
 
     normed_terms = [grad_normed_part(0), grad_normed_part(1)]
-    near_rights = gather_ctx(active_near, [order[-1]])
+    near_rights = gather_ctx(active_near, order[-1])
     up_pieces = ran(spread_pieces(place, then(normed_second), heavy=1))
     down_parts = [reduce_over_dp([(early_left, 0, near_rights)])]
     near_sent = after(grad_near, order[-1])
@@ -752,18 +751,20 @@
     grad_mixed = ran(
         mm(
             [then(grad_middle_low)], [out_weight], trans=False, start=0,
-            size=local_width, tile=1024, out_dtype=BF16,
+            size=local_width, tile=1024, out_dtype=BF16, heavy=1,
         )
     )
     down_parts.append(
-        reduce_over_dp([(early_left, 0, gather_ctx(active_far, [feed_gate]))], up_left)
+        reduce_over_dp([(early_left, 0, gather_ctx(active_far, feed_gate))], up_left)
     )
     far_sent = after(grad_far, order[-1])
+    mixed_all = gather_rest(mixed_seen, order[-1])
     grad_query, kv_near, kv_far = None, [], []
     for g in range(groups):
         grad_query, near, far = ran(
             attention_backward(
-                place, slopes, then(query), grad_mixed, doc_start, stats[g], keyvals[g],
+                slopes, after(then(query), mixed_all if g else []), grad_mixed, distance, stats[g],
+                keyvals[g],
                 g * group_heads, group_heads, grad_query, heavy=2 if g == 0 else 0,
             )
         )
@@ -772,8 +773,15 @@
     kv_received = [xperm(far, "ctx", 1) if n_ctx > 1 else None for far in kv_far]
     kv_near = after(kv_near, order[-1])
 
-    near_all = gather_ctx(near_sent, [order[-1]])
-    far_all = gather_ctx(far_sent, [order[-1]])
+    near_all = gather_ctx(near_sent, order[-1])
+    partial = []
+    for near, received in zip(kv_near, kv_received):
+        blocks = [near[:, k].astype(F32) for k in range(near.shape[1])]
+        if n_ctx > 1:
+            blocks = [block + received[:, k].astype(F32) for k, block in enumerate(blocks)]
+        partial.append(blocks)
+    sent = [block.astype(BF16) for blocks in partial for block in blocks[len(blocks) // 2 :]]
+    far_all = gather_ctx(far_sent, sent)
     up_part = reduce_over_dp([(up_left, 0, near_all), (up_left, 0, far_all)])
     up_gate = order[-1]
     late_pieces = ran(spread_pieces(place, then(grad_middle_low), heavy=2))
@@ -781,24 +789,20 @@
     outputs = (mine(middle) + tensor_scatter(feed) + down_bias.astype(F32)).astype(BF16)
 
     grad_keys, grad_values = [], []
-    for near, received in zip(kv_near, kv_received):
-        blocks = [near[:, k] for k in range(near.shape[1])]
-        if n_ctx > 1:
+    for g, blocks in enumerate(partial):
+        send_gate = up_gate if g else []
+        for bit in reversed(ctx_bits()[:-1]):
+            half = len(blocks) // 2
+            got = [
+                xperm(
+                    after(block.astype(BF16), send_gate), "ctx", bit, lambda i, bit=bit: i > i ^ bit
+                )
+                for block in blocks[half:]
+            ]
             blocks = [
-                (block.astype(F32) + received[:, k].astype(F32))
-                for k, block in enumerate(blocks)
+                after(block, order[-1]) + term.astype(F32)
+                for block, term in zip(blocks[:half], got)
             ]
-            bits = ctx_bits()[:-1]
-            for bit in reversed(bits):
-                half = len(blocks) // 2
-                got = [
-                    xperm(sent.astype(BF16), "ctx", bit, lambda i, bit=bit: i > i ^ bit)
-                    for sent in blocks[half:]
-                ]
-                blocks = [
-                    after(block, order[-1]) + term.astype(F32)
-                    for block, term in zip(blocks[:half], got)
-                ]
         final = blocks[0].astype(BF16)
         grad_keys.append(final[0])
         grad_values.append(final[1])
@@ -811,8 +815,8 @@
             tile=512, out_dtype=BF16, heavy=1,
         )
     )
-    query_all = gather_ctx(after(grad_query, up_gate), [order[-1]])
-    keyvals_all = gather_ctx(grad_keyvals, [order[-1]])
+    query_all = gather_ctx(after(grad_query, up_gate), order[-1])
+    keyvals_all = gather_ctx(grad_keyvals, order[-1])
     joint_part = reduce_over_dp(
         [(late_left, 0, mixed_all), (early_left, 1, query_all), (early_left, 1, keyvals_all)],
         outputs,

time: 412 us -> 401 us (0.973); the launches traced: 410 us -> 395 us
  Pallas kernels: 155 us -> 133 us
  starting transfers between devices: 48.1 us -> 57.5 us
  local copies, waits for them, and re-layouts: 22.8 us -> 29.2 us
  waiting for transfers between devices: 133 us -> 128 us
  other arithmetic: 36.7 us -> 32.1 us
    pallas_call x8, Pallas kernels: 55 us -> 44.4 us  [mm(): pl.pallas_call(functools.partial(mm_kernel, n_pairs=len(lefts), trans=tra...]
    unnamed x129 -> x157, local copies, waits for them, and re-layouts: 16.9 us -> 27.1 us
    ppermute x50, starting transfers between devices: 47.5 us -> 57.2 us  [xperm(): return lax.ppermute(values, axis, pairs)]
    reduce_scatter x4, waiting for transfers between devices: 23.9 us -> 18.1 us  [reduce_over_dp(): return lax.psum_scatter(whole, 'dp', scatter_dimension=0, tiled=True)]
    pallas_call x3, Pallas kernels: 10.4 us -> 5.49 us  [spread_pieces(): pl.pallas_call(functools.partial(spread_kernel, n_values=len(values), n_c...]
  transfers between devices with their start and end apart: 54 -> 54, of which waited for: 19 -> 18; matrix products, arithmetic and copies ran while one was open for 11% -> 10% of each run, Pallas kernels for 33% -> 29%
where the time goes in v3:
time: 401 us; the launch traced here: 395 us
  Pallas kernels  133 us (33%)
  waiting for transfers between devices  128 us (32%)
  starting transfers between devices  57.5 us (14%)
  other arithmetic  32.1 us (8%)
  local copies, waits for them, and re-layouts  29.2 us (7%)
  between operations  15.1 us (4%)
    ppermute x50, waiting for transfers between devices, xperm(): return lax.ppermute(values, axis, pairs)  109 us
    ppermute x50, starting transfers between devices, xperm(): return lax.ppermute(values, axis, pairs)  57.2 us
    pallas_call x8, Pallas kernels, mm(): pl.pallas_call(functools.partial(mm_kernel, n_pairs=len(lefts), trans=tra...  44.4 us
    pallas_call x4, Pallas kernels, weight_grad(): pl.pallas_call(functools.partial(weight_grad_kernel, blocks=blocks, n=n),...  32.1 us
    unnamed x157, local copies, waits for them, and re-layouts  27.1 us
    reduce_scatter x4, waiting for transfers between devices, reduce_over_dp(): return lax.psum_scatter(whole, 'dp', scatter_dimension=0, tiled=True)  18.1 us
    pallas_call x2, Pallas kernels, attention_backward(): pl.pallas_call(functools.partial(backward_kernel, n=n, first_head=first_h...  14 us
    pallas_call x2, Pallas kernels, attention_forward(): pl.pallas_call(functools.partial(forward_kernel, n=n, first_head=first_he...  12.3 us
  transfers between devices with their start and end apart: 54, of which 18 were waited for; matrix products, arithmetic and copies ran while one was open for 10% of the time, Pallas kernels for 29%

profile of v3, /device:TPU:0, one launch (start us, length us, event | category | flops | bytes accessed | tf_op | source)
XLA Modules:
  0.0 394.7 jit_solution(18227522250915750633)
XLA Ops:
  7.2 6.5 %shard_map.254 = (bf16[256,2048]{1,0:T(8,128)(2,1)}, bf16[2,256,512]{2,1,0:T(8,128)(2,1)}, bf16[2,256,512]{2,1,0:T(8,128)(2,1)}) custom-call(bf16[256,2048]{1,0:T(8,128)(2,1)} %bitcast.100, bf16[2048]{0:T(1024)(128)(2,1)} %gain.1, bf16[2048]{0:T(1024)(128)(2,1)} %shift.1, bf16[3,2048,1024]{2,1,0:T(8,128)(2,1)} %bitcast.95, bf16[2,1024]{1,0:T(2,128)(2,1)} %refs_2_.4), custom_call_target="tpu_custom_call" | custom-call | tf_op jit(solution)/shard_map/pallas_call | solution.py:165
  17.1 5.1 %collective-permute-start = (bf16[2,256,512]{2,1,0:T(8,128)(2,1)}, bf16[2,256,512]{2,1,0:T(8,128)(2,1)}, u32[]{:S(2)}, u32[]{:S(2)}) collective-permute-start(bf16[2,256,512]{2,1,0:T(8,128)(2,1)} %get-tuple-element.117.refs_0_), channel_id=1, source_target_pairs={{0,4},{2,6},{1,5},{3,7},{8,12},{10,14},{9,13},{11,15},{16,20},{18,... | collective-permute-start | bytes 1572872 | tf_op jit(solution)/shard_map/ppermute | solution.py:41
  25.5 4.6 %copy-done = bf16[2048,3,1024]{2,0,1:T(8,128)(2,1)S(1)} copy-done((bf16[2048,3,1024]{2,0,1:T(8,128)(2,1)S(1)}, bf16[2048,3,1024]{2,0,1:T(8,128)(2,1)}, u32[]{:S(2)}) %copy-start) | copy-done | bytes 12582936
  38.9 5.9 %shard_map.257 = (bf16[256,1024]{1,0:T(8,128)(2,1)}, f32[4,1,256]{2,1,0:T(1,128)S(1)}) custom-call(f32[8]{0:T(128)S(1)} %multiply_exponential_fusion.slopes, bf16[256,1024]{1,0:T(8,128)(2,1)S(1)} %shard_map.255.query, f32[4,256,256]{2,1,0:T(8,128)S(1)} %pad_maximum_fusion.1.distance, bf16[2,256,512]{2,1,0:T(8,128)(2,1)S(1)} %copy-done.30, ...), custom_call_target="tpu_custom_call" | custom-call | tf_op jit(solution)/shard_map/pallas_call | solution.py:428
  46.7 6.4 %shard_map.258 = (bf16[256,1024]{1,0:T(8,128)(2,1)}, f32[4,1,256]{2,1,0:T(1,128)S(1)}) custom-call(f32[8]{0:T(128)S(1)} %multiply_exponential_fusion.slopes, bf16[256,1024]{1,0:T(8,128)(2,1)S(1)} %shard_map.255.query, f32[4,256,256]{2,1,0:T(8,128)S(1)} %pad_maximum_fusion.1.distance, ...), custom_call_target="tpu_custom_call", output_to_operand_aliasing={{0}: (7, {})} | custom-call | tf_op jit(solution)/shard_map/pallas_call | solution.py:428
  58.0 4.1 %collective-permute-start.7 = (bf16[1024,256]{1,0:T(8,128)(2,1)}, bf16[1024,256]{1,0:T(8,128)(2,1)}, u32[]{:S(2)}, u32[]{:S(2)}) collective-permute-start(bf16[1024,256]{1,0:T(8,128)(2,1)} %get-tuple-element.137), channel_id=1, source_target_pairs={{0,4},{2,6},{4,0},{6,2},{1,5},{3,7},{5,1},{7,3},{8,12},{10,14},{12... | collective-permute-start | bytes 1572872 | tf_op jit(solution)/shard_map/ppermute | solution.py:41
  64.2 8.6 %shard_map.260.refs_6_.grad_active = f32[256,4096]{1,0:T(8,128)S(1)} custom-call(bf16[256,2048]{1,0:T(8,128)(2,1)S(1)} %bitcast.103, bf16[2048,4096]{1,0:T(8,128)(2,1)} %refs_3_.5), custom_call_target="tpu_custom_call" | custom-call | flops 999999995904 | bytes 10000000 | tf_op jit(solution)/shard_map/pallas_call | solution.py:135
  72.9 6.5 %collective-permute-done.6.refs_3_ = bf16[256,2048]{1,0:T(8,128)(2,1)} collective-permute-done((bf16[256,2048]{1,0:T(8,128)(2,1)}, bf16[256,2048]{1,0:T(8,128)(2,1)}, u32[]{:S(2)}, u32[]{:S(2)}) %collective-permute-start.6) | collective-permute-done | bytes 1048608 | tf_op jit(solution)/shard_map/ppermute | solution.py:41
  79.4 9.4 %shard_map.261 = (f32[256,2048]{1,0:T(8,128)S(1)}, bf16[256,2048]{1,0:T(8,128)(2,1)S(1)}, bf16[256,2048]{1,0:T(8,128)(2,1)}, bf16[256,2048]{1,0:T(8,128)(2,1)}, f32[1,2048]{1,0:T(1,128)S(1)}) custom-call(bf16[256,2048]{1,0:T(8,128)(2,1)S(1)} %bitcast.101, f32[3,2048]{1,0:T(4,128)S(1)} %maximum_convert_fusion.1.refs_1_, ...), custom_call_target="tpu_custom_call" | custom-call | tf_op jit(solution)/shard_map/pallas_call | solution.py:253
  88.8 6.7 %collective-permute-start.11 = (bf16[256,2048]{1,0:T(8,128)(2,1)}, bf16[256,2048]{1,0:T(8,128)(2,1)}, u32[]{:S(2)}, u32[]{:S(2)}) collective-permute-start(bf16[256,2048]{1,0:T(8,128)(2,1)} %get-tuple-element.153.refs_4_.refs_0_), channel_id=1, source_target_pairs={{0,4},{2,6},{4,0},{6,2},{1,5},{3,7},{5,1},{7,3},{8,12},{10,14},{12... | collective-permute-start | bytes 3145736 | tf_op jit(solution)/shard_map/ppermute | solution.py:41
  95.6 7.0 %shard_map.262 = (bf16[256,2048]{1,0:T(8,128)(2,1)}, bf16[256,2048]{1,0:T(8,128)(2,1)S(1)}, f32[1,2048]{1,0:T(1,128)S(1)}) custom-call(bf16[256,2048]{1,0:T(8,128)(2,1)S(1)} %get-tuple-element.148.norm.refs_0_, bf16[2048,4096]{1,0:T(8,128)(2,1)} %refs_3_.4, f32[1,4096]{1,0:T(1,128)S(1)} %bitcast.107, f32[256,4096]{1,0:T(8,128)S(1)} %shard_map.260.refs_6_.grad_active), custom_call_target="tpu_custom_call" | custom-call | flops 999999995904 | bytes 10000000 | tf_op jit(solution)/shard_map/pallas_call | solution.py:276
  102.6 6.8 %shard_map.263 = bf16[256,1024]{1,0:T(8,128)(2,1)} custom-call(bf16[256,2048]{1,0:T(8,128)(2,1)} %get-tuple-element.180.refs_0_.refs_4_, bf16[256,2048]{1,0:T(8,128)(2,1)S(1)} %get-tuple-element.185.refs_1_.refs_12_, bf16[2048,4096]{1,0:T(8,128)(2,1)} %refs_3_.4, bf16[2048,4096]{1,0:T(8,128)(2,1)} %refs_3_.4), custom_call_target="tpu_custom_call" | custom-call | tf_op jit(solution)/shard_map/pallas_call | solution.py:135
  109.3 6.4 %shard_map.264 = bf16[256,1024]{1,0:T(8,128)(2,1)} custom-call(bf16[256,2048]{1,0:T(8,128)(2,1)} %get-tuple-element.180.refs_0_.refs_4_, bf16[256,2048]{1,0:T(8,128)(2,1)S(1)} %get-tuple-element.185.refs_1_.refs_12_, bf16[2048,4096]{1,0:T(8,128)(2,1)} %refs_3_.4, bf16[2048,4096]{1,0:T(8,128)(2,1)} %refs_3_.4), custom_call_target="tpu_custom_call" | custom-call | tf_op jit(solution)/shard_map/pallas_call | solution.py:135
  126.1 5.6 %shard_map.266 = bf16[512,2048]{1,0:T(8,128)(2,1)} custom-call(bf16[1024,256]{1,0:T(8,128)(2,1)} %copy-done.11, bf16[1024,256]{1,0:T(8,128)(2,1)} %collective-permute-done.7.refs_1_.refs_9_.refs_17_, bf16[1024,256]{1,0:T(8,128)(2,1)} %collective-permute-done.8.refs_2_.refs_10_.refs_18_, bf16[1024,256]{1,0:T(8,128)(2,1)} %collective-permute-done.9.refs_3_.refs_11_.refs_19_, ...), custom_call_target="tpu_custom_call" | custom-call | tf_op jit(solution)/shard_map/pallas_call | solution.py:326
  131.9 9.5 %shard_map.267 = bf16[256,2048]{1,0:T(8,128)(2,1)S(1)} custom-call(bf16[256,2048]{1,0:T(8,128)(2,1)} %get-tuple-element.153.refs_4_.refs_0_, bf16[256,2048]{1,0:T(8,128)(2,1)} %get-tuple-element.163.refs_1_.refs_4_, bf16[2048,4096]{1,0:T(8,128)(2,1)} %refs_3_.5, bf16[2048,4096]{1,0:T(8,128)(2,1)} %refs_3_.5), custom_call_target="tpu_custom_call" | custom-call | flops 999999995904 | bytes 10000000 | tf_op jit(solution)/shard_map/pallas_call | solution.py:135
  157.4 5.7 %shard_map.269 = bf16[512,2048]{1,0:T(8,128)(2,1)} custom-call(bf16[1024,256]{1,0:T(8,128)(2,1)} %copy-done.11, bf16[1024,256]{1,0:T(8,128)(2,1)} %collective-permute-done.7.refs_1_.refs_9_.refs_17_, bf16[1024,256]{1,0:T(8,128)(2,1)} %collective-permute-done.8.refs_2_.refs_10_.refs_18_, bf16[1024,256]{1,0:T(8,128)(2,1)} %collective-permute-done.9.refs_3_.refs_11_.refs_19_, ...), custom_call_target="tpu_custom_call" | custom-call | tf_op jit(solution)/shard_map/pallas_call | solution.py:326
  165.7 7.0 %shard_map.270 = (bf16[256,1024]{1,0:T(8,128)(2,1)}, bf16[2,2,256,512]{3,2,1,0:T(8,128)(2,1)S(1)}, bf16[2,2,256,512]{3,2,1,0:T(8,128)(2,1)S(1)}) custom-call(f32[8]{0:T(128)S(1)} %copy-done.39, bf16[256,1024]{1,0:T(8,128)(2,1)S(1)} %copy-done.15, bf16[256,1024]{1,0:T(8,128)(2,1)S(1)} %copy-done.35, f32[4,256,256]{2,1,0:T(8,128)S(1)} %copy-done.6, ...), custom_call_target="tpu_custom_call" | custom-call | flops 999999995904 | bytes 10000000 | tf_op jit(solution)/shard_map/pallas_call | solution.py:508
  173.8 7.0 %shard_map.271 = (bf16[256,1024]{1,0:T(8,128)(2,1)}, bf16[2,2,256,512]{3,2,1,0:T(8,128)(2,1)S(1)}, bf16[2,2,256,512]{3,2,1,0:T(8,128)(2,1)S(1)}) custom-call(f32[8]{0:T(128)S(1)} %copy-done.39, bf16[256,1024]{1,0:T(8,128)(2,1)S(1)} %copy-done.15, bf16[256,1024]{1,0:T(8,128)(2,1)S(1)} %copy-done.36, ...), custom_call_target="tpu_custom_call", output_to_operand_aliasing={{0}: (9, {})} | custom-call | tf_op jit(solution)/shard_map/pallas_call | solution.py:508
  186.1 21.0 %collective-permute-done.29.refs_13_ = bf16[256,2048]{1,0:T(8,128)(2,1)S(1)} collective-permute-done((bf16[256,2048]{1,0:T(8,128)(2,1)S(1)}, bf16[256,2048]{1,0:T(8,128)(2,1)S(1)}, u32[]{:S(2)}, u32[]{:S(2)}) %collective-permute-start.29) | collective-permute-done | bytes 1048608 | tf_op jit(solution)/shard_map/ppermute | solution.py:41
  212.3 10.3 %shard_map.272 = bf16[512,4096]{1,0:T(8,128)(2,1)} custom-call(bf16[512,256]{1,0:T(8,128)(2,1)} %copy-done.24, bf16[512,256]{1,0:T(8,128)(2,1)} %collective-permute-done.17.refs_1_.refs_9_, bf16[512,256]{1,0:T(8,128)(2,1)} %collective-permute-done.18.refs_2_.refs_10_, bf16[512,256]{1,0:T(8,128)(2,1)} %copy-done.57, ...), custom_call_target="tpu_custom_call" | custom-call | tf_op jit(solution)/shard_map/pallas_call | solution.py:326
  231.0 8.8 %collective-permute-done.34 = bf16[2,256,512]{2,1,0:T(8,128)(2,1)} collective-permute-done((bf16[2,256,512]{2,1,0:T(8,128)(2,1)}, bf16[2,256,512]{2,1,0:T(8,128)(2,1)}, u32[]{:S(2)}, u32[]{:S(2)}) %collective-permute-start.34) | collective-permute-done | bytes 524320 | tf_op jit(solution)/shard_map/ppermute | solution.py:41
  245.4 4.0 %collective-permute-done.37.refs_3_ = bf16[512,256]{1,0:T(8,128)(2,1)} collective-permute-done((bf16[512,256]{1,0:T(8,128)(2,1)S(1)}, bf16[512,256]{1,0:T(8,128)(2,1)}, u32[]{:S(2)}, u32[]{:S(2)}) %collective-permute-start.37) | collective-permute-done | bytes 262176 | tf_op jit(solution)/shard_map/ppermute | solution.py:41
  249.4 7.2 %shard_map.274 = bf16[256,2048]{1,0:T(8,128)(2,1)S(1)} custom-call(bf16[256,1024]{1,0:T(8,128)(2,1)} %get-tuple-element.202.refs_0_.refs_12_, bf16[256,2048]{1,0:T(8,128)(2,1)S(1)} %pad_maximum_fusion.2.refs_1_.refs_2_.refs_20_, bf16[256,2048]{1,0:T(8,128)(2,1)S(1)} %pad_maximum_fusion.2.refs_1_.refs_2_.refs_20_, bf16[3,2048,1024]{2,1,0:T(8,128)(2,1)} %bitcast.96, ...), custom_call_target="tpu_custom_call" | custom-call | flops 10000000000 | bytes 10000000 | tf_op jit(solution)/shard_map/pallas_call | solution.py:135
  257.7 15.9 %collective-permute-done.47.refs_21_ = bf16[256,2048]{1,0:T(8,128)(2,1)} collective-permute-done((bf16[256,2048]{1,0:T(8,128)(2,1)S(1)}, bf16[256,2048]{1,0:T(8,128)(2,1)}, u32[]{:S(2)}, u32[]{:S(2)}) %collective-permute-start.47) | collective-permute-done | bytes 1048608 | tf_op jit(solution)/shard_map/ppermute | solution.py:41
  276.4 7.6 %collective-permute-done.44.refs_13_ = bf16[256,1024]{1,0:T(8,128)(2,1)} collective-permute-done((bf16[256,1024]{1,0:T(8,128)(2,1)}, bf16[256,1024]{1,0:T(8,128)(2,1)}, u32[]{:S(2)}, u32[]{:S(2)}) %collective-permute-start.44) | collective-permute-done | bytes 524320 | tf_op jit(solution)/shard_map/ppermute | solution.py:41
  284.5 4.6 %collective-permute-done.14 = bf16[128,2048]{1,0:T(8,128)(2,1)} collective-permute-done((bf16[128,2048]{1,0:T(8,128)(2,1)}, bf16[128,2048]{1,0:T(8,128)(2,1)}, u32[]{:S(2)}, u32[]{:S(2)}) %collective-permute-start.14) | collective-permute-done | bytes 524320 | tf_op jit(solution)/shard_map/ppermute | solution.py:41
  291.3 10.6 %shard_map.275 = bf16[512,4096]{1,0:T(8,128)(2,1)} custom-call(bf16[512,256]{1,0:T(8,128)(2,1)} %copy-done.37, bf16[512,256]{1,0:T(8,128)(2,1)} %collective-permute-done.35.refs_1_, bf16[512,256]{1,0:T(8,128)(2,1)} %collective-permute-done.36.refs_2_, bf16[512,256]{1,0:T(8,128)(2,1)} %collective-permute-done.37.refs_3_, ...), custom_call_target="tpu_custom_call" | custom-call | tf_op jit(solution)/shard_map/pallas_call | solution.py:326
  311.4 6.1 %collective-permute-done.38 = bf16[128,2048]{1,0:T(8,128)(2,1)} collective-permute-done((bf16[128,2048]{1,0:T(8,128)(2,1)}, bf16[128,2048]{1,0:T(8,128)(2,1)}, u32[]{:S(2)}, u32[]{:S(2)}) %collective-permute-start.38) | collective-permute-done | bytes 524320 | tf_op jit(solution)/shard_map/ppermute | solution.py:41
  327.9 4.8 %collective-permute-done.41 = f32[18,1024]{1,0:T(8,128)S(1)} collective-permute-done((f32[18,1024]{1,0:T(8,128)S(1)}, f32[18,1024]{1,0:T(8,128)S(1)}, u32[]{:S(2)}, u32[]{:S(2)}) %collective-permute-start.41) | collective-permute-done | bytes 73760 | tf_op jit(solution)/shard_map/ppermute | solution.py:41
  334.4 8.6 %collective-permute-done.42 = f32[18,1024]{1,0:T(8,128)S(1)} collective-permute-done((f32[18,1024]{1,0:T(8,128)S(1)}, f32[18,1024]{1,0:T(8,128)S(1)}, u32[]{:S(2)}, u32[]{:S(2)}) %collective-permute-start.42) | collective-permute-done | bytes 73760 | tf_op jit(solution)/shard_map/ppermute | solution.py:41
  344.8 11.5 %collective-permute-done.43 = f32[18,1024]{1,0:T(8,128)S(1)} collective-permute-done((f32[18,1024]{1,0:T(8,128)S(1)}, f32[18,1024]{1,0:T(8,128)S(1)}, u32[]{:S(2)}, u32[]{:S(2)}) %collective-permute-start.43) | collective-permute-done | bytes 73760 | tf_op jit(solution)/shard_map/ppermute | solution.py:41
  366.6 18.1 %reduce-scatter.5.cloned.1.call-done.values = bf16[128,4096]{1,0:T(8,128)(2,1)} async-done(((bf16[512,4096]{1,0:T(8,128)(2,1)}), bf16[128,4096]{1,0:T(8,128)(2,1)}) %reduce-scatter.5.cloned.1.call-update) | async-done | bytes 1048592 | tf_op jit(solution)/shard_map/reduce_scatter | solution.py:703
  (328 shorter events, 122.0 us)
Async XLA Ops:
  7.2 353.9 %reduce-scatter.9.cloned.1.call-start = ((), (), s32[]{:S(2)}) async-start(), calls=%async_computation.6 | async-start | bytes 2621440 | tf_op jit(solution)/shard_map/reduce_scatter | solution.py:703
  13.8 25.1 %collective-permute-start.1 = (bf16[2,256,512]{2,1,0:T(8,128)(2,1)}, bf16[2,256,512]{2,1,0:T(8,128)(2,1)}, u32[]{:S(2)}, u32[]{:S(2)}) collective-permute-start(bf16[2,256,512]{2,1,0:T(8,128)(2,1)} %get-tuple-element.117.refs_0_), channel_id=1, source_target_pairs={{0,2},{4,6},{1,3},{5,7},{8,10},{12,14},{9,11},{13,15},{16,18},{20,... | collective-permute-start | bytes 1572872 | tf_op jit(solution)/shard_map/ppermute | solution.py:41
  17.1 16.6 %collective-permute-start = (bf16[2,256,512]{2,1,0:T(8,128)(2,1)}, bf16[2,256,512]{2,1,0:T(8,128)(2,1)}, u32[]{:S(2)}, u32[]{:S(2)}) collective-permute-start(bf16[2,256,512]{2,1,0:T(8,128)(2,1)} %get-tuple-element.117.refs_0_), channel_id=1, source_target_pairs={{0,4},{2,6},{1,5},{3,7},{8,12},{10,14},{9,13},{11,15},{16,20},{18,... | collective-permute-start | bytes 1572872 | tf_op jit(solution)/shard_map/ppermute | solution.py:41
  22.1 24.5 %collective-permute-start.4 = (bf16[2,256,512]{2,1,0:T(8,128)(2,1)}, bf16[2,256,512]{2,1,0:T(8,128)(2,1)}, u32[]{:S(2)}, u32[]{:S(2)}) collective-permute-start(bf16[2,256,512]{2,1,0:T(8,128)(2,1)} %get-tuple-element.122.refs_0_), channel_id=1, source_target_pairs={{0,2},{4,6},{1,3},{5,7},{8,10},{12,14},{9,11},{13,15},{16,18},{20,... | collective-permute-start | bytes 1572872 | tf_op jit(solution)/shard_map/ppermute | solution.py:41
  56.5 22.9 %collective-permute-start.6 = (bf16[256,2048]{1,0:T(8,128)(2,1)}, bf16[256,2048]{1,0:T(8,128)(2,1)}, u32[]{:S(2)}, u32[]{:S(2)}) collective-permute-start(bf16[256,2048]{1,0:T(8,128)(2,1)} %shard_map.259.refs_2_), channel_id=1, source_target_pairs={{0,1},{1,0},{2,3},{3,2},{4,5},{5,4},{6,7},{7,6},{8,9},{9,8},{10,11... | collective-permute-start | bytes 3145736 | tf_op jit(solution)/shard_map/ppermute | solution.py:41
  58.0 30.8 %collective-permute-start.7 = (bf16[1024,256]{1,0:T(8,128)(2,1)}, bf16[1024,256]{1,0:T(8,128)(2,1)}, u32[]{:S(2)}, u32[]{:S(2)}) collective-permute-start(bf16[1024,256]{1,0:T(8,128)(2,1)} %get-tuple-element.137), channel_id=1, source_target_pairs={{0,4},{2,6},{4,0},{6,2},{1,5},{3,7},{5,1},{7,3},{8,12},{10,14},{12... | collective-permute-start | bytes 1572872 | tf_op jit(solution)/shard_map/ppermute | solution.py:41
  62.1 26.7 %collective-permute-start.8 = (bf16[1024,256]{1,0:T(8,128)(2,1)}, bf16[1024,256]{1,0:T(8,128)(2,1)}, u32[]{:S(2)}, u32[]{:S(2)}) collective-permute-start(bf16[1024,256]{1,0:T(8,128)(2,1)} %get-tuple-element.138), channel_id=1, source_target_pairs={{0,2},{2,0},{4,6},{6,4},{1,3},{3,1},{5,7},{7,5},{8,10},{10,8},{12,... | collective-permute-start | bytes 1572872 | tf_op jit(solution)/shard_map/ppermute | solution.py:41
  62.1 26.7 %collective-permute-start.9 = (bf16[1024,256]{1,0:T(8,128)(2,1)}, bf16[1024,256]{1,0:T(8,128)(2,1)}, u32[]{:S(2)}, u32[]{:S(2)}) collective-permute-start(bf16[1024,256]{1,0:T(8,128)(2,1)} %get-tuple-element.139), channel_id=1, source_target_pairs={{0,6},{2,4},{4,2},{6,0},{1,7},{3,5},{5,3},{7,1},{8,14},{10,12},{12... | collective-permute-start | bytes 1572872 | tf_op jit(solution)/shard_map/ppermute | solution.py:41
  62.2 40.3 %collective-permute-start.10 = (bf16[256,1024]{1,0:T(8,128)(2,1)}, bf16[256,1024]{1,0:T(8,128)(2,1)}, u32[]{:S(2)}, u32[]{:S(2)}) collective-permute-start(bf16[256,1024]{1,0:T(8,128)(2,1)} %get-tuple-element.169.refs_0_.refs_4_), channel_id=1, source_target_pairs={{0,4},{2,6},{4,0},{6,2},{1,5},{3,7},{5,1},{7,3},{8,12},{10,14},{12... | collective-permute-start | bytes 1572872 | tf_op jit(solution)/shard_map/ppermute | solution.py:41
  88.8 30.5 %collective-permute-start.11 = (bf16[256,2048]{1,0:T(8,128)(2,1)}, bf16[256,2048]{1,0:T(8,128)(2,1)}, u32[]{:S(2)}, u32[]{:S(2)}) collective-permute-start(bf16[256,2048]{1,0:T(8,128)(2,1)} %get-tuple-element.153.refs_4_.refs_0_), channel_id=1, source_target_pairs={{0,4},{2,6},{4,0},{6,2},{1,5},{3,7},{5,1},{7,3},{8,12},{10,14},{12... | collective-permute-start | bytes 3145736 | tf_op jit(solution)/shard_map/ppermute | solution.py:41
  115.7 28.5 %collective-permute-start.16 = (bf16[256,1024]{1,0:T(8,128)(2,1)}, bf16[256,1024]{1,0:T(8,128)(2,1)}, u32[]{:S(2)}, u32[]{:S(2)}) collective-permute-start(bf16[256,1024]{1,0:T(8,128)(2,1)} %shard_map.264), channel_id=1, source_target_pairs={{0,1},{1,0},{2,3},{3,2},{4,5},{5,4},{6,7},{7,6},{8,9},{9,8},{10,11... | collective-permute-start | bytes 1572872 | tf_op jit(solution)/shard_map/ppermute | solution.py:41
  117.2 29.2 %collective-permute-start.15 = (bf16[256,1024]{1,0:T(8,128)(2,1)}, bf16[256,1024]{1,0:T(8,128)(2,1)}, u32[]{:S(2)}, u32[]{:S(2)}) collective-permute-start(bf16[256,1024]{1,0:T(8,128)(2,1)} %shard_map.263), channel_id=1, source_target_pairs={{0,1},{1,0},{2,3},{3,2},{4,5},{5,4},{6,7},{7,6},{8,9},{9,8},{10,11... | collective-permute-start | bytes 1572872 | tf_op jit(solution)/shard_map/ppermute | solution.py:41
  117.8 26.4 %collective-permute-start.20 = (bf16[256,2048]{1,0:T(8,128)(2,1)}, bf16[256,2048]{1,0:T(8,128)(2,1)}, u32[]{:S(2)}, u32[]{:S(2)}) collective-permute-start(bf16[256,2048]{1,0:T(8,128)(2,1)} %get-tuple-element.163.refs_1_.refs_4_), channel_id=1, source_target_pairs={{0,4},{2,6},{4,0},{6,2},{1,5},{3,7},{5,1},{7,3},{8,12},{10,14},{12... | collective-permute-start | bytes 3145736 | tf_op jit(solution)/shard_map/ppermute | solution.py:41
  123.6 31.4 %collective-permute-start.17 = (bf16[512,256]{1,0:T(8,128)(2,1)}, bf16[512,256]{1,0:T(8,128)(2,1)}, u32[]{:S(2)}, u32[]{:S(2)}) collective-permute-start(bf16[512,256]{1,0:T(8,128)(2,1)} %get-tuple-element.159), channel_id=1, source_target_pairs={{0,4},{2,6},{4,0},{6,2},{1,5},{3,7},{5,1},{7,3},{8,12},{10,14},{12... | collective-permute-start | bytes 786440 | tf_op jit(solution)/shard_map/ppermute | solution.py:41
  126.1 28.9 %collective-permute-start.18 = (bf16[512,256]{1,0:T(8,128)(2,1)}, bf16[512,256]{1,0:T(8,128)(2,1)}, u32[]{:S(2)}, u32[]{:S(2)}) collective-permute-start(bf16[512,256]{1,0:T(8,128)(2,1)} %get-tuple-element.160), channel_id=1, source_target_pairs={{0,2},{2,0},{4,6},{6,4},{1,3},{3,1},{5,7},{7,5},{8,10},{10,8},{12,... | collective-permute-start | bytes 786440 | tf_op jit(solution)/shard_map/ppermute | solution.py:41
  131.7 229.4 %reduce-scatter.11.cloned.1.call-start = ((), (), s32[]{:S(2)}) async-start(), calls=%async_computation.7 | async-start | bytes 2621440 | tf_op jit(solution)/shard_map/reduce_scatter | solution.py:703
  155.0 27.7 %collective-permute-start.26 = (bf16[256,2048]{1,0:T(8,128)(2,1)}, bf16[256,2048]{1,0:T(8,128)(2,1)}, u32[]{:S(2)}, u32[]{:S(2)}) collective-permute-start(bf16[256,2048]{1,0:T(8,128)(2,1)} %get-tuple-element.180.refs_0_.refs_4_), channel_id=1, source_target_pairs={{0,4},{2,6},{4,0},{6,2},{1,5},{3,7},{5,1},{7,3},{8,12},{10,14},{12... | collective-permute-start | bytes 3145736 | tf_op jit(solution)/shard_map/ppermute | solution.py:41
  163.2 200.7 %reduce-scatter.7.cloned.1.call-start = ((), (), s32[]{:S(2)}) async-start(), calls=%async_computation.5 | async-start | bytes 5242880 | tf_op jit(solution)/shard_map/reduce_scatter | solution.py:703
  182.0 25.0 %collective-permute-start.29 = (bf16[256,2048]{1,0:T(8,128)(2,1)S(1)}, bf16[256,2048]{1,0:T(8,128)(2,1)S(1)}, u32[]{:S(2)}, u32[]{:S(2)}) collective-permute-start(bf16[256,2048]{1,0:T(8,128)(2,1)S(1)} %copy-done.10), channel_id=1, source_target_pairs={{0,4},{2,6},{4,0},{6,2},{1,5},{3,7},{5,1},{7,3},{8,12},{10,14},{12... | collective-permute-start | bytes 3145736 | tf_op jit(solution)/shard_map/ppermute | solution.py:41
  182.7 26.2 %collective-permute-start.27 = (bf16[256,2048]{1,0:T(8,128)(2,1)}, bf16[256,2048]{1,0:T(8,128)(2,1)S(1)}, u32[]{:S(2)}, u32[]{:S(2)}) collective-permute-start(bf16[256,2048]{1,0:T(8,128)(2,1)} %get-tuple-element.180.refs_0_.refs_4_), channel_id=1, source_target_pairs={{0,2},{2,0},{4,6},{6,4},{1,3},{3,1},{5,7},{7,5},{8,10},{10,8},{12,... | collective-permute-start | bytes 3145736 | tf_op jit(solution)/shard_map/ppermute | solution.py:41
  182.7 26.2 %collective-permute-start.28 = (bf16[256,2048]{1,0:T(8,128)(2,1)}, bf16[256,2048]{1,0:T(8,128)(2,1)S(1)}, u32[]{:S(2)}, u32[]{:S(2)}) collective-permute-start(bf16[256,2048]{1,0:T(8,128)(2,1)} %collective-permute-done.26.refs_5_), channel_id=1, source_target_pairs={{0,2},{2,0},{4,6},{6,4},{1,3},{3,1},{5,7},{7,5},{8,10},{10,8},{12,... | collective-permute-start | bytes 3145736 | tf_op jit(solution)/shard_map/ppermute | solution.py:41
  207.6 22.0 %collective-permute-start.33 = (bf16[2,256,512]{2,1,0:T(8,128)(2,1)}, bf16[2,256,512]{2,1,0:T(8,128)(2,1)}, u32[]{:S(2)}, u32[]{:S(2)}) collective-permute-start(bf16[2,256,512]{2,1,0:T(8,128)(2,1)} %get-tuple-element.222), channel_id=1, source_target_pairs={{4,0},{6,2},{5,1},{7,3},{12,8},{14,10},{13,9},{15,11},{20,16},{22,... | collective-permute-start | bytes 1572872 | tf_op jit(solution)/shard_map/ppermute | solution.py:41
  222.6 162.1 %reduce-scatter.5.cloned.1.call-start = ((), (), s32[]{:S(2)}) async-start(), calls=%async_computation.4 | async-start | bytes 5242880 | tf_op jit(solution)/shard_map/reduce_scatter | solution.py:703
  222.7 17.1 %collective-permute-start.34 = (bf16[2,256,512]{2,1,0:T(8,128)(2,1)}, bf16[2,256,512]{2,1,0:T(8,128)(2,1)}, u32[]{:S(2)}, u32[]{:S(2)}) collective-permute-start(bf16[2,256,512]{2,1,0:T(8,128)(2,1)} %get-tuple-element.191), channel_id=1, source_target_pairs={{4,0},{6,2},{5,1},{7,3},{12,8},{14,10},{13,9},{15,11},{20,16},{22,... | collective-permute-start | bytes 1572872 | tf_op jit(solution)/shard_map/ppermute | solution.py:41
  226.0 19.4 %collective-permute-start.35 = (bf16[512,256]{1,0:T(8,128)(2,1)}, bf16[512,256]{1,0:T(8,128)(2,1)}, u32[]{:S(2)}, u32[]{:S(2)}) collective-permute-start(bf16[512,256]{1,0:T(8,128)(2,1)} %get-tuple-element.193), channel_id=1, source_target_pairs={{0,4},{2,6},{4,0},{6,2},{1,5},{3,7},{5,1},{7,3},{8,12},{10,14},{12... | collective-permute-start | bytes 786440 | tf_op jit(solution)/shard_map/ppermute | solution.py:41
  229.4 16.0 %collective-permute-start.36 = (bf16[512,256]{1,0:T(8,128)(2,1)}, bf16[512,256]{1,0:T(8,128)(2,1)}, u32[]{:S(2)}, u32[]{:S(2)}) collective-permute-start(bf16[512,256]{1,0:T(8,128)(2,1)} %get-tuple-element.194), channel_id=1, source_target_pairs={{0,2},{2,0},{4,6},{6,4},{1,3},{3,1},{5,7},{7,5},{8,10},{10,8},{12,... | collective-permute-start | bytes 786440 | tf_op jit(solution)/shard_map/ppermute | solution.py:41
  229.4 20.0 %collective-permute-start.37 = (bf16[512,256]{1,0:T(8,128)(2,1)S(1)}, bf16[512,256]{1,0:T(8,128)(2,1)}, u32[]{:S(2)}, u32[]{:S(2)}) collective-permute-start(bf16[512,256]{1,0:T(8,128)(2,1)S(1)} %get-tuple-element.195), channel_id=1, source_target_pairs={{0,6},{2,4},{4,2},{6,0},{1,7},{3,5},{5,3},{7,1},{8,14},{10,12},{12... | collective-permute-start | bytes 786440 | tf_op jit(solution)/shard_map/ppermute | solution.py:41
  241.9 31.6 %collective-permute-start.47 = (bf16[256,2048]{1,0:T(8,128)(2,1)S(1)}, bf16[256,2048]{1,0:T(8,128)(2,1)}, u32[]{:S(2)}, u32[]{:S(2)}) collective-permute-start(bf16[256,2048]{1,0:T(8,128)(2,1)S(1)} %pad_maximum_fusion.2.refs_1_.refs_2_.refs_20_), channel_id=1, source_target_pairs={{0,4},{2,6},{4,0},{6,2},{1,5},{3,7},{5,1},{7,3},{8,12},{10,14},{12... | collective-permute-start | bytes 3145736 | tf_op jit(solution)/shard_map/ppermute | solution.py:41
  242.0 41.9 %collective-permute-start.44 = (bf16[256,1024]{1,0:T(8,128)(2,1)}, bf16[256,1024]{1,0:T(8,128)(2,1)}, u32[]{:S(2)}, u32[]{:S(2)}) collective-permute-start(bf16[256,1024]{1,0:T(8,128)(2,1)} %get-tuple-element.202.refs_0_.refs_12_), channel_id=1, source_target_pairs={{0,4},{2,6},{4,0},{6,2},{1,5},{3,7},{5,1},{7,3},{8,12},{10,14},{12... | collective-permute-start | bytes 1572872 | tf_op jit(solution)/shard_map/ppermute | solution.py:41
  273.5 17.8 %collective-permute-start.48 = (bf16[256,2048]{1,0:T(8,128)(2,1)S(1)}, bf16[256,2048]{1,0:T(8,128)(2,1)}, u32[]{:S(2)}, u32[]{:S(2)}) collective-permute-start(bf16[256,2048]{1,0:T(8,128)(2,1)S(1)} %pad_maximum_fusion.2.refs_1_.refs_2_.refs_20_), channel_id=1, source_target_pairs={{0,2},{2,0},{4,6},{6,4},{1,3},{3,1},{5,7},{7,5},{8,10},{10,8},{12,... | collective-permute-start | bytes 3145736 | tf_op jit(solution)/shard_map/ppermute | solution.py:41
  273.5 17.8 %collective-permute-start.49 = (bf16[256,2048]{1,0:T(8,128)(2,1)}, bf16[256,2048]{1,0:T(8,128)(2,1)}, u32[]{:S(2)}, u32[]{:S(2)}) collective-permute-start(bf16[256,2048]{1,0:T(8,128)(2,1)} %collective-permute-done.47.refs_21_), channel_id=1, source_target_pairs={{0,2},{2,0},{4,6},{6,4},{1,3},{3,1},{5,7},{7,5},{8,10},{10,8},{12,... | collective-permute-start | bytes 3145736 | tf_op jit(solution)/shard_map/ppermute | solution.py:41
  274.9 14.1 %collective-permute-start.14 = (bf16[128,2048]{1,0:T(8,128)(2,1)}, bf16[128,2048]{1,0:T(8,128)(2,1)}, u32[]{:S(2)}, u32[]{:S(2)}) collective-permute-start(bf16[128,2048]{1,0:T(8,128)(2,1)} %constant_dynamic-slice_fusion.1), channel_id=1, source_target_pairs={{0,1},{1,0},{2,3},{3,2},{4,5},{5,4},{6,7},{7,6},{8,9},{9,8},{10,11... | collective-permute-start | bytes 1572872 | tf_op jit(solution)/shard_map/ppermute | solution.py:41
  (96 other events, 691.4 us)
Sparse Core Ops, SparseCore 0:
  131.8 43.3 reduce-scatter.8
  177.6 43.1 reduce-scatter.10
  223.1 77.8 reduce-scatter.6
  303.2 81.4 reduce-scatter.4

commit v4 on v3

--- a/solution.py
+++ b/solution.py
@@ -62,8 +62,11 @@
     return [block] + ([xperm(block, "ctx", bits[0])] if bits else [])
 
 
-def gather_rest(blocks, gate):
+def gather_rest(blocks, gate, own_gate=None):
+    own = blocks[0] if own_gate is None else after(blocks[0], own_gate)
     blocks = lax.optimization_barrier((blocks, gate))[0]
+    if own_gate is not None:
+        blocks = [own] + blocks[1:]
     for bit in ctx_bits()[1:]:
         blocks = blocks + [xperm(b, "ctx", bit) for b in blocks]
     return blocks
@@ -73,14 +76,16 @@
     return gather_rest(gather_first(block), gate)
 
 
-def gather_ctx_causal(block, gate, first_gate=None):
+def gather_ctx_causal(block, gate, own_gate, first_gate=None):
     blocks, offsets = [block], [0]
     for bit in ctx_bits():
         fresh = []
         for b, o in zip(blocks, offsets):
             if o:
                 b = after(b, gate)
-            elif first_gate is not None and bit > 1:
+            elif bit == 1:
+                b = after(b, own_gate)
+            elif first_gate is not None:
                 b = after(b, first_gate)
             fresh.append(
                 xperm(b, "ctx", bit, lambda i, o=o, bit=bit: (i ^ o) < (i ^ bit))
@@ -335,13 +340,10 @@
 
 
 def widen_kernel(values, first, other):
-    @pl.when(pl.program_id(0) == 0)
-    def _():
-        first[...] = values[...].astype(F32)
-
-    @pl.when(pl.program_id(0) > 0)
-    def _():
-        other[...] = values[...].astype(F32)
+    tile = first.shape[1]
+    first[...] = values[:, :tile].astype(F32)
+    for k in range(other.shape[0]):
+        other[k] = values[:, (k + 1) * tile : (k + 2) * tile].astype(F32)
 
 
 def widen_joint(values, tile):
@@ -349,12 +351,6 @@
     blocks = size // tile
     return pl.pallas_call(
         widen_kernel,
-        grid=(blocks,),
-        in_specs=[pl.BlockSpec((rows, tile), lambda i: (0, i))],
-        out_specs=[
-            pl.BlockSpec((rows, tile), lambda i: (0, 0)),
-            pl.BlockSpec((None, rows, tile), lambda i: (jnp.maximum(i - 1, 0), 0, 0)),
-        ],
         out_shape=[
             jax.ShapeDtypeStruct((rows, tile), F32),
             jax.ShapeDtypeStruct((blocks - 1, rows, tile), F32),
@@ -647,11 +643,11 @@
     mixed, stats, keyvals = None, [], []
     for g in range(groups):
         keyvals.append(
-            gather_ctx_causal(own[g], query if g == 0 else order[-1], query if g else None)
+            gather_ctx_causal(own[g], order[-1] if g else query, query, query if g else None)
         )
         mixed, stat = ran(
             attention_forward(
-                slopes, then(query), distance, keyvals[g], g * group_heads, group_heads, mixed,
+                slopes, then(query), distance, keyvals[g], g * group_heads, group_heads, mixed
             )
         )
         stats.append(stat)
@@ -680,17 +676,17 @@
     tile = local_hidden // 8
     half_hidden = local_hidden // 2
     up_bias_row = up_bias.astype(F32)[None]
-    middle, normed_second, active_near, grad_near, bias_near = ran(
+    middle, normed_second, active_near, grad_hidden, bias_near = ran(
         first_up(
             residual, second_vectors, [then(attention[0])] + attention[1:],
-            up_weight, up_bias_row, grad_active, half_hidden, half_hidden, tile,
+            up_weight, up_bias_row, grad_active, half_hidden, local_hidden, 2 * tile,
         )
     )
     mixed_seen = gather_first(mixed_sent)
-    active_far, grad_far, bias_far = ran(
+    active_far, grad_hidden, bias_far = ran(
         more_up(
             after(then(normed_second), early_left), up_weight, up_bias_row, grad_active,
-            half_hidden, half_hidden, 2 * tile, heavy=2,
+            half_hidden, half_hidden, 2 * tile, grad_hidden, heavy=2,
         )
     )
 
@@ -705,9 +701,7 @@
     def grad_normed_part(side):
         part = ran(
             mm(
-                [after(then(grad_near), mixed_seen), grad_far],
-                [(up_weight, None, 0), (up_weight, None, 1)],
-                trans=True, start=side * (width // 2), size=width // 2, tile=512,
+                [after(then(grad_hidden), mixed_seen)], [up_weight], trans=True, start=side * (width // 2), size=width // 2, tile=512,
                 out_dtype=BF16,
             )
         )
@@ -717,7 +711,8 @@
     near_rights = gather_ctx(active_near, order[-1])
     up_pieces = ran(spread_pieces(place, then(normed_second), heavy=1))
     down_parts = [reduce_over_dp([(early_left, 0, near_rights)])]
-    near_sent = after(grad_near, order[-1])
+    grad_sent = after(grad_hidden, order[-1])
+    up_left = spread_left(lax.optimization_barrier((up_pieces, order[-1]))[0])
 
     feed = ran(
         mm(
@@ -735,7 +730,7 @@
         return total
 
     feed_gate = order[-1]
-    up_left = spread_left(up_pieces)
+    grad_blocks = gather_first(grad_sent)
 
     def added(terms):
         total = after(terms[0], order[-1]).astype(F32)
@@ -750,14 +745,14 @@
     grad_middle_low = grad_middle.astype(BF16)
     grad_mixed = ran(
         mm(
-            [then(grad_middle_low)], [out_weight], trans=False, start=0,
-            size=local_width, tile=1024, out_dtype=BF16, heavy=1,
+            [after(then(grad_middle_low), up_left[len(up_left) // 2])], [out_weight], trans=False,
+            start=0, size=local_width, tile=1024, out_dtype=BF16, heavy=1,
         )
     )
     down_parts.append(
         reduce_over_dp([(early_left, 0, gather_ctx(active_far, feed_gate))], up_left)
     )
-    far_sent = after(grad_far, order[-1])
+    own_gate = order[-1]
     mixed_all = gather_rest(mixed_seen, order[-1])
     grad_query, kv_near, kv_far = None, [], []
     for g in range(groups):
@@ -773,7 +768,6 @@
     kv_received = [xperm(far, "ctx", 1) if n_ctx > 1 else None for far in kv_far]
     kv_near = after(kv_near, order[-1])
 
-    near_all = gather_ctx(near_sent, order[-1])
     partial = []
     for near, received in zip(kv_near, kv_received):
         blocks = [near[:, k].astype(F32) for k in range(near.shape[1])]
@@ -781,8 +775,8 @@
             blocks = [block + received[:, k].astype(F32) for k, block in enumerate(blocks)]
         partial.append(blocks)
     sent = [block.astype(BF16) for blocks in partial for block in blocks[len(blocks) // 2 :]]
-    far_all = gather_ctx(far_sent, sent)
-    up_part = reduce_over_dp([(up_left, 0, near_all), (up_left, 0, far_all)])
+    grad_all = gather_rest(grad_blocks, sent, own_gate)
+    up_part = reduce_over_dp([(up_left, 0, grad_all)])
     up_gate = order[-1]
     late_pieces = ran(spread_pieces(place, then(grad_middle_low), heavy=2))
     late_left = spread_left(late_pieces)

time: 401 us -> 392 us (0.978); the launches traced: 395 us -> 390 us
  waiting for transfers between devices: 128 us -> 136 us
  starting transfers between devices: 57.5 us -> 52.7 us
  local copies, waits for them, and re-layouts: 29.2 us -> 25 us
    reduce_scatter x4, waiting for transfers between devices: 18.1 us -> 26.6 us  [reduce_over_dp(): return lax.psum_scatter(whole, 'dp', scatter_dimension=0, tiled=True)]
    ppermute x50 -> x47, starting transfers between devices: 57.2 us -> 52.3 us  [xperm(): return lax.ppermute(values, axis, pairs)]
    unnamed x157 -> x143, local copies, waits for them, and re-layouts: 27.1 us -> 22.9 us
    ppermute x50 -> x47, waiting for transfers between devices: 109 us -> 110 us  [xperm(): return lax.ppermute(values, axis, pairs)]
  transfers between devices with their start and end apart: 54 -> 51, of which waited for: 18 -> 21; matrix products, arithmetic and copies ran while one was open for 10% -> 10% of each run, Pallas kernels for 29% -> 29%
where the time goes in v4:
time: 392 us; the launch traced here: 390 us
  waiting for transfers between devices  136 us (35%)
  Pallas kernels  130 us (33%)
  starting transfers between devices  52.7 us (13%)
  other arithmetic  31.5 us (8%)
  local copies, waits for them, and re-layouts  25 us (6%)
  between operations  14.8 us (4%)
    ppermute x47, waiting for transfers between devices, xperm(): return lax.ppermute(values, axis, pairs)  110 us
    ppermute x47, starting transfers between devices, xperm(): return lax.ppermute(values, axis, pairs)  52.3 us
    pallas_call x8, Pallas kernels, mm(): pl.pallas_call(functools.partial(mm_kernel, n_pairs=len(lefts), trans=tra...  43.6 us
    pallas_call x4, Pallas kernels, weight_grad(): pl.pallas_call(functools.partial(weight_grad_kernel, blocks=blocks, n=n),...  30.8 us
    reduce_scatter x4, waiting for transfers between devices, reduce_over_dp(): return lax.psum_scatter(whole, 'dp', scatter_dimension=0, tiled=True)  26.6 us
    unnamed x143, local copies, waits for them, and re-layouts  22.9 us
    pallas_call x2, Pallas kernels, attention_backward(): pl.pallas_call(functools.partial(backward_kernel, n=n, first_head=first_h...  13.9 us
    pallas_call x2, Pallas kernels, attention_forward(): pl.pallas_call(functools.partial(forward_kernel, n=n, first_head=first_he...  12.3 us
  transfers between devices with their start and end apart: 51, of which 21 were waited for; matrix products, arithmetic and copies ran while one was open for 10% of the time, Pallas kernels for 29%

profile of v4, /device:TPU:0, one launch (start us, length us, event | category | flops | bytes accessed | tf_op | source)
XLA Modules:
  0.0 390.5 jit_solution(10116930751748856020)
XLA Ops:
  7.2 6.5 %shard_map.254 = (bf16[256,2048]{1,0:T(8,128)(2,1)}, bf16[2,256,512]{2,1,0:T(8,128)(2,1)}, bf16[2,256,512]{2,1,0:T(8,128)(2,1)}) custom-call(bf16[256,2048]{1,0:T(8,128)(2,1)} %bitcast.100, bf16[2048]{0:T(1024)(128)(2,1)} %gain.1, bf16[2048]{0:T(1024)(128)(2,1)} %shift.1, bf16[3,2048,1024]{2,1,0:T(8,128)(2,1)} %bitcast.95, bf16[2,1024]{1,0:T(2,128)(2,1)} %refs_2_.2), custom_call_target="tpu_custom_call" | custom-call | tf_op jit(solution)/shard_map/pallas_call | solution.py:170
  13.8 5.8 %collective-permute-start = (bf16[2,256,512]{2,1,0:T(8,128)(2,1)}, bf16[2,256,512]{2,1,0:T(8,128)(2,1)}, u32[]{:S(2)}, u32[]{:S(2)}) collective-permute-start(bf16[2,256,512]{2,1,0:T(8,128)(2,1)} %get-tuple-element.121.refs_0_), channel_id=1, source_target_pairs={{0,4},{2,6},{1,5},{3,7},{8,12},{10,14},{9,13},{11,15},{16,20},{18,... | collective-permute-start | bytes 1572872 | tf_op jit(solution)/shard_map/ppermute | solution.py:41
  20.8 4.6 %copy-done = bf16[2048,3,1024]{2,0,1:T(8,128)(2,1)S(1)} copy-done((bf16[2048,3,1024]{2,0,1:T(8,128)(2,1)S(1)}, bf16[2048,3,1024]{2,0,1:T(8,128)(2,1)}, u32[]{:S(2)}) %copy-start) | copy-done | bytes 12582936
  38.3 5.9 %shard_map.257 = (bf16[256,1024]{1,0:T(8,128)(2,1)}, f32[4,1,256]{2,1,0:T(1,128)S(1)}) custom-call(f32[8]{0:T(128)S(1)} %multiply_exponential_fusion.slopes, bf16[256,1024]{1,0:T(8,128)(2,1)S(1)} %shard_map.255.query, f32[4,256,256]{2,1,0:T(8,128)S(1)} %pad_maximum_fusion.1.distance, bf16[2,256,512]{2,1,0:T(8,128)(2,1)} %get-tuple-element.121.refs_0_, ...), custom_call_target="tpu_custom_call" | custom-call | tf_op jit(solution)/shard_map/pallas_call | solution.py:424
  46.0 6.4 %shard_map.258 = (bf16[256,1024]{1,0:T(8,128)(2,1)}, f32[4,1,256]{2,1,0:T(1,128)S(1)}) custom-call(f32[8]{0:T(128)S(1)} %multiply_exponential_fusion.slopes, bf16[256,1024]{1,0:T(8,128)(2,1)S(1)} %shard_map.255.query, f32[4,256,256]{2,1,0:T(8,128)S(1)} %pad_maximum_fusion.1.distance, ...), custom_call_target="tpu_custom_call", output_to_operand_aliasing={{0}: (7, {})} | custom-call | tf_op jit(solution)/shard_map/pallas_call | solution.py:424
  52.4 3.4 shard_map.259.refs_2_
  62.7 8.6 %shard_map.260.refs_6_.grad_active = f32[256,4096]{1,0:T(8,128)S(1)} custom-call(bf16[256,2048]{1,0:T(8,128)(2,1)S(1)} %bitcast.103, bf16[2048,4096]{1,0:T(8,128)(2,1)} %refs_3_.1), custom_call_target="tpu_custom_call" | custom-call | flops 999999995904 | bytes 10000000 | tf_op jit(solution)/shard_map/pallas_call | solution.py:140
  71.3 7.6 %collective-permute-done.6.refs_3_ = bf16[256,2048]{1,0:T(8,128)(2,1)} collective-permute-done((bf16[256,2048]{1,0:T(8,128)(2,1)}, bf16[256,2048]{1,0:T(8,128)(2,1)}, u32[]{:S(2)}, u32[]{:S(2)}) %collective-permute-start.6) | collective-permute-done | bytes 1048608 | tf_op jit(solution)/shard_map/ppermute | solution.py:41
  78.9 9.0 %shard_map.261 = (f32[256,2048]{1,0:T(8,128)S(1)}, bf16[256,2048]{1,0:T(8,128)(2,1)S(1)}, bf16[256,2048]{1,0:T(8,128)(2,1)}, bf16[256,4096]{1,0:T(8,128)(2,1)}, f32[1,2048]{1,0:T(1,128)S(1)}) custom-call(bf16[256,2048]{1,0:T(8,128)(2,1)S(1)} %bitcast.101, f32[3,2048]{1,0:T(4,128)S(1)} %maximum_convert_fusion.1.refs_1_, ...), custom_call_target="tpu_custom_call" | custom-call | tf_op jit(solution)/shard_map/pallas_call | solution.py:258
  88.0 5.9 %collective-permute-start.11 = (bf16[256,2048]{1,0:T(8,128)(2,1)}, bf16[256,2048]{1,0:T(8,128)(2,1)}, u32[]{:S(2)}, u32[]{:S(2)}) collective-permute-start(bf16[256,2048]{1,0:T(8,128)(2,1)} %get-tuple-element.157.refs_4_.refs_0_), channel_id=1, source_target_pairs={{0,4},{2,6},{4,0},{6,2},{1,5},{3,7},{5,1},{7,3},{8,12},{10,14},{12... | collective-permute-start | bytes 3145736 | tf_op jit(solution)/shard_map/ppermute | solution.py:41
  93.9 7.1 %shard_map.262 = (bf16[256,2048]{1,0:T(8,128)(2,1)}, bf16[256,4096]{1,0:T(8,128)(2,1)}, f32[1,2048]{1,0:T(1,128)S(1)}) custom-call(bf16[256,2048]{1,0:T(8,128)(2,1)S(1)} %get-tuple-element.152.norm.refs_0_, bf16[2048,4096]{1,0:T(8,128)(2,1)} %refs_1_.8, f32[1,4096]{1,0:T(1,128)S(1)} %bitcast.107, ...), custom_call_target="tpu_custom_call", output_to_operand_aliasing={{1}: (4, {})} | custom-call | flops 999999995904 | bytes 10000000 | tf_op jit(solution)/shard_map/pallas_call | solution.py:281
  101.0 6.2 %shard_map.263 = bf16[256,1024]{1,0:T(8,128)(2,1)} custom-call(bf16[256,4096]{1,0:T(8,128)(2,1)} %get-tuple-element.189.refs_0_.refs_4_, bf16[2048,4096]{1,0:T(8,128)(2,1)} %refs_1_.8), custom_call_target="tpu_custom_call" | custom-call | tf_op jit(solution)/shard_map/pallas_call | solution.py:140
  107.2 6.2 %shard_map.264 = bf16[256,1024]{1,0:T(8,128)(2,1)} custom-call(bf16[256,4096]{1,0:T(8,128)(2,1)} %get-tuple-element.189.refs_0_.refs_4_, bf16[2048,4096]{1,0:T(8,128)(2,1)} %refs_1_.8), custom_call_target="tpu_custom_call" | custom-call | tf_op jit(solution)/shard_map/pallas_call | solution.py:140
  123.0 5.7 %shard_map.266 = bf16[512,2048]{1,0:T(8,128)(2,1)} custom-call(bf16[1024,256]{1,0:T(8,128)(2,1)} %copy-done.9, bf16[1024,256]{1,0:T(8,128)(2,1)} %collective-permute-done.7.refs_1_.refs_9_.refs_17_, bf16[1024,256]{1,0:T(8,128)(2,1)} %collective-permute-done.8.refs_2_.refs_10_.refs_18_, bf16[1024,256]{1,0:T(8,128)(2,1)} %collective-permute-done.9.refs_3_.refs_11_.refs_19_, ...), custom_call_target="tpu_custom_call" | custom-call | tf_op jit(solution)/shard_map/pallas_call | solution.py:331
  129.0 9.5 %shard_map.267 = bf16[256,2048]{1,0:T(8,128)(2,1)S(1)} custom-call(bf16[256,2048]{1,0:T(8,128)(2,1)} %get-tuple-element.157.refs_4_.refs_0_, bf16[256,2048]{1,0:T(8,128)(2,1)} %get-tuple-element.172.refs_1_.refs_4_, bf16[2048,4096]{1,0:T(8,128)(2,1)} %refs_3_.1, bf16[2048,4096]{1,0:T(8,128)(2,1)} %refs_3_.1), custom_call_target="tpu_custom_call" | custom-call | flops 999999995904 | bytes 10000000 | tf_op jit(solution)/shard_map/pallas_call | solution.py:140
  157.3 5.6 %shard_map.269 = bf16[512,2048]{1,0:T(8,128)(2,1)} custom-call(bf16[1024,256]{1,0:T(8,128)(2,1)} %copy-done.9, bf16[1024,256]{1,0:T(8,128)(2,1)} %collective-permute-done.7.refs_1_.refs_9_.refs_17_, bf16[1024,256]{1,0:T(8,128)(2,1)} %collective-permute-done.8.refs_2_.refs_10_.refs_18_, bf16[1024,256]{1,0:T(8,128)(2,1)} %collective-permute-done.9.refs_3_.refs_11_.refs_19_, ...), custom_call_target="tpu_custom_call" | custom-call | tf_op jit(solution)/shard_map/pallas_call | solution.py:331
  164.4 6.9 %shard_map.270 = (bf16[256,1024]{1,0:T(8,128)(2,1)}, bf16[2,2,256,512]{3,2,1,0:T(8,128)(2,1)S(1)}, bf16[2,2,256,512]{3,2,1,0:T(8,128)(2,1)S(1)}) custom-call(f32[8]{0:T(128)S(1)} %copy-done.32, bf16[256,1024]{1,0:T(8,128)(2,1)S(1)} %copy-done.13, bf16[256,1024]{1,0:T(8,128)(2,1)S(1)} %shard_map.268.grad_mixed, f32[4,256,256]{2,1,0:T(8,128)S(1)} %copy-done.6, ...), custom_call_target="tpu_custom_call" | custom-call | flops 999999995904 | bytes 10000000 | tf_op jit(solution)/shard_map/pallas_call | solution.py:504
  172.5 7.0 %shard_map.271 = (bf16[256,1024]{1,0:T(8,128)(2,1)}, bf16[2,2,256,512]{3,2,1,0:T(8,128)(2,1)S(1)}, bf16[2,2,256,512]{3,2,1,0:T(8,128)(2,1)S(1)}) custom-call(f32[8]{0:T(128)S(1)} %copy-done.32, bf16[256,1024]{1,0:T(8,128)(2,1)S(1)} %copy-done.13, bf16[256,1024]{1,0:T(8,128)(2,1)S(1)} %shard_map.268.grad_mixed, ...), custom_call_target="tpu_custom_call", output_to_operand_aliasing={{0}: (9, {})} | custom-call | tf_op jit(solution)/shard_map/pallas_call | solution.py:504
  185.0 15.0 %collective-permute-done.26.refs_5_ = bf16[256,4096]{1,0:T(8,128)(2,1)} collective-permute-done((bf16[256,4096]{1,0:T(8,128)(2,1)}, bf16[256,4096]{1,0:T(8,128)(2,1)}, u32[]{:S(2)}, u32[]{:S(2)}) %collective-permute-start.26) | collective-permute-done | bytes 2097184 | tf_op jit(solution)/shard_map/ppermute | solution.py:41
  204.5 9.0 %shard_map.272 = bf16[512,4096]{1,0:T(8,128)(2,1)} custom-call(bf16[512,256]{1,0:T(8,128)(2,1)} %copy-done.30, bf16[512,256]{1,0:T(8,128)(2,1)} %copy-done.54, bf16[512,256]{1,0:T(8,128)(2,1)} %copy-done.53, bf16[512,256]{1,0:T(8,128)(2,1)} %copy-done.55, bf16[256,4096]{1,0:T(8,128)(2,1)} %get-tuple-element.189.refs_0_.refs_4_, ...), custom_call_target="tpu_custom_call" | custom-call | tf_op jit(solution)/shard_map/pallas_call | solution.py:331
  221.5 9.1 %collective-permute-done.31 = bf16[2,256,512]{2,1,0:T(8,128)(2,1)} collective-permute-done((bf16[2,256,512]{2,1,0:T(8,128)(2,1)}, bf16[2,256,512]{2,1,0:T(8,128)(2,1)}, u32[]{:S(2)}, u32[]{:S(2)}) %collective-permute-start.31) | collective-permute-done | bytes 524320 | tf_op jit(solution)/shard_map/ppermute | solution.py:41
  236.3 4.0 %collective-permute-done.34.refs_3_ = bf16[512,256]{1,0:T(8,128)(2,1)} collective-permute-done((bf16[512,256]{1,0:T(8,128)(2,1)S(1)}, bf16[512,256]{1,0:T(8,128)(2,1)}, u32[]{:S(2)}, u32[]{:S(2)}) %collective-permute-start.34) | collective-permute-done | bytes 262176 | tf_op jit(solution)/shard_map/ppermute | solution.py:41
  240.3 7.2 %shard_map.274 = bf16[256,2048]{1,0:T(8,128)(2,1)S(1)} custom-call(bf16[256,1024]{1,0:T(8,128)(2,1)} %get-tuple-element.208.refs_0_.refs_12_, bf16[256,2048]{1,0:T(8,128)(2,1)S(1)} %pad_maximum_fusion.2.refs_1_.refs_2_.refs_20_, bf16[256,2048]{1,0:T(8,128)(2,1)S(1)} %pad_maximum_fusion.2.refs_1_.refs_2_.refs_20_, bf16[3,2048,1024]{2,1,0:T(8,128)(2,1)} %bitcast.96, ...), custom_call_target="tpu_custom_call" | custom-call | flops 10000000000 | bytes 10000000 | tf_op jit(solution)/shard_map/pallas_call | solution.py:140
  248.5 15.9 %collective-permute-done.44.refs_21_ = bf16[256,2048]{1,0:T(8,128)(2,1)} collective-permute-done((bf16[256,2048]{1,0:T(8,128)(2,1)S(1)}, bf16[256,2048]{1,0:T(8,128)(2,1)}, u32[]{:S(2)}, u32[]{:S(2)}) %collective-permute-start.44) | collective-permute-done | bytes 1048608 | tf_op jit(solution)/shard_map/ppermute | solution.py:41
  266.4 8.4 %collective-permute-done.41.refs_13_ = bf16[256,1024]{1,0:T(8,128)(2,1)} collective-permute-done((bf16[256,1024]{1,0:T(8,128)(2,1)}, bf16[256,1024]{1,0:T(8,128)(2,1)}, u32[]{:S(2)}, u32[]{:S(2)}) %collective-permute-start.41) | collective-permute-done | bytes 524320 | tf_op jit(solution)/shard_map/ppermute | solution.py:41
  275.3 4.6 %collective-permute-done.14 = bf16[128,2048]{1,0:T(8,128)(2,1)} collective-permute-done((bf16[128,2048]{1,0:T(8,128)(2,1)}, bf16[128,2048]{1,0:T(8,128)(2,1)}, u32[]{:S(2)}, u32[]{:S(2)}) %collective-permute-start.14) | collective-permute-done | bytes 524320 | tf_op jit(solution)/shard_map/ppermute | solution.py:41
  282.2 10.6 %shard_map.275 = bf16[512,4096]{1,0:T(8,128)(2,1)} custom-call(bf16[512,256]{1,0:T(8,128)(2,1)} %copy-done.29, bf16[512,256]{1,0:T(8,128)(2,1)} %collective-permute-done.32.refs_1_, bf16[512,256]{1,0:T(8,128)(2,1)} %collective-permute-done.33.refs_2_, bf16[512,256]{1,0:T(8,128)(2,1)} %collective-permute-done.34.refs_3_, ...), custom_call_target="tpu_custom_call" | custom-call | tf_op jit(solution)/shard_map/pallas_call | solution.py:331
  301.1 7.2 %collective-permute-done.35 = bf16[128,2048]{1,0:T(8,128)(2,1)} collective-permute-done((bf16[128,2048]{1,0:T(8,128)(2,1)}, bf16[128,2048]{1,0:T(8,128)(2,1)}, u32[]{:S(2)}, u32[]{:S(2)}) %collective-permute-start.35) | collective-permute-done | bytes 524320 | tf_op jit(solution)/shard_map/ppermute | solution.py:41
  318.8 4.8 %collective-permute-done.38 = f32[18,1024]{1,0:T(8,128)S(1)} collective-permute-done((f32[18,1024]{1,0:T(8,128)S(1)}, f32[18,1024]{1,0:T(8,128)S(1)}, u32[]{:S(2)}, u32[]{:S(2)}) %collective-permute-start.38) | collective-permute-done | bytes 73760 | tf_op jit(solution)/shard_map/ppermute | solution.py:41
  325.2 8.4 %collective-permute-done.39 = f32[18,1024]{1,0:T(8,128)S(1)} collective-permute-done((f32[18,1024]{1,0:T(8,128)S(1)}, f32[18,1024]{1,0:T(8,128)S(1)}, u32[]{:S(2)}, u32[]{:S(2)}) %collective-permute-start.39) | collective-permute-done | bytes 73760 | tf_op jit(solution)/shard_map/ppermute | solution.py:41
  338.2 8.9 %collective-permute-done.40 = f32[18,1024]{1,0:T(8,128)S(1)} collective-permute-done((f32[18,1024]{1,0:T(8,128)S(1)}, f32[18,1024]{1,0:T(8,128)S(1)}, u32[]{:S(2)}, u32[]{:S(2)}) %collective-permute-start.40) | collective-permute-done | bytes 73760 | tf_op jit(solution)/shard_map/ppermute | solution.py:41
  354.7 26.6 %reduce-scatter.5.cloned.1.call-done.values = bf16[128,4096]{1,0:T(8,128)(2,1)} async-done(((bf16[512,4096]{1,0:T(8,128)(2,1)}), bf16[128,4096]{1,0:T(8,128)(2,1)}) %reduce-scatter.5.cloned.1.call-update) | async-done | bytes 1048592 | tf_op jit(solution)/shard_map/reduce_scatter | solution.py:699
  (308 shorter events, 118.0 us)
Async XLA Ops:
  7.2 328.3 %reduce-scatter.9.cloned.1.call-start = ((), (), s32[]{:S(2)}) async-start(), calls=%async_computation.6 | async-start | bytes 2621440 | tf_op jit(solution)/shard_map/reduce_scatter | solution.py:699
  13.8 19.6 %collective-permute-start = (bf16[2,256,512]{2,1,0:T(8,128)(2,1)}, bf16[2,256,512]{2,1,0:T(8,128)(2,1)}, u32[]{:S(2)}, u32[]{:S(2)}) collective-permute-start(bf16[2,256,512]{2,1,0:T(8,128)(2,1)} %get-tuple-element.121.refs_0_), channel_id=1, source_target_pairs={{0,4},{2,6},{1,5},{3,7},{8,12},{10,14},{9,13},{11,15},{16,20},{18,... | collective-permute-start | bytes 1572872 | tf_op jit(solution)/shard_map/ppermute | solution.py:41
  26.8 19.1 %collective-permute-start.4 = (bf16[2,256,512]{2,1,0:T(8,128)(2,1)S(1)}, bf16[2,256,512]{2,1,0:T(8,128)(2,1)}, u32[]{:S(2)}, u32[]{:S(2)}) collective-permute-start(bf16[2,256,512]{2,1,0:T(8,128)(2,1)S(1)} %copy-done.19), channel_id=1, source_target_pairs={{0,2},{4,6},{1,3},{5,7},{8,10},{12,14},{9,11},{13,15},{16,18},{20,... | collective-permute-start | bytes 1572872 | tf_op jit(solution)/shard_map/ppermute | solution.py:41
  29.1 15.2 %collective-permute-start.3 = (bf16[2,256,512]{2,1,0:T(8,128)(2,1)S(1)}, bf16[2,256,512]{2,1,0:T(8,128)(2,1)}, u32[]{:S(2)}, u32[]{:S(2)}) collective-permute-start(bf16[2,256,512]{2,1,0:T(8,128)(2,1)S(1)} %copy-done.19), channel_id=1, source_target_pairs={{0,4},{2,6},{1,5},{3,7},{8,12},{10,14},{9,13},{11,15},{16,20},{18,... | collective-permute-start | bytes 1572872 | tf_op jit(solution)/shard_map/ppermute | solution.py:41
  55.7 23.2 %collective-permute-start.6 = (bf16[256,2048]{1,0:T(8,128)(2,1)}, bf16[256,2048]{1,0:T(8,128)(2,1)}, u32[]{:S(2)}, u32[]{:S(2)}) collective-permute-start(bf16[256,2048]{1,0:T(8,128)(2,1)} %shard_map.259.refs_2_), channel_id=1, source_target_pairs={{0,1},{1,0},{2,3},{3,2},{4,5},{5,4},{6,7},{7,6},{8,9},{9,8},{10,11... | collective-permute-start | bytes 3145736 | tf_op jit(solution)/shard_map/ppermute | solution.py:41
  57.2 30.7 %collective-permute-start.7 = (bf16[1024,256]{1,0:T(8,128)(2,1)}, bf16[1024,256]{1,0:T(8,128)(2,1)}, u32[]{:S(2)}, u32[]{:S(2)}) collective-permute-start(bf16[1024,256]{1,0:T(8,128)(2,1)} %get-tuple-element.140), channel_id=1, source_target_pairs={{0,4},{2,6},{4,0},{6,2},{1,5},{3,7},{5,1},{7,3},{8,12},{10,14},{12... | collective-permute-start | bytes 1572872 | tf_op jit(solution)/shard_map/ppermute | solution.py:41
  60.5 27.4 %collective-permute-start.8 = (bf16[1024,256]{1,0:T(8,128)(2,1)}, bf16[1024,256]{1,0:T(8,128)(2,1)}, u32[]{:S(2)}, u32[]{:S(2)}) collective-permute-start(bf16[1024,256]{1,0:T(8,128)(2,1)} %get-tuple-element.141), channel_id=1, source_target_pairs={{0,2},{2,0},{4,6},{6,4},{1,3},{3,1},{5,7},{7,5},{8,10},{10,8},{12,... | collective-permute-start | bytes 1572872 | tf_op jit(solution)/shard_map/ppermute | solution.py:41
  60.5 27.4 %collective-permute-start.9 = (bf16[1024,256]{1,0:T(8,128)(2,1)}, bf16[1024,256]{1,0:T(8,128)(2,1)}, u32[]{:S(2)}, u32[]{:S(2)}) collective-permute-start(bf16[1024,256]{1,0:T(8,128)(2,1)} %get-tuple-element.142), channel_id=1, source_target_pairs={{0,6},{2,4},{4,2},{6,0},{1,7},{3,5},{5,3},{7,1},{8,14},{10,12},{12... | collective-permute-start | bytes 1572872 | tf_op jit(solution)/shard_map/ppermute | solution.py:41
  60.6 40.4 %collective-permute-start.10 = (bf16[256,1024]{1,0:T(8,128)(2,1)}, bf16[256,1024]{1,0:T(8,128)(2,1)}, u32[]{:S(2)}, u32[]{:S(2)}) collective-permute-start(bf16[256,1024]{1,0:T(8,128)(2,1)} %get-tuple-element.178.refs_0_.refs_4_), channel_id=1, source_target_pairs={{0,4},{2,6},{4,0},{6,2},{1,5},{3,7},{5,1},{7,3},{8,12},{10,14},{12... | collective-permute-start | bytes 1572872 | tf_op jit(solution)/shard_map/ppermute | solution.py:41
  88.0 30.5 %collective-permute-start.11 = (bf16[256,2048]{1,0:T(8,128)(2,1)}, bf16[256,2048]{1,0:T(8,128)(2,1)}, u32[]{:S(2)}, u32[]{:S(2)}) collective-permute-start(bf16[256,2048]{1,0:T(8,128)(2,1)} %get-tuple-element.157.refs_4_.refs_0_), channel_id=1, source_target_pairs={{0,4},{2,6},{4,0},{6,2},{1,5},{3,7},{5,1},{7,3},{8,12},{10,14},{12... | collective-permute-start | bytes 3145736 | tf_op jit(solution)/shard_map/ppermute | solution.py:41
  113.4 28.9 %collective-permute-start.16 = (bf16[256,1024]{1,0:T(8,128)(2,1)}, bf16[256,1024]{1,0:T(8,128)(2,1)}, u32[]{:S(2)}, u32[]{:S(2)}) collective-permute-start(bf16[256,1024]{1,0:T(8,128)(2,1)} %shard_map.264), channel_id=1, source_target_pairs={{0,1},{1,0},{2,3},{3,2},{4,5},{5,4},{6,7},{7,6},{8,9},{9,8},{10,11... | collective-permute-start | bytes 1572872 | tf_op jit(solution)/shard_map/ppermute | solution.py:41
  114.9 29.1 %collective-permute-start.15 = (bf16[256,1024]{1,0:T(8,128)(2,1)}, bf16[256,1024]{1,0:T(8,128)(2,1)}, u32[]{:S(2)}, u32[]{:S(2)}) collective-permute-start(bf16[256,1024]{1,0:T(8,128)(2,1)} %shard_map.263), channel_id=1, source_target_pairs={{0,1},{1,0},{2,3},{3,2},{4,5},{5,4},{6,7},{7,6},{8,9},{9,8},{10,11... | collective-permute-start | bytes 1572872 | tf_op jit(solution)/shard_map/ppermute | solution.py:41
  115.4 25.0 %collective-permute-start.20 = (bf16[256,2048]{1,0:T(8,128)(2,1)}, bf16[256,2048]{1,0:T(8,128)(2,1)}, u32[]{:S(2)}, u32[]{:S(2)}) collective-permute-start(bf16[256,2048]{1,0:T(8,128)(2,1)} %get-tuple-element.172.refs_1_.refs_4_), channel_id=1, source_target_pairs={{0,4},{2,6},{4,0},{6,2},{1,5},{3,7},{5,1},{7,3},{8,12},{10,14},{12... | collective-permute-start | bytes 3145736 | tf_op jit(solution)/shard_map/ppermute | solution.py:41
  128.7 206.8 %reduce-scatter.11.cloned.1.call-start = ((), (), s32[]{:S(2)}) async-start(), calls=%async_computation.7 | async-start | bytes 2621440 | tf_op jit(solution)/shard_map/reduce_scatter | solution.py:699
  140.4 12.9 %collective-permute-start.18 = (bf16[512,256]{1,0:T(8,128)(2,1)}, bf16[512,256]{1,0:T(8,128)(2,1)S(1)}, u32[]{:S(2)}, u32[]{:S(2)}) collective-permute-start(bf16[512,256]{1,0:T(8,128)(2,1)} %get-tuple-element.169), channel_id=1, source_target_pairs={{0,4},{2,6},{4,0},{6,2},{1,5},{3,7},{5,1},{7,3},{8,12},{10,14},{12... | collective-permute-start | bytes 786440 | tf_op jit(solution)/shard_map/ppermute | solution.py:41
  142.1 12.4 %collective-permute-start.19 = (bf16[512,256]{1,0:T(8,128)(2,1)S(1)}, bf16[512,256]{1,0:T(8,128)(2,1)S(1)}, u32[]{:S(2)}, u32[]{:S(2)}) collective-permute-start(bf16[512,256]{1,0:T(8,128)(2,1)S(1)} %get-tuple-element.170), channel_id=1, source_target_pairs={{0,6},{2,4},{4,2},{6,0},{1,7},{3,5},{5,3},{7,1},{8,14},{10,12},{12... | collective-permute-start | bytes 786440 | tf_op jit(solution)/shard_map/ppermute | solution.py:41
  150.3 49.7 %collective-permute-start.26 = (bf16[256,4096]{1,0:T(8,128)(2,1)}, bf16[256,4096]{1,0:T(8,128)(2,1)}, u32[]{:S(2)}, u32[]{:S(2)}) collective-permute-start(bf16[256,4096]{1,0:T(8,128)(2,1)} %get-tuple-element.189.refs_0_.refs_4_), channel_id=1, source_target_pairs={{0,4},{2,6},{4,0},{6,2},{1,5},{3,7},{5,1},{7,3},{8,12},{10,14},{12... | collective-permute-start | bytes 6291464 | tf_op jit(solution)/shard_map/ppermute | solution.py:41
  162.9 189.0 %reduce-scatter.7.cloned.1.call-start = ((), (), s32[]{:S(2)}) async-start(), calls=%async_computation.5 | async-start | bytes 5242880 | tf_op jit(solution)/shard_map/reduce_scatter | solution.py:699
  180.5 20.8 %collective-permute-start.28 = (bf16[256,4096]{1,0:T(8,128)(2,1)}, bf16[256,4096]{1,0:T(8,128)(2,1)S(1)}, u32[]{:S(2)}, u32[]{:S(2)}) collective-permute-start(bf16[256,4096]{1,0:T(8,128)(2,1)} %get-tuple-element.189.refs_0_.refs_4_), channel_id=1, source_target_pairs={{0,2},{2,0},{4,6},{6,4},{1,3},{3,1},{5,7},{7,5},{8,10},{10,8},{12,... | collective-permute-start | bytes 6291464 | tf_op jit(solution)/shard_map/ppermute | solution.py:41
  200.0 20.3 %collective-permute-start.30 = (bf16[2,256,512]{2,1,0:T(8,128)(2,1)}, bf16[2,256,512]{2,1,0:T(8,128)(2,1)}, u32[]{:S(2)}, u32[]{:S(2)}) collective-permute-start(bf16[2,256,512]{2,1,0:T(8,128)(2,1)} %get-tuple-element.228), channel_id=1, source_target_pairs={{4,0},{6,2},{5,1},{7,3},{12,8},{14,10},{13,9},{15,11},{20,16},{22,... | collective-permute-start | bytes 1572872 | tf_op jit(solution)/shard_map/ppermute | solution.py:41
  213.5 167.8 %reduce-scatter.5.cloned.1.call-start = ((), (), s32[]{:S(2)}) async-start(), calls=%async_computation.4 | async-start | bytes 5242880 | tf_op jit(solution)/shard_map/reduce_scatter | solution.py:699
  213.6 17.1 %collective-permute-start.31 = (bf16[2,256,512]{2,1,0:T(8,128)(2,1)}, bf16[2,256,512]{2,1,0:T(8,128)(2,1)}, u32[]{:S(2)}, u32[]{:S(2)}) collective-permute-start(bf16[2,256,512]{2,1,0:T(8,128)(2,1)} %get-tuple-element.197), channel_id=1, source_target_pairs={{4,0},{6,2},{5,1},{7,3},{12,8},{14,10},{13,9},{15,11},{20,16},{22,... | collective-permute-start | bytes 1572872 | tf_op jit(solution)/shard_map/ppermute | solution.py:41
  216.9 19.4 %collective-permute-start.32 = (bf16[512,256]{1,0:T(8,128)(2,1)}, bf16[512,256]{1,0:T(8,128)(2,1)}, u32[]{:S(2)}, u32[]{:S(2)}) collective-permute-start(bf16[512,256]{1,0:T(8,128)(2,1)} %get-tuple-element.199), channel_id=1, source_target_pairs={{0,4},{2,6},{4,0},{6,2},{1,5},{3,7},{5,1},{7,3},{8,12},{10,14},{12... | collective-permute-start | bytes 786440 | tf_op jit(solution)/shard_map/ppermute | solution.py:41
  220.1 16.2 %collective-permute-start.33 = (bf16[512,256]{1,0:T(8,128)(2,1)}, bf16[512,256]{1,0:T(8,128)(2,1)}, u32[]{:S(2)}, u32[]{:S(2)}) collective-permute-start(bf16[512,256]{1,0:T(8,128)(2,1)} %get-tuple-element.200), channel_id=1, source_target_pairs={{0,2},{2,0},{4,6},{6,4},{1,3},{3,1},{5,7},{7,5},{8,10},{10,8},{12,... | collective-permute-start | bytes 786440 | tf_op jit(solution)/shard_map/ppermute | solution.py:41
  220.1 20.2 %collective-permute-start.34 = (bf16[512,256]{1,0:T(8,128)(2,1)S(1)}, bf16[512,256]{1,0:T(8,128)(2,1)}, u32[]{:S(2)}, u32[]{:S(2)}) collective-permute-start(bf16[512,256]{1,0:T(8,128)(2,1)S(1)} %get-tuple-element.201), channel_id=1, source_target_pairs={{0,6},{2,4},{4,2},{6,0},{1,7},{3,5},{5,3},{7,1},{8,14},{10,12},{12... | collective-permute-start | bytes 786440 | tf_op jit(solution)/shard_map/ppermute | solution.py:41
  232.8 31.6 %collective-permute-start.44 = (bf16[256,2048]{1,0:T(8,128)(2,1)S(1)}, bf16[256,2048]{1,0:T(8,128)(2,1)}, u32[]{:S(2)}, u32[]{:S(2)}) collective-permute-start(bf16[256,2048]{1,0:T(8,128)(2,1)S(1)} %pad_maximum_fusion.2.refs_1_.refs_2_.refs_20_), channel_id=1, source_target_pairs={{0,4},{2,6},{4,0},{6,2},{1,5},{3,7},{5,1},{7,3},{8,12},{10,14},{12... | collective-permute-start | bytes 3145736 | tf_op jit(solution)/shard_map/ppermute | solution.py:41
  232.9 41.9 %collective-permute-start.41 = (bf16[256,1024]{1,0:T(8,128)(2,1)}, bf16[256,1024]{1,0:T(8,128)(2,1)}, u32[]{:S(2)}, u32[]{:S(2)}) collective-permute-start(bf16[256,1024]{1,0:T(8,128)(2,1)} %get-tuple-element.208.refs_0_.refs_12_), channel_id=1, source_target_pairs={{0,4},{2,6},{4,0},{6,2},{1,5},{3,7},{5,1},{7,3},{8,12},{10,14},{12... | collective-permute-start | bytes 1572872 | tf_op jit(solution)/shard_map/ppermute | solution.py:41
  264.4 17.8 %collective-permute-start.45 = (bf16[256,2048]{1,0:T(8,128)(2,1)S(1)}, bf16[256,2048]{1,0:T(8,128)(2,1)}, u32[]{:S(2)}, u32[]{:S(2)}) collective-permute-start(bf16[256,2048]{1,0:T(8,128)(2,1)S(1)} %pad_maximum_fusion.2.refs_1_.refs_2_.refs_20_), channel_id=1, source_target_pairs={{0,2},{2,0},{4,6},{6,4},{1,3},{3,1},{5,7},{7,5},{8,10},{10,8},{12,... | collective-permute-start | bytes 3145736 | tf_op jit(solution)/shard_map/ppermute | solution.py:41
  264.4 17.8 %collective-permute-start.46 = (bf16[256,2048]{1,0:T(8,128)(2,1)}, bf16[256,2048]{1,0:T(8,128)(2,1)}, u32[]{:S(2)}, u32[]{:S(2)}) collective-permute-start(bf16[256,2048]{1,0:T(8,128)(2,1)} %collective-permute-done.44.refs_21_), channel_id=1, source_target_pairs={{0,2},{2,0},{4,6},{6,4},{1,3},{3,1},{5,7},{7,5},{8,10},{10,8},{12,... | collective-permute-start | bytes 3145736 | tf_op jit(solution)/shard_map/ppermute | solution.py:41
  265.8 14.1 %collective-permute-start.14 = (bf16[128,2048]{1,0:T(8,128)(2,1)}, bf16[128,2048]{1,0:T(8,128)(2,1)}, u32[]{:S(2)}, u32[]{:S(2)}) collective-permute-start(bf16[128,2048]{1,0:T(8,128)(2,1)} %constant_dynamic-slice_fusion.1), channel_id=1, source_target_pairs={{0,1},{1,0},{2,3},{3,2},{4,5},{5,4},{6,7},{7,6},{8,9},{9,8},{10,11... | collective-permute-start | bytes 1572872 | tf_op jit(solution)/shard_map/ppermute | solution.py:41
  295.1 13.3 %collective-permute-start.35 = (bf16[128,2048]{1,0:T(8,128)(2,1)}, bf16[128,2048]{1,0:T(8,128)(2,1)}, u32[]{:S(2)}, u32[]{:S(2)}) collective-permute-start(bf16[128,2048]{1,0:T(8,128)(2,1)} %constant_dynamic-slice_fusion), channel_id=1, source_target_pairs={{0,1},{1,0},{2,3},{3,2},{4,5},{5,4},{6,7},{7,6},{8,9},{9,8},{10,11... | collective-permute-start | bytes 1572872 | tf_op jit(solution)/shard_map/ppermute | solution.py:41
  333.6 13.4 %collective-permute-start.40 = (f32[18,1024]{1,0:T(8,128)S(1)}, f32[18,1024]{1,0:T(8,128)S(1)}, u32[]{:S(2)}, u32[]{:S(2)}) collective-permute-start(f32[18,1024]{1,0:T(8,128)S(1)} %add.215), channel_id=1, source_target_pairs={{0,16},{8,24},{16,0},{24,8},{1,17},{9,25},{17,1},{25,9},{2,18},{10... | collective-permute-start | bytes 221192 | tf_op jit(solution)/shard_map/ppermute | solution.py:41
  (86 other events, 639.0 us)
Sparse Core Ops, SparseCore 0:
  128.8 44.6 reduce-scatter.8
  175.9 43.1 reduce-scatter.10
  221.4 76.0 reduce-scatter.6
  299.8 81.4 reduce-scatter.4

commit v5 on v4

--- a/solution.py
+++ b/solution.py
@@ -529,6 +529,27 @@
             values = values + xperm(values, axis, bit)
             bit *= 2
     return values
+
+
+def sum_shared(values, shared, axes):
+    n, place = lax.axis_size(shared), lax.axis_index(shared)
+    rows = values.shape[0]
+    values = jnp.pad(values, ((0, -rows % n), (0, 0)))
+    bits = [1 << b for b in range(n.bit_length() - 1)]
+    for bit in bits:
+        half, upper = values.shape[0] // 2, (place & bit) // bit
+        mine = lax.dynamic_slice_in_dim(values, upper * half, half)
+        other = lax.dynamic_slice_in_dim(values, (1 - upper) * half, half)
+        values = mine + xperm(other, shared, bit)
+    values = all_sum(values, axes)
+    for bit in reversed(bits):
+        received, upper = xperm(values, shared, bit), (place & bit) != 0
+        values = jnp.where(
+            upper,
+            jnp.concatenate([received, values]),
+            jnp.concatenate([values, received]),
+        )
+    return values[:rows]
 
 
 def spread_kernel(place, *refs, n_values, n_ctx, n_dp, piece):
@@ -708,7 +729,7 @@
         return exchanged(part)
 
     normed_terms = [grad_normed_part(0), grad_normed_part(1)]
-    near_rights = gather_ctx(active_near, order[-1])
+    near_rights = gather_rest(gather_first(active_near), order[-1], active_far)
     up_pieces = ran(spread_pieces(place, then(normed_second), heavy=1))
     down_parts = [reduce_over_dp([(early_left, 0, near_rights)])]
     grad_sent = after(grad_hidden, order[-1])
@@ -848,7 +869,7 @@
             jnp.concatenate([bias_near, bias_far], axis=1).reshape(-1, local_width),
         ]
     )
-    sums = all_sum(sums, ("ctx", "dp"))
+    sums = sum_shared(sums, "ctx", ("dp",))
     vectors = sums[:count].reshape(6, width)
     in_bias_grad = sums[count : count + 2]
     up_bias_grad = sums[count + 2 :].reshape(-1)

time: 392 us -> 393 us (level); the launches traced: 390 us -> 387 us
    ppermute x47 -> x49, waiting for transfers between devices: 110 us -> 107 us  [xperm(): return lax.ppermute(values, axis, pairs)]
    ppermute x47 -> x49, starting transfers between devices: 52.3 us -> 52.2 us  [xperm(): return lax.ppermute(values, axis, pairs)]
  transfers between devices with their start and end apart: 51 -> 53, of which waited for: 21 -> 21; matrix products, arithmetic and copies ran while one was open for 10% -> 10% of each run, Pallas kernels for 29% -> 29%
where the time goes in v5:
time: 393 us; the launch traced here: 387 us
  waiting for transfers between devices  133 us (34%)
  Pallas kernels  130 us (33%)
  starting transfers between devices  52.5 us (13%)
  other arithmetic  31.6 us (8%)
  local copies, waits for them, and re-layouts  25.1 us (6%)
  between operations  15.1 us (4%)
    ppermute x49, waiting for transfers between devices, xperm(): return lax.ppermute(values, axis, pairs)  107 us
    ppermute x49, starting transfers between devices, xperm(): return lax.ppermute(values, axis, pairs)  52.2 us
    pallas_call x8, Pallas kernels, mm(): pl.pallas_call(functools.partial(mm_kernel, n_pairs=len(lefts), trans=tra...  43.6 us
    pallas_call x4, Pallas kernels, weight_grad(): pl.pallas_call(functools.partial(weight_grad_kernel, blocks=blocks, n=n),...  30.7 us
    reduce_scatter x4, waiting for transfers between devices, reduce_over_dp(): return lax.psum_scatter(whole, 'dp', scatter_dimension=0, tiled=True)  26 us
    unnamed x143, local copies, waits for them, and re-layouts  23 us
    pallas_call x2, Pallas kernels, attention_backward(): pl.pallas_call(functools.partial(backward_kernel, n=n, first_head=first_h...  13.9 us
    pallas_call x2, Pallas kernels, attention_forward(): pl.pallas_call(functools.partial(forward_kernel, n=n, first_head=first_he...  12.3 us
  transfers between devices with their start and end apart: 53, of which 21 were waited for; matrix products, arithmetic and copies ran while one was open for 10% of the time, Pallas kernels for 29%

profile of v5, /device:TPU:0, one launch (start us, length us, event | category | flops | bytes accessed | tf_op | source)
XLA Modules:
  0.0 387.4 jit_solution(4186583333003993877)
XLA Ops:
  7.2 6.5 %shard_map.254 = (bf16[256,2048]{1,0:T(8,128)(2,1)}, bf16[2,256,512]{2,1,0:T(8,128)(2,1)}, bf16[2,256,512]{2,1,0:T(8,128)(2,1)}) custom-call(bf16[256,2048]{1,0:T(8,128)(2,1)} %bitcast.100, bf16[2048]{0:T(1024)(128)(2,1)} %gain.1, bf16[2048]{0:T(1024)(128)(2,1)} %shift.1, bf16[3,2048,1024]{2,1,0:T(8,128)(2,1)} %bitcast.95, bf16[2,1024]{1,0:T(2,128)(2,1)} %refs_2_.2), custom_call_target="tpu_custom_call" | custom-call | tf_op jit(solution)/shard_map/pallas_call | solution.py:170
  13.8 5.8 %collective-permute-start = (bf16[2,256,512]{2,1,0:T(8,128)(2,1)}, bf16[2,256,512]{2,1,0:T(8,128)(2,1)}, u32[]{:S(2)}, u32[]{:S(2)}) collective-permute-start(bf16[2,256,512]{2,1,0:T(8,128)(2,1)} %get-tuple-element.121.refs_0_), channel_id=1, source_target_pairs={{0,4},{2,6},{1,5},{3,7},{8,12},{10,14},{9,13},{11,15},{16,20},{18,... | collective-permute-start | bytes 1572872 | tf_op jit(solution)/shard_map/ppermute | solution.py:41
  20.8 4.6 %copy-done = bf16[2048,3,1024]{2,0,1:T(8,128)(2,1)S(1)} copy-done((bf16[2048,3,1024]{2,0,1:T(8,128)(2,1)S(1)}, bf16[2048,3,1024]{2,0,1:T(8,128)(2,1)}, u32[]{:S(2)}) %copy-start) | copy-done | bytes 12582936
  38.3 5.9 %shard_map.257 = (bf16[256,1024]{1,0:T(8,128)(2,1)}, f32[4,1,256]{2,1,0:T(1,128)S(1)}) custom-call(f32[8]{0:T(128)S(1)} %multiply_exponential_fusion.slopes, bf16[256,1024]{1,0:T(8,128)(2,1)S(1)} %shard_map.255.query, f32[4,256,256]{2,1,0:T(8,128)S(1)} %pad_maximum_fusion.1.distance, bf16[2,256,512]{2,1,0:T(8,128)(2,1)} %get-tuple-element.121.refs_0_, ...), custom_call_target="tpu_custom_call" | custom-call | tf_op jit(solution)/shard_map/pallas_call | solution.py:424
  46.2 6.4 %shard_map.258 = (bf16[256,1024]{1,0:T(8,128)(2,1)}, f32[4,1,256]{2,1,0:T(1,128)S(1)}) custom-call(f32[8]{0:T(128)S(1)} %multiply_exponential_fusion.slopes, bf16[256,1024]{1,0:T(8,128)(2,1)S(1)} %shard_map.255.query, f32[4,256,256]{2,1,0:T(8,128)S(1)} %pad_maximum_fusion.1.distance, ...), custom_call_target="tpu_custom_call", output_to_operand_aliasing={{0}: (7, {})} | custom-call | tf_op jit(solution)/shard_map/pallas_call | solution.py:424
  62.9 8.6 %shard_map.260.refs_6_.grad_active = f32[256,4096]{1,0:T(8,128)S(1)} custom-call(bf16[256,2048]{1,0:T(8,128)(2,1)S(1)} %bitcast.103, bf16[2048,4096]{1,0:T(8,128)(2,1)} %refs_3_.1), custom_call_target="tpu_custom_call" | custom-call | flops 999999995904 | bytes 10000000 | tf_op jit(solution)/shard_map/pallas_call | solution.py:140
  71.6 7.6 %collective-permute-done.6.refs_3_ = bf16[256,2048]{1,0:T(8,128)(2,1)} collective-permute-done((bf16[256,2048]{1,0:T(8,128)(2,1)}, bf16[256,2048]{1,0:T(8,128)(2,1)}, u32[]{:S(2)}, u32[]{:S(2)}) %collective-permute-start.6) | collective-permute-done | bytes 1048608 | tf_op jit(solution)/shard_map/ppermute | solution.py:41
  79.2 9.0 %shard_map.261 = (f32[256,2048]{1,0:T(8,128)S(1)}, bf16[256,2048]{1,0:T(8,128)(2,1)S(1)}, bf16[256,2048]{1,0:T(8,128)(2,1)}, bf16[256,4096]{1,0:T(8,128)(2,1)}, f32[1,2048]{1,0:T(1,128)S(1)}) custom-call(bf16[256,2048]{1,0:T(8,128)(2,1)S(1)} %bitcast.101, f32[3,2048]{1,0:T(4,128)S(1)} %maximum_convert_fusion.1.refs_1_, ...), custom_call_target="tpu_custom_call" | custom-call | tf_op jit(solution)/shard_map/pallas_call | solution.py:258
  88.2 5.6 %collective-permute-start.11 = (bf16[256,2048]{1,0:T(8,128)(2,1)}, bf16[256,2048]{1,0:T(8,128)(2,1)}, u32[]{:S(2)}, u32[]{:S(2)}) collective-permute-start(bf16[256,2048]{1,0:T(8,128)(2,1)} %get-tuple-element.157.refs_4_.refs_0_), channel_id=1, source_target_pairs={{0,4},{2,6},{4,0},{6,2},{1,5},{3,7},{5,1},{7,3},{8,12},{10,14},{12... | collective-permute-start | bytes 3145736 | tf_op jit(solution)/shard_map/ppermute | solution.py:41
  93.9 7.1 %shard_map.262 = (bf16[256,2048]{1,0:T(8,128)(2,1)}, bf16[256,4096]{1,0:T(8,128)(2,1)}, f32[1,2048]{1,0:T(1,128)S(1)}) custom-call(bf16[256,2048]{1,0:T(8,128)(2,1)S(1)} %get-tuple-element.152.norm.refs_0_, bf16[2048,4096]{1,0:T(8,128)(2,1)} %refs_1_.8, f32[1,4096]{1,0:T(1,128)S(1)} %bitcast.107, ...), custom_call_target="tpu_custom_call", output_to_operand_aliasing={{1}: (4, {})} | custom-call | flops 999999995904 | bytes 10000000 | tf_op jit(solution)/shard_map/pallas_call | solution.py:281
  101.0 6.2 %shard_map.263 = bf16[256,1024]{1,0:T(8,128)(2,1)} custom-call(bf16[256,4096]{1,0:T(8,128)(2,1)} %get-tuple-element.189.refs_0_.refs_4_, bf16[2048,4096]{1,0:T(8,128)(2,1)} %refs_1_.8), custom_call_target="tpu_custom_call" | custom-call | tf_op jit(solution)/shard_map/pallas_call | solution.py:140
  107.2 6.2 %shard_map.264 = bf16[256,1024]{1,0:T(8,128)(2,1)} custom-call(bf16[256,4096]{1,0:T(8,128)(2,1)} %get-tuple-element.189.refs_0_.refs_4_, bf16[2048,4096]{1,0:T(8,128)(2,1)} %refs_1_.8), custom_call_target="tpu_custom_call" | custom-call | tf_op jit(solution)/shard_map/pallas_call | solution.py:140
  122.4 5.7 %shard_map.266 = bf16[512,2048]{1,0:T(8,128)(2,1)} custom-call(bf16[1024,256]{1,0:T(8,128)(2,1)} %copy-done.9, bf16[1024,256]{1,0:T(8,128)(2,1)} %collective-permute-done.7.refs_1_.refs_9_.refs_17_, bf16[1024,256]{1,0:T(8,128)(2,1)} %collective-permute-done.8.refs_2_.refs_10_.refs_18_, bf16[1024,256]{1,0:T(8,128)(2,1)} %collective-permute-done.9.refs_3_.refs_11_.refs_19_, ...), custom_call_target="tpu_custom_call" | custom-call | tf_op jit(solution)/shard_map/pallas_call | solution.py:331
  128.3 9.5 %shard_map.267 = bf16[256,2048]{1,0:T(8,128)(2,1)S(1)} custom-call(bf16[256,2048]{1,0:T(8,128)(2,1)} %get-tuple-element.157.refs_4_.refs_0_, bf16[256,2048]{1,0:T(8,128)(2,1)} %get-tuple-element.172.refs_1_.refs_4_, bf16[2048,4096]{1,0:T(8,128)(2,1)} %refs_3_.1, bf16[2048,4096]{1,0:T(8,128)(2,1)} %refs_3_.1), custom_call_target="tpu_custom_call" | custom-call | flops 999999995904 | bytes 10000000 | tf_op jit(solution)/shard_map/pallas_call | solution.py:140
  157.3 5.6 %shard_map.269 = bf16[512,2048]{1,0:T(8,128)(2,1)} custom-call(bf16[1024,256]{1,0:T(8,128)(2,1)} %copy-done.9, bf16[1024,256]{1,0:T(8,128)(2,1)} %collective-permute-done.7.refs_1_.refs_9_.refs_17_, bf16[1024,256]{1,0:T(8,128)(2,1)} %collective-permute-done.8.refs_2_.refs_10_.refs_18_, bf16[1024,256]{1,0:T(8,128)(2,1)} %collective-permute-done.9.refs_3_.refs_11_.refs_19_, ...), custom_call_target="tpu_custom_call" | custom-call | tf_op jit(solution)/shard_map/pallas_call | solution.py:331
  164.4 6.9 %shard_map.270 = (bf16[256,1024]{1,0:T(8,128)(2,1)}, bf16[2,2,256,512]{3,2,1,0:T(8,128)(2,1)S(1)}, bf16[2,2,256,512]{3,2,1,0:T(8,128)(2,1)S(1)}) custom-call(f32[8]{0:T(128)S(1)} %copy-done.32, bf16[256,1024]{1,0:T(8,128)(2,1)S(1)} %copy-done.13, bf16[256,1024]{1,0:T(8,128)(2,1)S(1)} %shard_map.268.grad_mixed, f32[4,256,256]{2,1,0:T(8,128)S(1)} %copy-done.6, ...), custom_call_target="tpu_custom_call" | custom-call | flops 999999995904 | bytes 10000000 | tf_op jit(solution)/shard_map/pallas_call | solution.py:504
  172.5 7.0 %shard_map.271 = (bf16[256,1024]{1,0:T(8,128)(2,1)}, bf16[2,2,256,512]{3,2,1,0:T(8,128)(2,1)S(1)}, bf16[2,2,256,512]{3,2,1,0:T(8,128)(2,1)S(1)}) custom-call(f32[8]{0:T(128)S(1)} %copy-done.32, bf16[256,1024]{1,0:T(8,128)(2,1)S(1)} %copy-done.13, bf16[256,1024]{1,0:T(8,128)(2,1)S(1)} %shard_map.268.grad_mixed, ...), custom_call_target="tpu_custom_call", output_to_operand_aliasing={{0}: (9, {})} | custom-call | tf_op jit(solution)/shard_map/pallas_call | solution.py:504
  184.9 15.1 %collective-permute-done.26.refs_5_ = bf16[256,4096]{1,0:T(8,128)(2,1)} collective-permute-done((bf16[256,4096]{1,0:T(8,128)(2,1)}, bf16[256,4096]{1,0:T(8,128)(2,1)}, u32[]{:S(2)}, u32[]{:S(2)}) %collective-permute-start.26) | collective-permute-done | bytes 2097184 | tf_op jit(solution)/shard_map/ppermute | solution.py:41
  204.5 8.9 %shard_map.272 = bf16[512,4096]{1,0:T(8,128)(2,1)} custom-call(bf16[512,256]{1,0:T(8,128)(2,1)} %copy-done.30, bf16[512,256]{1,0:T(8,128)(2,1)} %copy-done.54, bf16[512,256]{1,0:T(8,128)(2,1)} %copy-done.53, bf16[512,256]{1,0:T(8,128)(2,1)} %copy-done.55, bf16[256,4096]{1,0:T(8,128)(2,1)} %get-tuple-element.189.refs_0_.refs_4_, ...), custom_call_target="tpu_custom_call" | custom-call | tf_op jit(solution)/shard_map/pallas_call | solution.py:331
  221.7 9.0 %collective-permute-done.31 = bf16[2,256,512]{2,1,0:T(8,128)(2,1)} collective-permute-done((bf16[2,256,512]{2,1,0:T(8,128)(2,1)}, bf16[2,256,512]{2,1,0:T(8,128)(2,1)}, u32[]{:S(2)}, u32[]{:S(2)}) %collective-permute-start.31) | collective-permute-done | bytes 524320 | tf_op jit(solution)/shard_map/ppermute | solution.py:41
  236.2 4.0 %collective-permute-done.34.refs_3_ = bf16[512,256]{1,0:T(8,128)(2,1)} collective-permute-done((bf16[512,256]{1,0:T(8,128)(2,1)S(1)}, bf16[512,256]{1,0:T(8,128)(2,1)}, u32[]{:S(2)}, u32[]{:S(2)}) %collective-permute-start.34) | collective-permute-done | bytes 262176 | tf_op jit(solution)/shard_map/ppermute | solution.py:41
  240.2 7.3 %shard_map.274 = bf16[256,2048]{1,0:T(8,128)(2,1)S(1)} custom-call(bf16[256,1024]{1,0:T(8,128)(2,1)} %get-tuple-element.208.refs_0_.refs_12_, bf16[256,2048]{1,0:T(8,128)(2,1)S(1)} %pad_maximum_fusion.2.refs_1_.refs_2_.refs_20_, bf16[256,2048]{1,0:T(8,128)(2,1)S(1)} %pad_maximum_fusion.2.refs_1_.refs_2_.refs_20_, bf16[3,2048,1024]{2,1,0:T(8,128)(2,1)} %bitcast.96, ...), custom_call_target="tpu_custom_call" | custom-call | flops 10000000000 | bytes 10000000 | tf_op jit(solution)/shard_map/pallas_call | solution.py:140
  248.4 15.9 %collective-permute-done.46.refs_21_ = bf16[256,2048]{1,0:T(8,128)(2,1)} collective-permute-done((bf16[256,2048]{1,0:T(8,128)(2,1)S(1)}, bf16[256,2048]{1,0:T(8,128)(2,1)}, u32[]{:S(2)}, u32[]{:S(2)}) %collective-permute-start.46) | collective-permute-done | bytes 1048608 | tf_op jit(solution)/shard_map/ppermute | solution.py:41
  266.2 8.5 %collective-permute-done.43.refs_13_ = bf16[256,1024]{1,0:T(8,128)(2,1)} collective-permute-done((bf16[256,1024]{1,0:T(8,128)(2,1)}, bf16[256,1024]{1,0:T(8,128)(2,1)}, u32[]{:S(2)}, u32[]{:S(2)}) %collective-permute-start.43) | collective-permute-done | bytes 524320 | tf_op jit(solution)/shard_map/ppermute | solution.py:41
  275.2 4.6 %collective-permute-done.14 = bf16[128,2048]{1,0:T(8,128)(2,1)} collective-permute-done((bf16[128,2048]{1,0:T(8,128)(2,1)}, bf16[128,2048]{1,0:T(8,128)(2,1)}, u32[]{:S(2)}, u32[]{:S(2)}) %collective-permute-start.14) | collective-permute-done | bytes 524320 | tf_op jit(solution)/shard_map/ppermute | solution.py:41
  282.1 10.5 %shard_map.275 = bf16[512,4096]{1,0:T(8,128)(2,1)} custom-call(bf16[512,256]{1,0:T(8,128)(2,1)} %copy-done.29, bf16[512,256]{1,0:T(8,128)(2,1)} %collective-permute-done.32.refs_1_, bf16[512,256]{1,0:T(8,128)(2,1)} %collective-permute-done.33.refs_2_, bf16[512,256]{1,0:T(8,128)(2,1)} %collective-permute-done.34.refs_3_, ...), custom_call_target="tpu_custom_call" | custom-call | tf_op jit(solution)/shard_map/pallas_call | solution.py:331
  300.9 7.3 %collective-permute-done.35 = bf16[128,2048]{1,0:T(8,128)(2,1)} collective-permute-done((bf16[128,2048]{1,0:T(8,128)(2,1)}, bf16[128,2048]{1,0:T(8,128)(2,1)}, u32[]{:S(2)}, u32[]{:S(2)}) %collective-permute-start.35) | collective-permute-done | bytes 524320 | tf_op jit(solution)/shard_map/ppermute | solution.py:41
  318.7 3.9 %collective-permute-done.38 = f32[5,1024]{1,0:T(8,128)S(1)} collective-permute-done((f32[5,1024]{1,0:T(8,128)S(1)}, f32[5,1024]{1,0:T(8,128)S(1)}, u32[]{:S(2)}, u32[]{:S(2)}) %collective-permute-start.38) | collective-permute-done | bytes 20512 | tf_op jit(solution)/shard_map/ppermute | solution.py:41
  324.2 4.8 %collective-permute-done.39 = f32[5,1024]{1,0:T(8,128)S(1)} collective-permute-done((f32[5,1024]{1,0:T(8,128)S(1)}, f32[5,1024]{1,0:T(8,128)S(1)}, u32[]{:S(2)}, u32[]{:S(2)}) %collective-permute-start.39) | collective-permute-done | bytes 20512 | tf_op jit(solution)/shard_map/ppermute | solution.py:41
  331.3 6.3 %collective-permute-done.40 = f32[5,1024]{1,0:T(8,128)S(1)} collective-permute-done((f32[5,1024]{1,0:T(8,128)S(1)}, f32[5,1024]{1,0:T(8,128)S(1)}, u32[]{:S(2)}, u32[]{:S(2)}) %collective-permute-start.40) | collective-permute-done | bytes 20512 | tf_op jit(solution)/shard_map/ppermute | solution.py:41
  337.6 3.9 %collective-permute-done.41 = f32[5,1024]{1,0:T(8,128)S(1)} collective-permute-done((f32[5,1024]{1,0:T(8,128)S(1)}, f32[5,1024]{1,0:T(8,128)S(1)}, u32[]{:S(2)}, u32[]{:S(2)}) %collective-permute-start.41) | collective-permute-done | bytes 20512 | tf_op jit(solution)/shard_map/ppermute | solution.py:41
  352.1 25.9 %reduce-scatter.5.cloned.1.call-done.values = bf16[128,4096]{1,0:T(8,128)(2,1)} async-done(((bf16[512,4096]{1,0:T(8,128)(2,1)}), bf16[128,4096]{1,0:T(8,128)(2,1)}) %reduce-scatter.5.cloned.1.call-update) | async-done | bytes 1048592 | tf_op jit(solution)/shard_map/reduce_scatter | solution.py:720
  (316 shorter events, 122.3 us)
Async XLA Ops:
  7.2 334.5 %reduce-scatter.9.cloned.1.call-start = ((), (), s32[]{:S(2)}) async-start(), calls=%async_computation.6 | async-start | bytes 2621440 | tf_op jit(solution)/shard_map/reduce_scatter | solution.py:720
  13.8 19.6 %collective-permute-start = (bf16[2,256,512]{2,1,0:T(8,128)(2,1)}, bf16[2,256,512]{2,1,0:T(8,128)(2,1)}, u32[]{:S(2)}, u32[]{:S(2)}) collective-permute-start(bf16[2,256,512]{2,1,0:T(8,128)(2,1)} %get-tuple-element.121.refs_0_), channel_id=1, source_target_pairs={{0,4},{2,6},{1,5},{3,7},{8,12},{10,14},{9,13},{11,15},{16,20},{18,... | collective-permute-start | bytes 1572872 | tf_op jit(solution)/shard_map/ppermute | solution.py:41
  26.8 19.4 %collective-permute-start.4 = (bf16[2,256,512]{2,1,0:T(8,128)(2,1)S(1)}, bf16[2,256,512]{2,1,0:T(8,128)(2,1)}, u32[]{:S(2)}, u32[]{:S(2)}) collective-permute-start(bf16[2,256,512]{2,1,0:T(8,128)(2,1)S(1)} %copy-done.19), channel_id=1, source_target_pairs={{0,2},{4,6},{1,3},{5,7},{8,10},{12,14},{9,11},{13,15},{16,18},{20,... | collective-permute-start | bytes 1572872 | tf_op jit(solution)/shard_map/ppermute | solution.py:41
  29.1 15.2 %collective-permute-start.3 = (bf16[2,256,512]{2,1,0:T(8,128)(2,1)S(1)}, bf16[2,256,512]{2,1,0:T(8,128)(2,1)}, u32[]{:S(2)}, u32[]{:S(2)}) collective-permute-start(bf16[2,256,512]{2,1,0:T(8,128)(2,1)S(1)} %copy-done.19), channel_id=1, source_target_pairs={{0,4},{2,6},{1,5},{3,7},{8,12},{10,14},{9,13},{11,15},{16,20},{18,... | collective-permute-start | bytes 1572872 | tf_op jit(solution)/shard_map/ppermute | solution.py:41
  56.0 23.2 %collective-permute-start.6 = (bf16[256,2048]{1,0:T(8,128)(2,1)}, bf16[256,2048]{1,0:T(8,128)(2,1)}, u32[]{:S(2)}, u32[]{:S(2)}) collective-permute-start(bf16[256,2048]{1,0:T(8,128)(2,1)} %shard_map.259.refs_2_), channel_id=1, source_target_pairs={{0,1},{1,0},{2,3},{3,2},{4,5},{5,4},{6,7},{7,6},{8,9},{9,8},{10,11... | collective-permute-start | bytes 3145736 | tf_op jit(solution)/shard_map/ppermute | solution.py:41
  57.5 30.7 %collective-permute-start.7 = (bf16[1024,256]{1,0:T(8,128)(2,1)}, bf16[1024,256]{1,0:T(8,128)(2,1)}, u32[]{:S(2)}, u32[]{:S(2)}) collective-permute-start(bf16[1024,256]{1,0:T(8,128)(2,1)} %get-tuple-element.140), channel_id=1, source_target_pairs={{0,4},{2,6},{4,0},{6,2},{1,5},{3,7},{5,1},{7,3},{8,12},{10,14},{12... | collective-permute-start | bytes 1572872 | tf_op jit(solution)/shard_map/ppermute | solution.py:41
  60.8 27.4 %collective-permute-start.8 = (bf16[1024,256]{1,0:T(8,128)(2,1)}, bf16[1024,256]{1,0:T(8,128)(2,1)}, u32[]{:S(2)}, u32[]{:S(2)}) collective-permute-start(bf16[1024,256]{1,0:T(8,128)(2,1)} %get-tuple-element.141), channel_id=1, source_target_pairs={{0,2},{2,0},{4,6},{6,4},{1,3},{3,1},{5,7},{7,5},{8,10},{10,8},{12,... | collective-permute-start | bytes 1572872 | tf_op jit(solution)/shard_map/ppermute | solution.py:41
  60.8 27.4 %collective-permute-start.9 = (bf16[1024,256]{1,0:T(8,128)(2,1)}, bf16[1024,256]{1,0:T(8,128)(2,1)}, u32[]{:S(2)}, u32[]{:S(2)}) collective-permute-start(bf16[1024,256]{1,0:T(8,128)(2,1)} %get-tuple-element.142), channel_id=1, source_target_pairs={{0,6},{2,4},{4,2},{6,0},{1,7},{3,5},{5,3},{7,1},{8,14},{10,12},{12... | collective-permute-start | bytes 1572872 | tf_op jit(solution)/shard_map/ppermute | solution.py:41
  60.9 40.1 %collective-permute-start.10 = (bf16[256,1024]{1,0:T(8,128)(2,1)}, bf16[256,1024]{1,0:T(8,128)(2,1)}, u32[]{:S(2)}, u32[]{:S(2)}) collective-permute-start(bf16[256,1024]{1,0:T(8,128)(2,1)} %get-tuple-element.178.refs_0_.refs_4_), channel_id=1, source_target_pairs={{0,4},{2,6},{4,0},{6,2},{1,5},{3,7},{5,1},{7,3},{8,12},{10,14},{12... | collective-permute-start | bytes 1572872 | tf_op jit(solution)/shard_map/ppermute | solution.py:41
  88.2 30.6 %collective-permute-start.11 = (bf16[256,2048]{1,0:T(8,128)(2,1)}, bf16[256,2048]{1,0:T(8,128)(2,1)}, u32[]{:S(2)}, u32[]{:S(2)}) collective-permute-start(bf16[256,2048]{1,0:T(8,128)(2,1)} %get-tuple-element.157.refs_4_.refs_0_), channel_id=1, source_target_pairs={{0,4},{2,6},{4,0},{6,2},{1,5},{3,7},{5,1},{7,3},{8,12},{10,14},{12... | collective-permute-start | bytes 3145736 | tf_op jit(solution)/shard_map/ppermute | solution.py:41
  113.4 28.9 %collective-permute-start.16 = (bf16[256,1024]{1,0:T(8,128)(2,1)}, bf16[256,1024]{1,0:T(8,128)(2,1)}, u32[]{:S(2)}, u32[]{:S(2)}) collective-permute-start(bf16[256,1024]{1,0:T(8,128)(2,1)} %shard_map.264), channel_id=1, source_target_pairs={{0,1},{1,0},{2,3},{3,2},{4,5},{5,4},{6,7},{7,6},{8,9},{9,8},{10,11... | collective-permute-start | bytes 1572872 | tf_op jit(solution)/shard_map/ppermute | solution.py:41
  114.9 29.1 %collective-permute-start.15 = (bf16[256,1024]{1,0:T(8,128)(2,1)}, bf16[256,1024]{1,0:T(8,128)(2,1)}, u32[]{:S(2)}, u32[]{:S(2)}) collective-permute-start(bf16[256,1024]{1,0:T(8,128)(2,1)} %shard_map.263), channel_id=1, source_target_pairs={{0,1},{1,0},{2,3},{3,2},{4,5},{5,4},{6,7},{7,6},{8,9},{9,8},{10,11... | collective-permute-start | bytes 1572872 | tf_op jit(solution)/shard_map/ppermute | solution.py:41
  115.4 25.0 %collective-permute-start.20 = (bf16[256,2048]{1,0:T(8,128)(2,1)}, bf16[256,2048]{1,0:T(8,128)(2,1)}, u32[]{:S(2)}, u32[]{:S(2)}) collective-permute-start(bf16[256,2048]{1,0:T(8,128)(2,1)} %get-tuple-element.172.refs_1_.refs_4_), channel_id=1, source_target_pairs={{0,4},{2,6},{4,0},{6,2},{1,5},{3,7},{5,1},{7,3},{8,12},{10,14},{12... | collective-permute-start | bytes 3145736 | tf_op jit(solution)/shard_map/ppermute | solution.py:41
  128.1 213.6 %reduce-scatter.11.cloned.1.call-start = ((), (), s32[]{:S(2)}) async-start(), calls=%async_computation.7 | async-start | bytes 2621440 | tf_op jit(solution)/shard_map/reduce_scatter | solution.py:720
  140.4 12.9 %collective-permute-start.18 = (bf16[512,256]{1,0:T(8,128)(2,1)}, bf16[512,256]{1,0:T(8,128)(2,1)S(1)}, u32[]{:S(2)}, u32[]{:S(2)}) collective-permute-start(bf16[512,256]{1,0:T(8,128)(2,1)} %get-tuple-element.169), channel_id=1, source_target_pairs={{0,4},{2,6},{4,0},{6,2},{1,5},{3,7},{5,1},{7,3},{8,12},{10,14},{12... | collective-permute-start | bytes 786440 | tf_op jit(solution)/shard_map/ppermute | solution.py:41
  142.2 12.4 %collective-permute-start.19 = (bf16[512,256]{1,0:T(8,128)(2,1)S(1)}, bf16[512,256]{1,0:T(8,128)(2,1)S(1)}, u32[]{:S(2)}, u32[]{:S(2)}) collective-permute-start(bf16[512,256]{1,0:T(8,128)(2,1)S(1)} %get-tuple-element.170), channel_id=1, source_target_pairs={{0,6},{2,4},{4,2},{6,0},{1,7},{3,5},{5,3},{7,1},{8,14},{10,12},{12... | collective-permute-start | bytes 786440 | tf_op jit(solution)/shard_map/ppermute | solution.py:41
  142.3 12.3 %collective-permute-start.21 = (bf16[256,2048]{1,0:T(8,128)(2,1)}, bf16[256,2048]{1,0:T(8,128)(2,1)S(1)}, u32[]{:S(2)}, u32[]{:S(2)}) collective-permute-start(bf16[256,2048]{1,0:T(8,128)(2,1)} %get-tuple-element.172.refs_1_.refs_4_), channel_id=1, source_target_pairs={{0,2},{2,0},{4,6},{6,4},{1,3},{3,1},{5,7},{7,5},{8,10},{10,8},{12,... | collective-permute-start | bytes 3145736 | tf_op jit(solution)/shard_map/ppermute | solution.py:41
  150.3 49.7 %collective-permute-start.26 = (bf16[256,4096]{1,0:T(8,128)(2,1)}, bf16[256,4096]{1,0:T(8,128)(2,1)}, u32[]{:S(2)}, u32[]{:S(2)}) collective-permute-start(bf16[256,4096]{1,0:T(8,128)(2,1)} %get-tuple-element.189.refs_0_.refs_4_), channel_id=1, source_target_pairs={{0,4},{2,6},{4,0},{6,2},{1,5},{3,7},{5,1},{7,3},{8,12},{10,14},{12... | collective-permute-start | bytes 6291464 | tf_op jit(solution)/shard_map/ppermute | solution.py:41
  162.9 186.4 %reduce-scatter.7.cloned.1.call-start = ((), (), s32[]{:S(2)}) async-start(), calls=%async_computation.5 | async-start | bytes 5242880 | tf_op jit(solution)/shard_map/reduce_scatter | solution.py:720
  180.5 20.8 %collective-permute-start.28 = (bf16[256,4096]{1,0:T(8,128)(2,1)}, bf16[256,4096]{1,0:T(8,128)(2,1)S(1)}, u32[]{:S(2)}, u32[]{:S(2)}) collective-permute-start(bf16[256,4096]{1,0:T(8,128)(2,1)} %get-tuple-element.189.refs_0_.refs_4_), channel_id=1, source_target_pairs={{0,2},{2,0},{4,6},{6,4},{1,3},{3,1},{5,7},{7,5},{8,10},{10,8},{12,... | collective-permute-start | bytes 6291464 | tf_op jit(solution)/shard_map/ppermute | solution.py:41
  200.0 20.4 %collective-permute-start.30 = (bf16[2,256,512]{2,1,0:T(8,128)(2,1)}, bf16[2,256,512]{2,1,0:T(8,128)(2,1)}, u32[]{:S(2)}, u32[]{:S(2)}) collective-permute-start(bf16[2,256,512]{2,1,0:T(8,128)(2,1)} %get-tuple-element.228), channel_id=1, source_target_pairs={{4,0},{6,2},{5,1},{7,3},{12,8},{14,10},{13,9},{15,11},{20,16},{22,... | collective-permute-start | bytes 1572872 | tf_op jit(solution)/shard_map/ppermute | solution.py:41
  213.4 164.5 %reduce-scatter.5.cloned.1.call-start = ((), (), s32[]{:S(2)}) async-start(), calls=%async_computation.4 | async-start | bytes 5242880 | tf_op jit(solution)/shard_map/reduce_scatter | solution.py:720
  213.5 17.1 %collective-permute-start.31 = (bf16[2,256,512]{2,1,0:T(8,128)(2,1)}, bf16[2,256,512]{2,1,0:T(8,128)(2,1)}, u32[]{:S(2)}, u32[]{:S(2)}) collective-permute-start(bf16[2,256,512]{2,1,0:T(8,128)(2,1)} %get-tuple-element.197), channel_id=1, source_target_pairs={{4,0},{6,2},{5,1},{7,3},{12,8},{14,10},{13,9},{15,11},{20,16},{22,... | collective-permute-start | bytes 1572872 | tf_op jit(solution)/shard_map/ppermute | solution.py:41
  216.8 19.5 %collective-permute-start.32 = (bf16[512,256]{1,0:T(8,128)(2,1)}, bf16[512,256]{1,0:T(8,128)(2,1)}, u32[]{:S(2)}, u32[]{:S(2)}) collective-permute-start(bf16[512,256]{1,0:T(8,128)(2,1)} %get-tuple-element.199), channel_id=1, source_target_pairs={{0,4},{2,6},{4,0},{6,2},{1,5},{3,7},{5,1},{7,3},{8,12},{10,14},{12... | collective-permute-start | bytes 786440 | tf_op jit(solution)/shard_map/ppermute | solution.py:41
  220.2 16.0 %collective-permute-start.33 = (bf16[512,256]{1,0:T(8,128)(2,1)}, bf16[512,256]{1,0:T(8,128)(2,1)}, u32[]{:S(2)}, u32[]{:S(2)}) collective-permute-start(bf16[512,256]{1,0:T(8,128)(2,1)} %get-tuple-element.200), channel_id=1, source_target_pairs={{0,2},{2,0},{4,6},{6,4},{1,3},{3,1},{5,7},{7,5},{8,10},{10,8},{12,... | collective-permute-start | bytes 786440 | tf_op jit(solution)/shard_map/ppermute | solution.py:41
  220.2 20.0 %collective-permute-start.34 = (bf16[512,256]{1,0:T(8,128)(2,1)S(1)}, bf16[512,256]{1,0:T(8,128)(2,1)}, u32[]{:S(2)}, u32[]{:S(2)}) collective-permute-start(bf16[512,256]{1,0:T(8,128)(2,1)S(1)} %get-tuple-element.201), channel_id=1, source_target_pairs={{0,6},{2,4},{4,2},{6,0},{1,7},{3,5},{5,3},{7,1},{8,14},{10,12},{12... | collective-permute-start | bytes 786440 | tf_op jit(solution)/shard_map/ppermute | solution.py:41
  232.7 31.6 %collective-permute-start.46 = (bf16[256,2048]{1,0:T(8,128)(2,1)S(1)}, bf16[256,2048]{1,0:T(8,128)(2,1)}, u32[]{:S(2)}, u32[]{:S(2)}) collective-permute-start(bf16[256,2048]{1,0:T(8,128)(2,1)S(1)} %pad_maximum_fusion.2.refs_1_.refs_2_.refs_20_), channel_id=1, source_target_pairs={{0,4},{2,6},{4,0},{6,2},{1,5},{3,7},{5,1},{7,3},{8,12},{10,14},{12... | collective-permute-start | bytes 3145736 | tf_op jit(solution)/shard_map/ppermute | solution.py:41
  232.9 41.9 %collective-permute-start.43 = (bf16[256,1024]{1,0:T(8,128)(2,1)}, bf16[256,1024]{1,0:T(8,128)(2,1)}, u32[]{:S(2)}, u32[]{:S(2)}) collective-permute-start(bf16[256,1024]{1,0:T(8,128)(2,1)} %get-tuple-element.208.refs_0_.refs_12_), channel_id=1, source_target_pairs={{0,4},{2,6},{4,0},{6,2},{1,5},{3,7},{5,1},{7,3},{8,12},{10,14},{12... | collective-permute-start | bytes 1572872 | tf_op jit(solution)/shard_map/ppermute | solution.py:41
  264.3 17.8 %collective-permute-start.47 = (bf16[256,2048]{1,0:T(8,128)(2,1)S(1)}, bf16[256,2048]{1,0:T(8,128)(2,1)}, u32[]{:S(2)}, u32[]{:S(2)}) collective-permute-start(bf16[256,2048]{1,0:T(8,128)(2,1)S(1)} %pad_maximum_fusion.2.refs_1_.refs_2_.refs_20_), channel_id=1, source_target_pairs={{0,2},{2,0},{4,6},{6,4},{1,3},{3,1},{5,7},{7,5},{8,10},{10,8},{12,... | collective-permute-start | bytes 3145736 | tf_op jit(solution)/shard_map/ppermute | solution.py:41
  264.3 17.8 %collective-permute-start.48 = (bf16[256,2048]{1,0:T(8,128)(2,1)}, bf16[256,2048]{1,0:T(8,128)(2,1)}, u32[]{:S(2)}, u32[]{:S(2)}) collective-permute-start(bf16[256,2048]{1,0:T(8,128)(2,1)} %collective-permute-done.46.refs_21_), channel_id=1, source_target_pairs={{0,2},{2,0},{4,6},{6,4},{1,3},{3,1},{5,7},{7,5},{8,10},{10,8},{12,... | collective-permute-start | bytes 3145736 | tf_op jit(solution)/shard_map/ppermute | solution.py:41
  265.7 14.1 %collective-permute-start.14 = (bf16[128,2048]{1,0:T(8,128)(2,1)}, bf16[128,2048]{1,0:T(8,128)(2,1)}, u32[]{:S(2)}, u32[]{:S(2)}) collective-permute-start(bf16[128,2048]{1,0:T(8,128)(2,1)} %constant_dynamic-slice_fusion.3), channel_id=1, source_target_pairs={{0,1},{1,0},{2,3},{3,2},{4,5},{5,4},{6,7},{7,6},{8,9},{9,8},{10,11... | collective-permute-start | bytes 1572872 | tf_op jit(solution)/shard_map/ppermute | solution.py:41
  295.0 13.3 %collective-permute-start.35 = (bf16[128,2048]{1,0:T(8,128)(2,1)}, bf16[128,2048]{1,0:T(8,128)(2,1)}, u32[]{:S(2)}, u32[]{:S(2)}) collective-permute-start(bf16[128,2048]{1,0:T(8,128)(2,1)} %constant_dynamic-slice_fusion.2), channel_id=1, source_target_pairs={{0,1},{1,0},{2,3},{3,2},{4,5},{5,4},{6,7},{7,6},{8,9},{9,8},{10,11... | collective-permute-start | bytes 1572872 | tf_op jit(solution)/shard_map/ppermute | solution.py:41
  (88 other events, 643.7 us)
Sparse Core Ops, SparseCore 0:
  128.2 44.7 reduce-scatter.8
  175.3 43.1 reduce-scatter.10
  220.9 76.0 reduce-scatter.6
  299.3 78.6 reduce-scatter.4

commit v6 on v5

--- a/solution.py
+++ b/solution.py
@@ -355,7 +355,7 @@
             jax.ShapeDtypeStruct((rows, tile), F32),
             jax.ShapeDtypeStruct((blocks - 1, rows, tile), F32),
         ],
-        compiler_params=params(VMEM),
+        compiler_params=params(ALL_VMEM),
         cost_estimate=load(),
     )(values)
 

time: 393 us -> 393 us (level)
    unnamed x143 -> x141, local copies, waits for them, and re-layouts: 23 us -> 21.7 us
where the time goes in v6:
time: 393 us; the launch traced here: 387 us
  waiting for transfers between devices  134 us (34%)
  Pallas kernels  131 us (33%)
  starting transfers between devices  51.5 us (13%)
  other arithmetic  31.6 us (8%)
  local copies, waits for them, and re-layouts  23.8 us (6%)
  between operations  15.1 us (4%)
    ppermute x49, waiting for transfers between devices, xperm(): return lax.ppermute(values, axis, pairs)  108 us
    ppermute x49, starting transfers between devices, xperm(): return lax.ppermute(values, axis, pairs)  51.1 us
    pallas_call x8, Pallas kernels, mm(): pl.pallas_call(functools.partial(mm_kernel, n_pairs=len(lefts), trans=tra...  43.6 us
    pallas_call x4, Pallas kernels, weight_grad(): pl.pallas_call(functools.partial(weight_grad_kernel, blocks=blocks, n=n),...  30.8 us
    reduce_scatter x4, waiting for transfers between devices, reduce_over_dp(): return lax.psum_scatter(whole, 'dp', scatter_dimension=0, tiled=True)  25.8 us
    unnamed x141, local copies, waits for them, and re-layouts  21.7 us
    pallas_call x2, Pallas kernels, attention_backward(): pl.pallas_call(functools.partial(backward_kernel, n=n, first_head=first_h...  13.9 us
    pallas_call x2, Pallas kernels, attention_forward(): pl.pallas_call(functools.partial(forward_kernel, n=n, first_head=first_he...  12.3 us
  transfers between devices with their start and end apart: 53, of which 21 were waited for; matrix products, arithmetic and copies ran while one was open for 10% of the time, Pallas kernels for 29%

profile of v6, /device:TPU:0, one launch (start us, length us, event | category | flops | bytes accessed | tf_op | source)
XLA Modules:
  0.0 387.2 jit_solution(1733027587876182587)
XLA Ops:
  7.2 6.5 %shard_map.254 = (bf16[256,2048]{1,0:T(8,128)(2,1)}, bf16[2,256,512]{2,1,0:T(8,128)(2,1)}, bf16[2,256,512]{2,1,0:T(8,128)(2,1)}) custom-call(bf16[256,2048]{1,0:T(8,128)(2,1)} %bitcast.100, bf16[2048]{0:T(1024)(128)(2,1)} %gain.1, bf16[2048]{0:T(1024)(128)(2,1)} %shift.1, bf16[3,2048,1024]{2,1,0:T(8,128)(2,1)} %bitcast.95, bf16[2,1024]{1,0:T(2,128)(2,1)} %refs_2_.2), custom_call_target="tpu_custom_call" | custom-call | tf_op jit(solution)/shard_map/pallas_call | solution.py:170
  13.8 5.8 %collective-permute-start = (bf16[2,256,512]{2,1,0:T(8,128)(2,1)}, bf16[2,256,512]{2,1,0:T(8,128)(2,1)}, u32[]{:S(2)}, u32[]{:S(2)}) collective-permute-start(bf16[2,256,512]{2,1,0:T(8,128)(2,1)} %get-tuple-element.121.refs_0_), channel_id=1, source_target_pairs={{0,4},{2,6},{1,5},{3,7},{8,12},{10,14},{9,13},{11,15},{16,20},{18,... | collective-permute-start | bytes 1572872 | tf_op jit(solution)/shard_map/ppermute | solution.py:41
  20.8 4.6 %copy-done = bf16[2048,3,1024]{2,0,1:T(8,128)(2,1)S(1)} copy-done((bf16[2048,3,1024]{2,0,1:T(8,128)(2,1)S(1)}, bf16[2048,3,1024]{2,0,1:T(8,128)(2,1)}, u32[]{:S(2)}) %copy-start) | copy-done | bytes 12582936
  38.3 5.9 %shard_map.257 = (bf16[256,1024]{1,0:T(8,128)(2,1)}, f32[4,1,256]{2,1,0:T(1,128)S(1)}) custom-call(f32[8]{0:T(128)S(1)} %multiply_exponential_fusion.slopes, bf16[256,1024]{1,0:T(8,128)(2,1)S(1)} %shard_map.255.query, f32[4,256,256]{2,1,0:T(8,128)S(1)} %pad_maximum_fusion.1.distance, bf16[2,256,512]{2,1,0:T(8,128)(2,1)} %get-tuple-element.121.refs_0_, ...), custom_call_target="tpu_custom_call" | custom-call | tf_op jit(solution)/shard_map/pallas_call | solution.py:424
  46.2 6.4 %shard_map.258 = (bf16[256,1024]{1,0:T(8,128)(2,1)}, f32[4,1,256]{2,1,0:T(1,128)S(1)}) custom-call(f32[8]{0:T(128)S(1)} %multiply_exponential_fusion.slopes, bf16[256,1024]{1,0:T(8,128)(2,1)S(1)} %shard_map.255.query, f32[4,256,256]{2,1,0:T(8,128)S(1)} %pad_maximum_fusion.1.distance, ...), custom_call_target="tpu_custom_call", output_to_operand_aliasing={{0}: (7, {})} | custom-call | tf_op jit(solution)/shard_map/pallas_call | solution.py:424
  62.9 8.6 %shard_map.260.refs_6_.grad_active = f32[256,4096]{1,0:T(8,128)S(1)} custom-call(bf16[256,2048]{1,0:T(8,128)(2,1)S(1)} %bitcast.103, bf16[2048,4096]{1,0:T(8,128)(2,1)} %refs_3_.1), custom_call_target="tpu_custom_call" | custom-call | flops 999999995904 | bytes 10000000 | tf_op jit(solution)/shard_map/pallas_call | solution.py:140
  71.6 7.5 %collective-permute-done.6.refs_3_ = bf16[256,2048]{1,0:T(8,128)(2,1)} collective-permute-done((bf16[256,2048]{1,0:T(8,128)(2,1)}, bf16[256,2048]{1,0:T(8,128)(2,1)}, u32[]{:S(2)}, u32[]{:S(2)}) %collective-permute-start.6) | collective-permute-done | bytes 1048608 | tf_op jit(solution)/shard_map/ppermute | solution.py:41
  79.1 9.0 %shard_map.261 = (f32[256,2048]{1,0:T(8,128)S(1)}, bf16[256,2048]{1,0:T(8,128)(2,1)S(1)}, bf16[256,2048]{1,0:T(8,128)(2,1)}, bf16[256,4096]{1,0:T(8,128)(2,1)}, f32[1,2048]{1,0:T(1,128)S(1)}) custom-call(bf16[256,2048]{1,0:T(8,128)(2,1)S(1)} %bitcast.101, f32[3,2048]{1,0:T(4,128)S(1)} %maximum_convert_fusion.1.refs_1_, ...), custom_call_target="tpu_custom_call" | custom-call | tf_op jit(solution)/shard_map/pallas_call | solution.py:258
  88.2 5.7 %collective-permute-start.11 = (bf16[256,2048]{1,0:T(8,128)(2,1)}, bf16[256,2048]{1,0:T(8,128)(2,1)}, u32[]{:S(2)}, u32[]{:S(2)}) collective-permute-start(bf16[256,2048]{1,0:T(8,128)(2,1)} %get-tuple-element.157.refs_4_.refs_0_), channel_id=1, source_target_pairs={{0,4},{2,6},{4,0},{6,2},{1,5},{3,7},{5,1},{7,3},{8,12},{10,14},{12... | collective-permute-start | bytes 3145736 | tf_op jit(solution)/shard_map/ppermute | solution.py:41
  93.9 7.1 %shard_map.262 = (bf16[256,2048]{1,0:T(8,128)(2,1)}, bf16[256,4096]{1,0:T(8,128)(2,1)}, f32[1,2048]{1,0:T(1,128)S(1)}) custom-call(bf16[256,2048]{1,0:T(8,128)(2,1)S(1)} %get-tuple-element.152.norm.refs_0_, bf16[2048,4096]{1,0:T(8,128)(2,1)} %refs_1_.8, f32[1,4096]{1,0:T(1,128)S(1)} %bitcast.107, ...), custom_call_target="tpu_custom_call", output_to_operand_aliasing={{1}: (4, {})} | custom-call | flops 999999995904 | bytes 10000000 | tf_op jit(solution)/shard_map/pallas_call | solution.py:281
  101.0 6.2 %shard_map.263 = bf16[256,1024]{1,0:T(8,128)(2,1)} custom-call(bf16[256,4096]{1,0:T(8,128)(2,1)} %get-tuple-element.189.refs_0_.refs_4_, bf16[2048,4096]{1,0:T(8,128)(2,1)} %refs_1_.8), custom_call_target="tpu_custom_call" | custom-call | tf_op jit(solution)/shard_map/pallas_call | solution.py:140
  107.2 6.2 %shard_map.264 = bf16[256,1024]{1,0:T(8,128)(2,1)} custom-call(bf16[256,4096]{1,0:T(8,128)(2,1)} %get-tuple-element.189.refs_0_.refs_4_, bf16[2048,4096]{1,0:T(8,128)(2,1)} %refs_1_.8), custom_call_target="tpu_custom_call" | custom-call | tf_op jit(solution)/shard_map/pallas_call | solution.py:140
  122.4 5.6 %shard_map.266 = bf16[512,2048]{1,0:T(8,128)(2,1)} custom-call(bf16[1024,256]{1,0:T(8,128)(2,1)} %copy-done.9, bf16[1024,256]{1,0:T(8,128)(2,1)} %collective-permute-done.7.refs_1_.refs_9_.refs_17_, bf16[1024,256]{1,0:T(8,128)(2,1)} %collective-permute-done.8.refs_2_.refs_10_.refs_18_, bf16[1024,256]{1,0:T(8,128)(2,1)} %collective-permute-done.9.refs_3_.refs_11_.refs_19_, ...), custom_call_target="tpu_custom_call" | custom-call | tf_op jit(solution)/shard_map/pallas_call | solution.py:331
  128.2 9.5 %shard_map.267 = bf16[256,2048]{1,0:T(8,128)(2,1)S(1)} custom-call(bf16[256,2048]{1,0:T(8,128)(2,1)} %get-tuple-element.157.refs_4_.refs_0_, bf16[256,2048]{1,0:T(8,128)(2,1)} %get-tuple-element.172.refs_1_.refs_4_, bf16[2048,4096]{1,0:T(8,128)(2,1)} %refs_3_.1, bf16[2048,4096]{1,0:T(8,128)(2,1)} %refs_3_.1), custom_call_target="tpu_custom_call" | custom-call | flops 999999995904 | bytes 10000000 | tf_op jit(solution)/shard_map/pallas_call | solution.py:140
  157.3 5.6 %shard_map.269 = bf16[512,2048]{1,0:T(8,128)(2,1)} custom-call(bf16[1024,256]{1,0:T(8,128)(2,1)} %copy-done.9, bf16[1024,256]{1,0:T(8,128)(2,1)} %collective-permute-done.7.refs_1_.refs_9_.refs_17_, bf16[1024,256]{1,0:T(8,128)(2,1)} %collective-permute-done.8.refs_2_.refs_10_.refs_18_, bf16[1024,256]{1,0:T(8,128)(2,1)} %collective-permute-done.9.refs_3_.refs_11_.refs_19_, ...), custom_call_target="tpu_custom_call" | custom-call | tf_op jit(solution)/shard_map/pallas_call | solution.py:331
  164.4 6.9 %shard_map.270 = (bf16[256,1024]{1,0:T(8,128)(2,1)}, bf16[2,2,256,512]{3,2,1,0:T(8,128)(2,1)S(1)}, bf16[2,2,256,512]{3,2,1,0:T(8,128)(2,1)S(1)}) custom-call(f32[8]{0:T(128)S(1)} %copy-done.31, bf16[256,1024]{1,0:T(8,128)(2,1)S(1)} %copy-done.13, bf16[256,1024]{1,0:T(8,128)(2,1)S(1)} %shard_map.268.grad_mixed, f32[4,256,256]{2,1,0:T(8,128)S(1)} %copy-done.6, ...), custom_call_target="tpu_custom_call" | custom-call | flops 999999995904 | bytes 10000000 | tf_op jit(solution)/shard_map/pallas_call | solution.py:504
  172.4 7.0 %shard_map.271 = (bf16[256,1024]{1,0:T(8,128)(2,1)}, bf16[2,2,256,512]{3,2,1,0:T(8,128)(2,1)S(1)}, bf16[2,2,256,512]{3,2,1,0:T(8,128)(2,1)S(1)}) custom-call(f32[8]{0:T(128)S(1)} %copy-done.31, bf16[256,1024]{1,0:T(8,128)(2,1)S(1)} %copy-done.13, bf16[256,1024]{1,0:T(8,128)(2,1)S(1)} %shard_map.268.grad_mixed, ...), custom_call_target="tpu_custom_call", output_to_operand_aliasing={{0}: (9, {})} | custom-call | tf_op jit(solution)/shard_map/pallas_call | solution.py:504
  184.9 15.1 %collective-permute-done.26.refs_5_ = bf16[256,4096]{1,0:T(8,128)(2,1)} collective-permute-done((bf16[256,4096]{1,0:T(8,128)(2,1)}, bf16[256,4096]{1,0:T(8,128)(2,1)}, u32[]{:S(2)}, u32[]{:S(2)}) %collective-permute-start.26) | collective-permute-done | bytes 2097184 | tf_op jit(solution)/shard_map/ppermute | solution.py:41
  204.5 9.0 %shard_map.272 = bf16[512,4096]{1,0:T(8,128)(2,1)} custom-call(bf16[512,256]{1,0:T(8,128)(2,1)} %copy-done.29, bf16[512,256]{1,0:T(8,128)(2,1)} %copy-done.53, bf16[512,256]{1,0:T(8,128)(2,1)} %copy-done.52, bf16[512,256]{1,0:T(8,128)(2,1)} %copy-done.54, bf16[256,4096]{1,0:T(8,128)(2,1)} %get-tuple-element.189.refs_0_.refs_4_, ...), custom_call_target="tpu_custom_call" | custom-call | tf_op jit(solution)/shard_map/pallas_call | solution.py:331
  221.8 8.9 %collective-permute-done.31 = bf16[2,256,512]{2,1,0:T(8,128)(2,1)} collective-permute-done((bf16[2,256,512]{2,1,0:T(8,128)(2,1)}, bf16[2,256,512]{2,1,0:T(8,128)(2,1)}, u32[]{:S(2)}, u32[]{:S(2)}) %collective-permute-start.31) | collective-permute-done | bytes 524320 | tf_op jit(solution)/shard_map/ppermute | solution.py:41
  236.3 4.0 %collective-permute-done.34.refs_3_ = bf16[512,256]{1,0:T(8,128)(2,1)} collective-permute-done((bf16[512,256]{1,0:T(8,128)(2,1)S(1)}, bf16[512,256]{1,0:T(8,128)(2,1)}, u32[]{:S(2)}, u32[]{:S(2)}) %collective-permute-start.34) | collective-permute-done | bytes 262176 | tf_op jit(solution)/shard_map/ppermute | solution.py:41
  240.3 7.2 %shard_map.274 = bf16[256,2048]{1,0:T(8,128)(2,1)S(1)} custom-call(bf16[256,1024]{1,0:T(8,128)(2,1)} %get-tuple-element.208.refs_0_.refs_12_, bf16[256,2048]{1,0:T(8,128)(2,1)S(1)} %pad_maximum_fusion.2.refs_1_.refs_2_.refs_20_, bf16[256,2048]{1,0:T(8,128)(2,1)S(1)} %pad_maximum_fusion.2.refs_1_.refs_2_.refs_20_, bf16[3,2048,1024]{2,1,0:T(8,128)(2,1)} %bitcast.96, ...), custom_call_target="tpu_custom_call" | custom-call | flops 10000000000 | bytes 10000000 | tf_op jit(solution)/shard_map/pallas_call | solution.py:140
  248.5 15.9 %collective-permute-done.46.refs_21_ = bf16[256,2048]{1,0:T(8,128)(2,1)} collective-permute-done((bf16[256,2048]{1,0:T(8,128)(2,1)S(1)}, bf16[256,2048]{1,0:T(8,128)(2,1)}, u32[]{:S(2)}, u32[]{:S(2)}) %collective-permute-start.46) | collective-permute-done | bytes 1048608 | tf_op jit(solution)/shard_map/ppermute | solution.py:41
  266.3 8.5 %collective-permute-done.43.refs_13_ = bf16[256,1024]{1,0:T(8,128)(2,1)} collective-permute-done((bf16[256,1024]{1,0:T(8,128)(2,1)}, bf16[256,1024]{1,0:T(8,128)(2,1)}, u32[]{:S(2)}, u32[]{:S(2)}) %collective-permute-start.43) | collective-permute-done | bytes 524320 | tf_op jit(solution)/shard_map/ppermute | solution.py:41
  275.4 4.6 %collective-permute-done.14 = bf16[128,2048]{1,0:T(8,128)(2,1)} collective-permute-done((bf16[128,2048]{1,0:T(8,128)(2,1)}, bf16[128,2048]{1,0:T(8,128)(2,1)}, u32[]{:S(2)}, u32[]{:S(2)}) %collective-permute-start.14) | collective-permute-done | bytes 524320 | tf_op jit(solution)/shard_map/ppermute | solution.py:41
  282.2 10.6 %shard_map.275 = bf16[512,4096]{1,0:T(8,128)(2,1)} custom-call(bf16[512,256]{1,0:T(8,128)(2,1)} %copy-done.28, bf16[512,256]{1,0:T(8,128)(2,1)} %collective-permute-done.32.refs_1_, bf16[512,256]{1,0:T(8,128)(2,1)} %collective-permute-done.33.refs_2_, bf16[512,256]{1,0:T(8,128)(2,1)} %collective-permute-done.34.refs_3_, ...), custom_call_target="tpu_custom_call" | custom-call | tf_op jit(solution)/shard_map/pallas_call | solution.py:331
  301.2 7.3 %collective-permute-done.35 = bf16[128,2048]{1,0:T(8,128)(2,1)} collective-permute-done((bf16[128,2048]{1,0:T(8,128)(2,1)}, bf16[128,2048]{1,0:T(8,128)(2,1)}, u32[]{:S(2)}, u32[]{:S(2)}) %collective-permute-start.35) | collective-permute-done | bytes 524320 | tf_op jit(solution)/shard_map/ppermute | solution.py:41
  318.9 3.9 %collective-permute-done.38 = f32[5,1024]{1,0:T(8,128)S(1)} collective-permute-done((f32[5,1024]{1,0:T(8,128)S(1)}, f32[5,1024]{1,0:T(8,128)S(1)}, u32[]{:S(2)}, u32[]{:S(2)}) %collective-permute-start.38) | collective-permute-done | bytes 20512 | tf_op jit(solution)/shard_map/ppermute | solution.py:41
  324.4 5.9 %collective-permute-done.39 = f32[5,1024]{1,0:T(8,128)S(1)} collective-permute-done((f32[5,1024]{1,0:T(8,128)S(1)}, f32[5,1024]{1,0:T(8,128)S(1)}, u32[]{:S(2)}, u32[]{:S(2)}) %collective-permute-start.39) | collective-permute-done | bytes 20512 | tf_op jit(solution)/shard_map/ppermute | solution.py:41
  331.6 6.1 %collective-permute-done.40 = f32[5,1024]{1,0:T(8,128)S(1)} collective-permute-done((f32[5,1024]{1,0:T(8,128)S(1)}, f32[5,1024]{1,0:T(8,128)S(1)}, u32[]{:S(2)}, u32[]{:S(2)}) %collective-permute-start.40) | collective-permute-done | bytes 20512 | tf_op jit(solution)/shard_map/ppermute | solution.py:41
  337.7 3.9 %collective-permute-done.41 = f32[5,1024]{1,0:T(8,128)S(1)} collective-permute-done((f32[5,1024]{1,0:T(8,128)S(1)}, f32[5,1024]{1,0:T(8,128)S(1)}, u32[]{:S(2)}, u32[]{:S(2)}) %collective-permute-start.41) | collective-permute-done | bytes 20512 | tf_op jit(solution)/shard_map/ppermute | solution.py:41
  352.1 25.8 %reduce-scatter.5.cloned.1.call-done.values = bf16[128,4096]{1,0:T(8,128)(2,1)} async-done(((bf16[512,4096]{1,0:T(8,128)(2,1)}), bf16[128,4096]{1,0:T(8,128)(2,1)}) %reduce-scatter.5.cloned.1.call-update) | async-done | bytes 1048592 | tf_op jit(solution)/shard_map/reduce_scatter | solution.py:720
  (314 shorter events, 121.2 us)
Async XLA Ops:
  7.2 334.5 %reduce-scatter.9.cloned.1.call-start = ((), (), s32[]{:S(2)}) async-start(), calls=%async_computation.6 | async-start | bytes 2621440 | tf_op jit(solution)/shard_map/reduce_scatter | solution.py:720
  13.8 19.6 %collective-permute-start = (bf16[2,256,512]{2,1,0:T(8,128)(2,1)}, bf16[2,256,512]{2,1,0:T(8,128)(2,1)}, u32[]{:S(2)}, u32[]{:S(2)}) collective-permute-start(bf16[2,256,512]{2,1,0:T(8,128)(2,1)} %get-tuple-element.121.refs_0_), channel_id=1, source_target_pairs={{0,4},{2,6},{1,5},{3,7},{8,12},{10,14},{9,13},{11,15},{16,20},{18,... | collective-permute-start | bytes 1572872 | tf_op jit(solution)/shard_map/ppermute | solution.py:41
  26.8 19.4 %collective-permute-start.4 = (bf16[2,256,512]{2,1,0:T(8,128)(2,1)S(1)}, bf16[2,256,512]{2,1,0:T(8,128)(2,1)}, u32[]{:S(2)}, u32[]{:S(2)}) collective-permute-start(bf16[2,256,512]{2,1,0:T(8,128)(2,1)S(1)} %copy-done.19), channel_id=1, source_target_pairs={{0,2},{4,6},{1,3},{5,7},{8,10},{12,14},{9,11},{13,15},{16,18},{20,... | collective-permute-start | bytes 1572872 | tf_op jit(solution)/shard_map/ppermute | solution.py:41
  29.1 15.2 %collective-permute-start.3 = (bf16[2,256,512]{2,1,0:T(8,128)(2,1)S(1)}, bf16[2,256,512]{2,1,0:T(8,128)(2,1)}, u32[]{:S(2)}, u32[]{:S(2)}) collective-permute-start(bf16[2,256,512]{2,1,0:T(8,128)(2,1)S(1)} %copy-done.19), channel_id=1, source_target_pairs={{0,4},{2,6},{1,5},{3,7},{8,12},{10,14},{9,13},{11,15},{16,20},{18,... | collective-permute-start | bytes 1572872 | tf_op jit(solution)/shard_map/ppermute | solution.py:41
  56.0 23.2 %collective-permute-start.6 = (bf16[256,2048]{1,0:T(8,128)(2,1)}, bf16[256,2048]{1,0:T(8,128)(2,1)}, u32[]{:S(2)}, u32[]{:S(2)}) collective-permute-start(bf16[256,2048]{1,0:T(8,128)(2,1)} %shard_map.259.refs_2_), channel_id=1, source_target_pairs={{0,1},{1,0},{2,3},{3,2},{4,5},{5,4},{6,7},{7,6},{8,9},{9,8},{10,11... | collective-permute-start | bytes 3145736 | tf_op jit(solution)/shard_map/ppermute | solution.py:41
  57.5 30.7 %collective-permute-start.7 = (bf16[1024,256]{1,0:T(8,128)(2,1)}, bf16[1024,256]{1,0:T(8,128)(2,1)}, u32[]{:S(2)}, u32[]{:S(2)}) collective-permute-start(bf16[1024,256]{1,0:T(8,128)(2,1)} %get-tuple-element.140), channel_id=1, source_target_pairs={{0,4},{2,6},{4,0},{6,2},{1,5},{3,7},{5,1},{7,3},{8,12},{10,14},{12... | collective-permute-start | bytes 1572872 | tf_op jit(solution)/shard_map/ppermute | solution.py:41
  60.8 27.4 %collective-permute-start.8 = (bf16[1024,256]{1,0:T(8,128)(2,1)}, bf16[1024,256]{1,0:T(8,128)(2,1)}, u32[]{:S(2)}, u32[]{:S(2)}) collective-permute-start(bf16[1024,256]{1,0:T(8,128)(2,1)} %get-tuple-element.141), channel_id=1, source_target_pairs={{0,2},{2,0},{4,6},{6,4},{1,3},{3,1},{5,7},{7,5},{8,10},{10,8},{12,... | collective-permute-start | bytes 1572872 | tf_op jit(solution)/shard_map/ppermute | solution.py:41
  60.8 27.4 %collective-permute-start.9 = (bf16[1024,256]{1,0:T(8,128)(2,1)}, bf16[1024,256]{1,0:T(8,128)(2,1)}, u32[]{:S(2)}, u32[]{:S(2)}) collective-permute-start(bf16[1024,256]{1,0:T(8,128)(2,1)} %get-tuple-element.142), channel_id=1, source_target_pairs={{0,6},{2,4},{4,2},{6,0},{1,7},{3,5},{5,3},{7,1},{8,14},{10,12},{12... | collective-permute-start | bytes 1572872 | tf_op jit(solution)/shard_map/ppermute | solution.py:41
  60.9 40.1 %collective-permute-start.10 = (bf16[256,1024]{1,0:T(8,128)(2,1)}, bf16[256,1024]{1,0:T(8,128)(2,1)}, u32[]{:S(2)}, u32[]{:S(2)}) collective-permute-start(bf16[256,1024]{1,0:T(8,128)(2,1)} %get-tuple-element.178.refs_0_.refs_4_), channel_id=1, source_target_pairs={{0,4},{2,6},{4,0},{6,2},{1,5},{3,7},{5,1},{7,3},{8,12},{10,14},{12... | collective-permute-start | bytes 1572872 | tf_op jit(solution)/shard_map/ppermute | solution.py:41
  88.2 30.6 %collective-permute-start.11 = (bf16[256,2048]{1,0:T(8,128)(2,1)}, bf16[256,2048]{1,0:T(8,128)(2,1)}, u32[]{:S(2)}, u32[]{:S(2)}) collective-permute-start(bf16[256,2048]{1,0:T(8,128)(2,1)} %get-tuple-element.157.refs_4_.refs_0_), channel_id=1, source_target_pairs={{0,4},{2,6},{4,0},{6,2},{1,5},{3,7},{5,1},{7,3},{8,12},{10,14},{12... | collective-permute-start | bytes 3145736 | tf_op jit(solution)/shard_map/ppermute | solution.py:41
  113.4 28.9 %collective-permute-start.16 = (bf16[256,1024]{1,0:T(8,128)(2,1)}, bf16[256,1024]{1,0:T(8,128)(2,1)}, u32[]{:S(2)}, u32[]{:S(2)}) collective-permute-start(bf16[256,1024]{1,0:T(8,128)(2,1)} %shard_map.264), channel_id=1, source_target_pairs={{0,1},{1,0},{2,3},{3,2},{4,5},{5,4},{6,7},{7,6},{8,9},{9,8},{10,11... | collective-permute-start | bytes 1572872 | tf_op jit(solution)/shard_map/ppermute | solution.py:41
  114.9 29.1 %collective-permute-start.15 = (bf16[256,1024]{1,0:T(8,128)(2,1)}, bf16[256,1024]{1,0:T(8,128)(2,1)}, u32[]{:S(2)}, u32[]{:S(2)}) collective-permute-start(bf16[256,1024]{1,0:T(8,128)(2,1)} %shard_map.263), channel_id=1, source_target_pairs={{0,1},{1,0},{2,3},{3,2},{4,5},{5,4},{6,7},{7,6},{8,9},{9,8},{10,11... | collective-permute-start | bytes 1572872 | tf_op jit(solution)/shard_map/ppermute | solution.py:41
  115.4 25.0 %collective-permute-start.20 = (bf16[256,2048]{1,0:T(8,128)(2,1)}, bf16[256,2048]{1,0:T(8,128)(2,1)}, u32[]{:S(2)}, u32[]{:S(2)}) collective-permute-start(bf16[256,2048]{1,0:T(8,128)(2,1)} %get-tuple-element.172.refs_1_.refs_4_), channel_id=1, source_target_pairs={{0,4},{2,6},{4,0},{6,2},{1,5},{3,7},{5,1},{7,3},{8,12},{10,14},{12... | collective-permute-start | bytes 3145736 | tf_op jit(solution)/shard_map/ppermute | solution.py:41
  128.0 213.7 %reduce-scatter.11.cloned.1.call-start = ((), (), s32[]{:S(2)}) async-start(), calls=%async_computation.7 | async-start | bytes 2621440 | tf_op jit(solution)/shard_map/reduce_scatter | solution.py:720
  140.4 12.9 %collective-permute-start.18 = (bf16[512,256]{1,0:T(8,128)(2,1)}, bf16[512,256]{1,0:T(8,128)(2,1)S(1)}, u32[]{:S(2)}, u32[]{:S(2)}) collective-permute-start(bf16[512,256]{1,0:T(8,128)(2,1)} %get-tuple-element.169), channel_id=1, source_target_pairs={{0,4},{2,6},{4,0},{6,2},{1,5},{3,7},{5,1},{7,3},{8,12},{10,14},{12... | collective-permute-start | bytes 786440 | tf_op jit(solution)/shard_map/ppermute | solution.py:41
  142.2 12.4 %collective-permute-start.19 = (bf16[512,256]{1,0:T(8,128)(2,1)S(1)}, bf16[512,256]{1,0:T(8,128)(2,1)S(1)}, u32[]{:S(2)}, u32[]{:S(2)}) collective-permute-start(bf16[512,256]{1,0:T(8,128)(2,1)S(1)} %get-tuple-element.170), channel_id=1, source_target_pairs={{0,6},{2,4},{4,2},{6,0},{1,7},{3,5},{5,3},{7,1},{8,14},{10,12},{12... | collective-permute-start | bytes 786440 | tf_op jit(solution)/shard_map/ppermute | solution.py:41
  142.3 12.3 %collective-permute-start.21 = (bf16[256,2048]{1,0:T(8,128)(2,1)}, bf16[256,2048]{1,0:T(8,128)(2,1)S(1)}, u32[]{:S(2)}, u32[]{:S(2)}) collective-permute-start(bf16[256,2048]{1,0:T(8,128)(2,1)} %get-tuple-element.172.refs_1_.refs_4_), channel_id=1, source_target_pairs={{0,2},{2,0},{4,6},{6,4},{1,3},{3,1},{5,7},{7,5},{8,10},{10,8},{12,... | collective-permute-start | bytes 3145736 | tf_op jit(solution)/shard_map/ppermute | solution.py:41
  150.3 49.7 %collective-permute-start.26 = (bf16[256,4096]{1,0:T(8,128)(2,1)}, bf16[256,4096]{1,0:T(8,128)(2,1)}, u32[]{:S(2)}, u32[]{:S(2)}) collective-permute-start(bf16[256,4096]{1,0:T(8,128)(2,1)} %get-tuple-element.189.refs_0_.refs_4_), channel_id=1, source_target_pairs={{0,4},{2,6},{4,0},{6,2},{1,5},{3,7},{5,1},{7,3},{8,12},{10,14},{12... | collective-permute-start | bytes 6291464 | tf_op jit(solution)/shard_map/ppermute | solution.py:41
  162.9 186.4 %reduce-scatter.7.cloned.1.call-start = ((), (), s32[]{:S(2)}) async-start(), calls=%async_computation.5 | async-start | bytes 5242880 | tf_op jit(solution)/shard_map/reduce_scatter | solution.py:720
  180.5 20.8 %collective-permute-start.28 = (bf16[256,4096]{1,0:T(8,128)(2,1)}, bf16[256,4096]{1,0:T(8,128)(2,1)S(1)}, u32[]{:S(2)}, u32[]{:S(2)}) collective-permute-start(bf16[256,4096]{1,0:T(8,128)(2,1)} %get-tuple-element.189.refs_0_.refs_4_), channel_id=1, source_target_pairs={{0,2},{2,0},{4,6},{6,4},{1,3},{3,1},{5,7},{7,5},{8,10},{10,8},{12,... | collective-permute-start | bytes 6291464 | tf_op jit(solution)/shard_map/ppermute | solution.py:41
  200.0 20.5 %collective-permute-start.30 = (bf16[2,256,512]{2,1,0:T(8,128)(2,1)}, bf16[2,256,512]{2,1,0:T(8,128)(2,1)}, u32[]{:S(2)}, u32[]{:S(2)}) collective-permute-start(bf16[2,256,512]{2,1,0:T(8,128)(2,1)} %get-tuple-element.228), channel_id=1, source_target_pairs={{4,0},{6,2},{5,1},{7,3},{12,8},{14,10},{13,9},{15,11},{20,16},{22,... | collective-permute-start | bytes 1572872 | tf_op jit(solution)/shard_map/ppermute | solution.py:41
  213.6 164.3 %reduce-scatter.5.cloned.1.call-start = ((), (), s32[]{:S(2)}) async-start(), calls=%async_computation.4 | async-start | bytes 5242880 | tf_op jit(solution)/shard_map/reduce_scatter | solution.py:720
  213.6 17.1 %collective-permute-start.31 = (bf16[2,256,512]{2,1,0:T(8,128)(2,1)}, bf16[2,256,512]{2,1,0:T(8,128)(2,1)}, u32[]{:S(2)}, u32[]{:S(2)}) collective-permute-start(bf16[2,256,512]{2,1,0:T(8,128)(2,1)} %get-tuple-element.197), channel_id=1, source_target_pairs={{4,0},{6,2},{5,1},{7,3},{12,8},{14,10},{13,9},{15,11},{20,16},{22,... | collective-permute-start | bytes 1572872 | tf_op jit(solution)/shard_map/ppermute | solution.py:41
  216.9 19.4 %collective-permute-start.32 = (bf16[512,256]{1,0:T(8,128)(2,1)}, bf16[512,256]{1,0:T(8,128)(2,1)}, u32[]{:S(2)}, u32[]{:S(2)}) collective-permute-start(bf16[512,256]{1,0:T(8,128)(2,1)} %get-tuple-element.199), channel_id=1, source_target_pairs={{0,4},{2,6},{4,0},{6,2},{1,5},{3,7},{5,1},{7,3},{8,12},{10,14},{12... | collective-permute-start | bytes 786440 | tf_op jit(solution)/shard_map/ppermute | solution.py:41
  220.3 16.0 %collective-permute-start.33 = (bf16[512,256]{1,0:T(8,128)(2,1)}, bf16[512,256]{1,0:T(8,128)(2,1)}, u32[]{:S(2)}, u32[]{:S(2)}) collective-permute-start(bf16[512,256]{1,0:T(8,128)(2,1)} %get-tuple-element.200), channel_id=1, source_target_pairs={{0,2},{2,0},{4,6},{6,4},{1,3},{3,1},{5,7},{7,5},{8,10},{10,8},{12,... | collective-permute-start | bytes 786440 | tf_op jit(solution)/shard_map/ppermute | solution.py:41
  220.3 20.0 %collective-permute-start.34 = (bf16[512,256]{1,0:T(8,128)(2,1)S(1)}, bf16[512,256]{1,0:T(8,128)(2,1)}, u32[]{:S(2)}, u32[]{:S(2)}) collective-permute-start(bf16[512,256]{1,0:T(8,128)(2,1)S(1)} %get-tuple-element.201), channel_id=1, source_target_pairs={{0,6},{2,4},{4,2},{6,0},{1,7},{3,5},{5,3},{7,1},{8,14},{10,12},{12... | collective-permute-start | bytes 786440 | tf_op jit(solution)/shard_map/ppermute | solution.py:41
  232.8 31.6 %collective-permute-start.46 = (bf16[256,2048]{1,0:T(8,128)(2,1)S(1)}, bf16[256,2048]{1,0:T(8,128)(2,1)}, u32[]{:S(2)}, u32[]{:S(2)}) collective-permute-start(bf16[256,2048]{1,0:T(8,128)(2,1)S(1)} %pad_maximum_fusion.2.refs_1_.refs_2_.refs_20_), channel_id=1, source_target_pairs={{0,4},{2,6},{4,0},{6,2},{1,5},{3,7},{5,1},{7,3},{8,12},{10,14},{12... | collective-permute-start | bytes 3145736 | tf_op jit(solution)/shard_map/ppermute | solution.py:41
  233.0 41.9 %collective-permute-start.43 = (bf16[256,1024]{1,0:T(8,128)(2,1)}, bf16[256,1024]{1,0:T(8,128)(2,1)}, u32[]{:S(2)}, u32[]{:S(2)}) collective-permute-start(bf16[256,1024]{1,0:T(8,128)(2,1)} %get-tuple-element.208.refs_0_.refs_12_), channel_id=1, source_target_pairs={{0,4},{2,6},{4,0},{6,2},{1,5},{3,7},{5,1},{7,3},{8,12},{10,14},{12... | collective-permute-start | bytes 1572872 | tf_op jit(solution)/shard_map/ppermute | solution.py:41
  264.4 17.7 %collective-permute-start.47 = (bf16[256,2048]{1,0:T(8,128)(2,1)S(1)}, bf16[256,2048]{1,0:T(8,128)(2,1)}, u32[]{:S(2)}, u32[]{:S(2)}) collective-permute-start(bf16[256,2048]{1,0:T(8,128)(2,1)S(1)} %pad_maximum_fusion.2.refs_1_.refs_2_.refs_20_), channel_id=1, source_target_pairs={{0,2},{2,0},{4,6},{6,4},{1,3},{3,1},{5,7},{7,5},{8,10},{10,8},{12,... | collective-permute-start | bytes 3145736 | tf_op jit(solution)/shard_map/ppermute | solution.py:41
  264.4 17.7 %collective-permute-start.48 = (bf16[256,2048]{1,0:T(8,128)(2,1)}, bf16[256,2048]{1,0:T(8,128)(2,1)}, u32[]{:S(2)}, u32[]{:S(2)}) collective-permute-start(bf16[256,2048]{1,0:T(8,128)(2,1)} %collective-permute-done.46.refs_21_), channel_id=1, source_target_pairs={{0,2},{2,0},{4,6},{6,4},{1,3},{3,1},{5,7},{7,5},{8,10},{10,8},{12,... | collective-permute-start | bytes 3145736 | tf_op jit(solution)/shard_map/ppermute | solution.py:41
  265.8 14.1 %collective-permute-start.14 = (bf16[128,2048]{1,0:T(8,128)(2,1)}, bf16[128,2048]{1,0:T(8,128)(2,1)}, u32[]{:S(2)}, u32[]{:S(2)}) collective-permute-start(bf16[128,2048]{1,0:T(8,128)(2,1)} %constant_dynamic-slice_fusion.3), channel_id=1, source_target_pairs={{0,1},{1,0},{2,3},{3,2},{4,5},{5,4},{6,7},{7,6},{8,9},{9,8},{10,11... | collective-permute-start | bytes 1572872 | tf_op jit(solution)/shard_map/ppermute | solution.py:41
  295.2 13.3 %collective-permute-start.35 = (bf16[128,2048]{1,0:T(8,128)(2,1)}, bf16[128,2048]{1,0:T(8,128)(2,1)}, u32[]{:S(2)}, u32[]{:S(2)}) collective-permute-start(bf16[128,2048]{1,0:T(8,128)(2,1)} %constant_dynamic-slice_fusion.2), channel_id=1, source_target_pairs={{0,1},{1,0},{2,3},{3,2},{4,5},{5,4},{6,7},{7,6},{8,9},{9,8},{10,11... | collective-permute-start | bytes 1572872 | tf_op jit(solution)/shard_map/ppermute | solution.py:41
  (87 other events, 642.4 us)
Sparse Core Ops, SparseCore 0:
  128.1 44.7 reduce-scatter.8
  175.3 43.1 reduce-scatter.10
  220.8 76.0 reduce-scatter.6
  299.2 78.6 reduce-scatter.4
